TPU v7x, 32 devices: a whole 2x2x4 slice. The times are simulated.
32 devices in a mesh: row: 16 (over z, y, x), col: 2 (over core).
Axes of the slice: x: 2, y: 2, z: 4, core: 2. Of those that a mesh axis runs over, the one named last changes fastest.
Arguments:
- block_input: bfloat16 [16384, 1024], P(('row', 'col')), may hold values from -6 to 6
- teacher: bfloat16 [16384, 1024], P(('row', 'col')), may hold values from -6 to 6
- lengths: int32 [16], P('row'), may hold values from 256 to 1024, as said below
- head_routes: int32 [16384, 4, 2], P(('row', 'col')), may hold values from 0 to 4, all different within a row
- expert_routes: int32 [16384, 16], P('row'), may hold values from 0 to 31, all different within a row; in each aligned block of 1024 rows (0 to 1023, 1024 to 2047, ...) at most 768 rows name the same one
- first_gain: bfloat16 [1024], P(('row', 'col')), may hold values from 0.5 to 1.5
- query_weight: bfloat16 [1024, 512], P(('row', 'col')), may hold values from -0.1875 to 0.1875
- key_weight: bfloat16 [1024, 512], P(('row', 'col')), may hold values from -0.1875 to 0.1875
- value_weight: bfloat16 [1024, 2560], P(('row', 'col')), may hold values from -0.1875 to 0.1875
- head_router: bfloat16 [1024, 40], P(('row', 'col')), may hold values from -0.3125 to 0.3125
- output_weight: bfloat16 [2560, 1024], P(None, ('row', 'col')), may hold values from -4 to 4
- second_gain: bfloat16 [1024], P(('row', 'col')), may hold values from 0.5 to 1.5
- expert_router: bfloat16 [1024, 32], P('row', 'col'), may hold values from -0.21875 to 0.21875
- expert_up: bfloat16 [32, 1024, 128], P('col', 'row'), may hold values from -0.1875 to 0.1875
- expert_down: bfloat16 [32, 128, 1024], P('col', None, 'row'), may hold values from -0.5 to 0.5
Outputs:
- block_output: bfloat16 [16384, 1024], P(('row', 'col'))
- input_grad: float32 [16384, 1024], P(('row', 'col'))
- first_gain_grad: float32 [1024], P(('row', 'col'))
- query_weight_grad: float32 [1024, 512], P(('row', 'col'))
- key_weight_grad: float32 [1024, 512], P(('row', 'col'))
- value_weight_grad: float32 [1024, 2560], P(('row', 'col'))
- head_router_grad: float32 [1024, 40], P(('row', 'col'))
- output_weight_grad: float32 [2560, 1024], P(None, ('row', 'col'))
- second_gain_grad: float32 [1024], P(('row', 'col'))
- expert_router_grad: float32 [1024, 32], P('row', 'col')
- expert_up_grad: float32 [32, 1024, 128], P('col', 'row')
- expert_down_grad: float32 [32, 128, 1024], P('col', None, 'row')
Inputs may be any that keep to these rules, and one draw needn't show every extreme that they name: `lengths`: every sequence is at most 1024 long and some sequence is exactly 1024 long; some is 256 long. `head_routes`: the 2 experts of one token in one head are different. `expert_routes`: the 16 experts of one token are different. In each aligned block of 1024 rows (the tokens of one index of row), no expert is named by more than 768 rows, a bound that some block reaches.
All inputs are finite; a program needn't handle non-finite values.
Results may differ from a plain program's by a relative error of at most 0.025.
The roundings to bfloat16 on the way count: a program that leaves them out, or rounds other values in their place, can miss the bound.
Values may be sent and summed in bfloat16 or wider, within the bound.
A program may use at most 384 MiB of HBM per device.

v0:
```python
import math

import jax
import jax.numpy as jnp
from jax import lax
from jax.sharding import PartitionSpec as P

H = 4
DH = 128
AEXP = 5
MAXLEN = 2048
CAP = 768


EPS = 1e-05
MASKED = -1e30


def shifted(value, axis, steps):
    count = lax.axis_size(axis)
    leading, last = (max(0, -steps), min(count, count - steps))
    return lax.ppermute(value, axis, [(source, source + steps) for source in range(leading, last)])


def contract_last(left, right):
    return lax.dot_general(
        left, right, (((1,), (1,)), ((), ())), preferred_element_type=jnp.float32
    )


def contract_first(left, right):
    return lax.dot_general(
        left, right, (((0,), (0,)), ((), ())), preferred_element_type=jnp.float32
    )


def norm_parts(values, gain):
    average = jnp.mean(values, axis=-1, keepdims=True)
    centred = values - average
    inv_std = lax.rsqrt(jnp.mean(centred * centred, axis=-1, keepdims=True) + EPS)
    normed = centred * inv_std
    return (normed * gain, normed, inv_std)


def norm_back(grad_in, gain, normed, inv_std):
    grad_hat = grad_in * gain
    mean_one = jnp.mean(grad_hat, axis=-1, keepdims=True)
    mean_two = jnp.mean(grad_hat * normed, axis=-1, keepdims=True)
    return inv_std * (grad_hat - mean_one - normed * mean_two)


def rope_tables(positions, width):
    half_width = width // 2
    freq = jnp.exp(jnp.arange(half_width).astype(jnp.float32) * (-2.0 * math.log(10000.0) / width))
    angle = positions.astype(jnp.float32)[:, None] * freq[None, :]
    return (jnp.cos(angle), jnp.sin(angle))


def rotate(values, cosine, sines):
    half_width = values.shape[-1] // 2
    front_half = values[..., :half_width]
    back_half = values[..., half_width:]
    cos_part = cosine[:, None, :]
    sin_part = sines[:, None, :]
    return jnp.concatenate(
        [
            front_half * cos_part - back_half * sin_part,
            back_half * cos_part + front_half * sin_part,
        ],
        axis=-1,
    )


def unrotate(values, cosine, sines):
    half_width = values.shape[-1] // 2
    front_half = values[..., :half_width]
    back_half = values[..., half_width:]
    cos_part = cosine[:, None, :]
    sin_part = sines[:, None, :]
    return jnp.concatenate(
        [
            front_half * cos_part + back_half * sin_part,
            back_half * cos_part - front_half * sin_part,
        ],
        axis=-1,
    )


def router_parts(group_rows_in, gain_two, router_cols):
    normed_two, hat_two, inv_two = norm_parts(group_rows_in.astype(jnp.float32), gain_two)
    normed_low = normed_two.astype(jnp.bfloat16)
    gates = jax.nn.sigmoid(jnp.dot(normed_low, router_cols, preferred_element_type=jnp.float32))
    return (normed_low, hat_two, inv_two, gates)


def expert_compute(rows_source, safe_rows, up_full, down_full):
    local_experts = safe_rows.shape[0]
    rows_in = rows_source[safe_rows.reshape(-1)].reshape(
        local_experts, safe_rows.shape[1], rows_source.shape[1]
    )
    inner = jnp.einsum("ecd,edg->ecg", rows_in, up_full, preferred_element_type=jnp.float32)
    active = jnp.maximum(inner, 0.0).astype(jnp.bfloat16)
    expert_out = jnp.einsum("ecg,egd->ecd", active, down_full, preferred_element_type=jnp.float32)
    return (rows_in, inner, active, expert_out)


def shards(
    block_input,
    teacher,
    lengths,
    head_routes,
    expert_routes,
    first_gain,
    query_weight,
    key_weight,
    value_weight,
    head_router,
    output_weight,
    second_gain,
    expert_router,
    expert_up,
    expert_down,
):
    tok_rows = block_input.shape[0]
    width = block_input.shape[1]
    col_count = lax.axis_size("col")
    col_index = lax.axis_index("col")
    total_rows = tok_rows * lax.axis_size("row") * col_count
    group_size = tok_rows * col_count
    seq_length = min(MAXLEN, group_size)
    key_span = seq_length // tok_rows
    gated = H * AEXP
    first_full, query_full, key_full, value_full, router_full, output_full, second_full = (
        lax.all_gather(first_gain, ("row", "col"), axis=0, tiled=True),
        lax.all_gather(query_weight, ("row", "col"), axis=0, tiled=True),
        lax.all_gather(key_weight, ("row", "col"), axis=0, tiled=True),
        lax.all_gather(value_weight, ("row", "col"), axis=0, tiled=True),
        lax.all_gather(head_router, ("row", "col"), axis=0, tiled=True),
        lax.all_gather(output_weight, ("row", "col"), axis=1, tiled=True),
        lax.all_gather(second_gain, ("row", "col"), axis=0, tiled=True),
    )
    router_cols, up_full, down_full = (
        lax.all_gather(expert_router, "row", axis=0, tiled=True),
        lax.all_gather(expert_up, "row", axis=1, tiled=True),
        lax.all_gather(expert_down, "row", axis=2, tiled=True),
    )
    token_count = lax.psum(jnp.sum(lengths), "row")
    gain_one = first_full.astype(jnp.float32)
    gain_two = second_full.astype(jnp.float32)
    local_ids = jnp.arange(tok_rows, dtype=jnp.int32)
    group_ids = col_index * tok_rows + local_ids
    seq_pos = group_ids % seq_length
    seq_ids = group_ids // seq_length
    seq_slots = jnp.arange(lengths.shape[0], dtype=jnp.int32)
    tok_length = jnp.sum(
        jnp.where(seq_ids[:, None] == seq_slots[None, :], lengths[None, :], 0), axis=1
    )
    valid = (seq_pos < tok_length).astype(jnp.float32)
    inputs_full = block_input.astype(jnp.float32)
    normed_one, hat_one, inv_one = norm_parts(inputs_full, gain_one)
    normed_low = normed_one.astype(jnp.bfloat16)
    query_raw = jnp.dot(normed_low, query_full, preferred_element_type=jnp.float32)
    key_raw = jnp.dot(normed_low, key_full, preferred_element_type=jnp.float32)
    cosine, sines = rope_tables(seq_pos, DH)
    query_scale = DH ** (-0.5)
    query_rot = (rotate(query_raw.reshape(tok_rows, H, DH), cosine, sines) * query_scale).astype(
        jnp.bfloat16
    )
    key_rot = rotate(key_raw.reshape(tok_rows, H, DH), cosine, sines).astype(jnp.bfloat16)
    route_logits = jnp.dot(normed_low, router_full, preferred_element_type=jnp.float32)
    chosen = jnp.any(
        head_routes[:, :, :, None] == jnp.arange(AEXP, dtype=jnp.int32)[None, None, None, :], axis=2
    ).astype(jnp.float32)
    value_sig = jax.nn.sigmoid(route_logits[:, :gated]).reshape(tok_rows, H, AEXP)
    output_sig = jax.nn.sigmoid(route_logits[:, gated:]).reshape(tok_rows, H, AEXP)
    value_gates = value_sig * chosen
    output_gates = output_sig * chosen
    value_all = jnp.dot(block_input, value_full, preferred_element_type=jnp.float32).reshape(
        tok_rows, H, AEXP, DH
    )
    values_low = jnp.sum(value_all * value_gates[..., None], axis=2).astype(jnp.bfloat16)
    key_parts = [key_rot]
    value_parts = [values_low]
    id_parts = [group_ids]
    for offset in range(1, key_span):
        came_keys, came_values = shifted((key_rot, values_low), "col", offset)
        key_parts.append(came_keys)
        value_parts.append(came_values)
        id_parts.append(group_ids - offset * tok_rows)
    keys_all = jnp.concatenate(key_parts, axis=0)
    values_all = jnp.concatenate(value_parts, axis=0)
    key_ids = jnp.concatenate(id_parts, axis=0)
    allowed = (
        (key_ids[None, :] // seq_length == seq_ids[:, None])
        & (key_ids[None, :] <= group_ids[:, None])
        & (key_ids[None, :] % seq_length < tok_length[:, None])
    )

    def head_scores(head_idx):
        raw_scores = jnp.einsum(
            "qd,kd->qk",
            query_rot[:, head_idx],
            keys_all[:, head_idx],
            preferred_element_type=jnp.float32,
        )
        return jnp.where(allowed, raw_scores, MASKED)

    attended_list = []
    lse_list = []
    for head_idx in range(H):
        scores = head_scores(head_idx)
        row_top = jnp.max(scores, axis=1, keepdims=True)
        exponent = jnp.exp(scores - row_top)
        row_total = jnp.sum(exponent, axis=1, keepdims=True)
        probs_low = (exponent / row_total).astype(jnp.bfloat16)
        attended_list.append(
            jnp.dot(probs_low, values_all[:, head_idx], preferred_element_type=jnp.float32)
        )
        lse_list.append(row_top + jnp.log(row_total))
    attended = jnp.stack(attended_list, axis=1)
    mixed_low = (
        (attended[:, :, None, :] * output_gates[..., None])
        .astype(jnp.bfloat16)
        .reshape(tok_rows, gated * DH)
    )
    resid = inputs_full + jnp.dot(mixed_low, output_full, preferred_element_type=jnp.float32)
    resid_low = resid.astype(jnp.bfloat16)
    group_in = lax.all_gather(resid_low, "col", axis=0, tiled=True)
    normed_two, hat_two, inv_two, expert_gates = router_parts(group_in, gain_two, router_cols)
    local_experts = router_cols.shape[1]
    expert_ids = col_index * local_experts + jnp.arange(local_experts, dtype=jnp.int32)
    member = jnp.any(expert_routes[:, :, None] == expert_ids[None, None, :], axis=1)
    member_float = member.astype(jnp.float32)
    counts_cum = jnp.cumsum(member.astype(jnp.int32), axis=0)
    slot_ids = jnp.arange(CAP, dtype=jnp.int32)

    def count_below(cum_column):
        return jnp.sum((cum_column[None, :] <= slot_ids[:, None]).astype(jnp.int32), axis=1)

    slot_rows = lax.map(count_below, counts_cum.T)
    live_slot = slot_rows < group_size
    live_float = live_slot.astype(jnp.float32)
    safe_rows = jnp.minimum(slot_rows, group_size - 1)
    target_rows = jnp.where(live_slot, slot_rows, group_size).reshape(-1)
    token_rank = jnp.clip(counts_cum.T - 1, 0, CAP - 1)
    rows_in, inner, active, expert_out = expert_compute(group_in, safe_rows, up_full, down_full)
    gate_slots = jnp.take_along_axis(expert_gates.T, safe_rows, axis=1)
    weighted = expert_out * (gate_slots * live_float)[..., None]
    partial_value = (
        jnp.zeros((group_size, width), jnp.float32)
        .at[target_rows]
        .add(weighted.reshape(-1, width), mode="drop")
    )
    expert_sum = lax.psum_scatter(partial_value, "col", scatter_dimension=0, tiled=True)
    output_full_rows = resid + expert_sum
    block_output = output_full_rows.astype(jnp.bfloat16)
    ratio = total_rows / token_count.astype(jnp.float32)
    grad_output = ratio * (output_full_rows - teacher.astype(jnp.float32)) * valid[:, None]
    grad_output_low = grad_output.astype(jnp.bfloat16)
    group_grad = lax.all_gather(grad_output_low, "col", axis=0, tiled=True)
    normed_back, hat_back, inv_back = (normed_two, hat_two, inv_two)
    rows_back, inner_back, active_back, out_back = (rows_in, inner, active, expert_out)
    grad_slot = (
        group_grad[safe_rows.reshape(-1)].reshape(local_experts, CAP, width).astype(jnp.float32)
    )
    grad_expert = (grad_slot * (gate_slots * live_float)[..., None]).astype(jnp.bfloat16)
    gate_grad = jnp.sum(out_back * grad_slot, axis=2) * live_float
    grad_active = jnp.einsum(
        "ecd,egd->ecg", grad_expert, down_full, preferred_element_type=jnp.float32
    )
    grad_inner = jnp.where(inner_back > 0, grad_active, 0.0).astype(jnp.bfloat16)
    down_grads = jnp.einsum(
        "ecg,ecd->egd", active_back, grad_expert, preferred_element_type=jnp.float32
    )
    up_grads = jnp.einsum("ecd,ecg->edg", rows_back, grad_inner, preferred_element_type=jnp.float32)
    slot_back = jnp.einsum("ecg,edg->ecd", grad_inner, up_full, preferred_element_type=jnp.float32)
    grad_rows = (
        jnp.zeros((group_size, width), jnp.float32)
        .at[target_rows]
        .add(slot_back.reshape(-1, width), mode="drop")
    )
    slot_logit = gate_grad * gate_slots * (1.0 - gate_slots)
    logit_grads = jnp.take_along_axis(slot_logit, token_rank, axis=1).T * member_float
    logit_low = logit_grads.astype(jnp.bfloat16)
    router_grad = contract_first(normed_back, logit_low)
    grad_norm_two = contract_last(logit_low, router_cols)
    second_gain_part = jnp.sum(grad_norm_two * hat_back, axis=0)
    grad_rows = grad_rows + norm_back(grad_norm_two, gain_two, hat_back, inv_back)
    moe_grad = lax.psum_scatter(grad_rows, "col", scatter_dimension=0, tiled=True)
    router_sum, up_sum, down_sum = (
        lax.psum_scatter(router_grad, "row", scatter_dimension=0, tiled=True),
        lax.psum_scatter(up_grads, "row", scatter_dimension=1, tiled=True),
        lax.psum_scatter(down_grads, "row", scatter_dimension=2, tiled=True),
    )
    grad_resid = grad_output + moe_grad
    grad_branch = grad_resid.astype(jnp.bfloat16)
    output_grad = contract_first(mixed_low, grad_branch)
    grad_mixed = (
        contract_last(grad_branch, output_full)
        .astype(jnp.bfloat16)
        .astype(jnp.float32)
        .reshape(tok_rows, H, AEXP, DH)
    )
    grad_attended = jnp.sum(grad_mixed * output_gates[..., None], axis=2).astype(jnp.bfloat16)
    grad_output_gates = jnp.sum(grad_mixed * attended[:, :, None, :], axis=3)
    query_grads = []
    key_grads = []
    value_grads = []
    for head_idx in range(H):
        scores = head_scores(head_idx)
        probs_full = jnp.exp(scores - lse_list[head_idx])
        probs_low = probs_full.astype(jnp.bfloat16)
        grad_probs = jnp.einsum(
            "qd,kd->qk",
            grad_attended[:, head_idx],
            values_all[:, head_idx],
            preferred_element_type=jnp.float32,
        )
        grad_scores = (
            probs_full * (grad_probs - jnp.sum(probs_full * grad_probs, axis=1, keepdims=True))
        ).astype(jnp.bfloat16)
        query_grads.append(
            jnp.dot(grad_scores, keys_all[:, head_idx], preferred_element_type=jnp.float32)
        )
        key_grads.append(contract_first(grad_scores, query_rot[:, head_idx]))
        value_grads.append(contract_first(probs_low, grad_attended[:, head_idx]))
    grad_queries = jnp.stack(query_grads, axis=1)
    key_grads_all = jnp.stack(key_grads, axis=1)
    value_grads_all = jnp.stack(value_grads, axis=1)
    grad_key_rot = key_grads_all[:tok_rows]
    grad_values = value_grads_all[:tok_rows]
    for offset in range(1, key_span):
        back_keys, back_values = (
            shifted(
                key_grads_all[offset * tok_rows : (offset + 1) * tok_rows].astype(jnp.bfloat16),
                "col",
                -offset,
            ).astype(jnp.float32),
            shifted(
                value_grads_all[offset * tok_rows : (offset + 1) * tok_rows].astype(jnp.bfloat16),
                "col",
                -offset,
            ).astype(jnp.float32),
        )
        grad_key_rot = grad_key_rot + back_keys
        grad_values = grad_values + back_values
    grad_value_all = (
        (grad_values[:, :, None, :] * value_gates[..., None])
        .astype(jnp.bfloat16)
        .reshape(tok_rows, gated * DH)
    )
    grad_value_gates = jnp.sum(value_all * grad_values[:, :, None, :], axis=3)
    grad_query_raw = (
        unrotate(grad_queries * query_scale, cosine, sines)
        .astype(jnp.bfloat16)
        .reshape(tok_rows, H * DH)
    )
    grad_key_raw = (
        unrotate(grad_key_rot, cosine, sines).astype(jnp.bfloat16).reshape(tok_rows, H * DH)
    )
    grad_route = jnp.concatenate(
        [
            (grad_value_gates * chosen * value_sig * (1.0 - value_sig)).reshape(tok_rows, gated),
            (grad_output_gates * chosen * output_sig * (1.0 - output_sig)).reshape(tok_rows, gated),
        ],
        axis=1,
    ).astype(jnp.bfloat16)
    query_grad = contract_first(normed_low, grad_query_raw)
    key_grad = contract_first(normed_low, grad_key_raw)
    router_head_grad = contract_first(normed_low, grad_route)
    value_grad = contract_first(block_input, grad_value_all)
    grad_norm_one = (
        contract_last(grad_query_raw, query_full)
        + contract_last(grad_key_raw, key_full)
        + contract_last(grad_route, router_full)
    )
    first_gain_part = jnp.sum(grad_norm_one * hat_one, axis=0)
    input_grad = (
        grad_resid
        + norm_back(grad_norm_one, gain_one, hat_one, inv_one)
        + contract_last(grad_value_all, value_full)
    )
    first_sum, query_sum, key_sum, value_sum, router_head_sum, output_sum, second_sum = (
        lax.psum_scatter(first_gain_part, ("row", "col"), scatter_dimension=0, tiled=True),
        lax.psum_scatter(query_grad, ("row", "col"), scatter_dimension=0, tiled=True),
        lax.psum_scatter(key_grad, ("row", "col"), scatter_dimension=0, tiled=True),
        lax.psum_scatter(value_grad, ("row", "col"), scatter_dimension=0, tiled=True),
        lax.psum_scatter(router_head_grad, ("row", "col"), scatter_dimension=0, tiled=True),
        lax.psum_scatter(output_grad, ("row", "col"), scatter_dimension=1, tiled=True),
        lax.psum_scatter(second_gain_part, ("row", "col"), scatter_dimension=0, tiled=True),
    )
    return (
        block_output,
        input_grad,
        first_sum,
        query_sum,
        key_sum,
        value_sum,
        router_head_sum,
        output_sum,
        second_sum,
        router_sum,
        up_sum,
        down_sum,
    )


def solution(mesh):
    return jax.shard_map(
        shards,
        mesh=mesh,
        in_specs=(
            P(("row", "col"), None),
            P(("row", "col"), None),
            P("row"),
            P(("row", "col"), None, None),
            P("row", None),
            P(("row", "col")),
            P(("row", "col"), None),
            P(("row", "col"), None),
            P(("row", "col"), None),
            P(("row", "col"), None),
            P(None, ("row", "col")),
            P(("row", "col")),
            P("row", "col"),
            P("col", "row", None),
            P("col", None, "row"),
        ),
        out_specs=(
            P(("row", "col"), None),
            P(("row", "col"), None),
            P(("row", "col")),
            P(("row", "col"), None),
            P(("row", "col"), None),
            P(("row", "col"), None),
            P(("row", "col"), None),
            P(None, ("row", "col")),
            P(("row", "col")),
            P("row", "col"),
            P("col", "row", None),
            P("col", None, "row"),
        ),
        check_vma=False,
    )
```

profile of v0, /device:TPU:0, one launch (start us, length us, event | category | flops | bytes accessed | tf_op | source)
XLA Modules:
  0.0 2219.0 jit_solution(12689136263649341197)
XLA Ops:
  11.7 42.0 %all-reduce.5 = (bf16[1024]{0:T(1024)(128)(2,1)S(1)}, bf16[1024]{0:T(1024)(128)(2,1)S(1)}) all-reduce(bf16[1024]{0:T(1024)(128)(2,1)S(1)} %dynamic-update-slice, bf16[1024]{0:T(1024)(128)(2,1)S(1)} %dynamic-update-slice.1), channel_id=1, replica_groups=mesh['row'=16,'col'=2] {'row','col'}, use_global_device_ids=true, to_apply=%add | all-reduce | flops 2048 | bytes 8192
  54.4 41.3 %all_gather.40 = bf16[1024,40]{1,0:T(8,128)(2,1)S(1)} all-gather(bf16[32,40]{1,0:T(8,128)(2,1)} %param.26), channel_id=1, replica_groups=mesh['row'=16,'col'=2] {'row','col'}, dimensions={0}, use_global_device_ids=true | all-gather | bytes 84480 | tf_op jit(solution)/shard_map/all_gather | solution.py:138
  100.0 3.0 fusion.115
  103.0 19.9 all-gather.10.cloned.1.call-done
  135.3 54.8 %all-gather.14.cloned.1.call-done = bf16[1024,2560]{1,0:T(8,128)(2,1)} async-done(((bf16[32,2560]{1,0:T(8,128)(2,1)}), bf16[1024,2560]{1,0:T(8,128)(2,1)}) %all-gather.14.cloned.1.call-update) | async-done | bytes 5242896 | tf_op jit(solution)/shard_map/all_gather | solution.py:137
  190.0 4.9 fusion.116
  197.2 2.6 collective-permute-start.1
  210.8 45.8 %all-gather.16.cloned.1.call-done = bf16[2560,1024]{0,1:T(8,128)(2,1)} async-done(((bf16[2560,32]{0,1:T(8,128)(2,1)}), bf16[2560,1024]{0,1:T(8,128)(2,1)}) %all-gather.16.cloned.1.call-update) | async-done | bytes 5242896 | tf_op jit(solution)/shard_map/all_gather | solution.py:139
  256.6 7.9 fusion.113
  266.7 4.5 reduce-window.6
  272.3 8.5 while.12
  281.0 38.8 %all-gather = bf16[16,64,16]{1,2,0:T(8,128)(2,1)S(1)} all-gather(bf16[1,64,16]{1,2,0:T(8,128)(2,1)S(1)} %bitcast.294), channel_id=1, replica_groups=mesh['row'=16,'col'=2] {'row'}, dimensions={0}, use_global_device_ids=true | all-gather | bytes 34816 | tf_op jit(solution)/shard_map/all_gather | solution.py:143
  325.8 97.2 %gather_fusion.2 = f32[12288]{0:T(1024)S(1)} fusion(f32[16,1024]{1,0:T(8,128)S(1)} %fusion.54, s32[12288]{0:T(1024)S(1)} %reshape.577), kind=kCustom, calls=%fused_computation.2 | custom fusion | bytes 196608 | tf_op jit(solution)/shard_map/jit(take_along_axis)/gather | solution.py:247
  423.1 52.6 %gather_fusion = bf16[12288,1024]{1,0:T(8,128)(2,1)} fusion(bf16[1024,1024]{1,0:T(8,128)(2,1)S(1)} %copy-done, s32[12288]{0:T(1024)S(1)} %broadcast_clamp_fusion), kind=kCustom, calls=%fused_computation | custom fusion | bytes 50380800 | tf_op jit(solution)/shard_map/gather | solution.py:98
  475.7 13.5 fusion.21
  489.2 36.0 %broadcast_multiply_fusion = (f32[16,768,1024]{2,1,0:T(8,128)}, f32[16,768,1024]{2,1,0:T(8,128)}) fusion(f32[16,768]{1,0:T(8,128)S(1)} %broadcast_select_fusion, bf16[16,128,1024]{1,2,0:T(8,128)(2,1)} %all-gather.22.cloned.1.call-done, bf16[16,768,128]{2,1,0:T(8,128)(2,1)S(1)} %get-tuple-element.168), kind=kOutput, calls=%fused_computation.14 | convolution fusion | flops 3238526976 | bytes 108052480 | tf_op jit(solution)/shard_map/ecg,egd->ecd/dot_general | solution.py:103
  525.2 108.2 %scatter_custom_fusion = f32[1024,1024]{1,0:T(8,128)} fusion(s32[12288]{0:T(1024)S(1)} %bitcast.286, f32[12288,1024]{1,0:T(8,128)} %bitcast.269, f32[]{:T(128)} %constant.134.clone.1), kind=kCustom, calls=%fused_computation.79 | custom fusion | flops 12582912 | bytes 4194816 | tf_op jit(solution)/shard_map/scatter-add | solution.py:252
  633.5 9.1 psum.7
  643.4 2.9 fusion.49
  646.5 12.8 all-gather.24.cloned.1.call-done
  659.3 62.2 %gather_fusion.1 = bf16[12288,1024]{1,0:T(8,128)(2,1)} fusion(bf16[1024,1024]{1,0:T(8,128)(2,1)} %all-gather.24.cloned.1.call-done, s32[12288]{0:T(1024)S(1)} %broadcast_clamp_fusion), kind=kCustom, calls=%fused_computation.1 | custom fusion | bytes 50380800 | tf_op jit(solution)/shard_map/gather | solution.py:264
  721.5 23.4 %fusion.2 = f32[16,768]{1,0:T(8,128)S(1)} fusion(f32[16,768,1024]{2,1,0:T(8,128)} %get-tuple-element.165, bf16[16,768,1024]{2,1,0:T(8,128)(2,1)} %bitcast.266), kind=kLoop, calls=%fused_computation.12 | loop fusion | flops 37736448 | bytes 75546624 | tf_op jit(solution)/shard_map/reduce_sum | solution.py:267
  745.0 138.9 %gather_fusion.3 = bf16[16384]{0:T(1024)(128)(2,1)S(1)} fusion(bf16[16,768]{1,0:T(8,128)(2,1)S(1)} %subtract_multiply_fusion, s32[16384]{0:T(1024)S(1)} %bitcast.262), kind=kCustom, calls=%fused_computation.3 | custom fusion | bytes 196608 | tf_op jit(solution)/shard_map/jit(take_along_axis)/gather | solution.py:283
  884.1 3.8 fusion.19
  887.9 14.2 select_convert_fusion
  902.1 21.4 fusion.118
  923.5 4.2 fusion.18
  927.7 109.8 %scatter_fusion = f32[1024,1024]{1,0:T(8,128)} fusion(f32[1024,1024]{1,0:T(8,128)} %fusion.18, s32[12288]{0:T(1024)S(1)} %bitcast.287, f32[12288,1024]{1,0:T(8,128)} %bitcast.263), kind=kCustom, calls=%fused_computation.5 | custom fusion | flops 12582912 | bytes 151044096 | tf_op jit(solution)/shard_map/scatter-add | solution.py:280
  1041.0 10.0 reduce-scatter.17.cloned.1.call-done
  1051.0 4.3 fusion.48
  1056.7 7.2 fusion.14
  1063.9 6.0 copy.118
  1069.9 3.7 multiply_reduce_fusion.2
  1093.4 5.4 multiply_convert_fusion
  1108.1 14.8 fusion.122
  1124.8 15.9 fusion.4
  1142.4 7.2 fusion.64
  1150.8 7.2 convolution_bitcast_fusion
  1158.0 11.5 copy.136
  1174.5 41.4 %all-reduce.4 = (f32[1024]{0:T(1024)S(1)}, f32[1024]{0:T(1024)S(1)}) all-reduce(f32[1024]{0:T(1024)S(1)} %get-tuple-element.108, f32[1024]{0:T(1024)S(1)} %copy-done.102), channel_id=4, replica_groups=mesh['row'=16,'col'=2] {'row','col'}, use_global_device_ids=true, to_apply=%region_38.39.clone | all-reduce | flops 2048 | bytes 16384
  1217.1 8.8 fusion.33
  1225.8 41.2 %reduce-scatter.23.cloned.1.call-done = f32[32,40]{1,0:T(8,128)} async-done(((f32[1024,40]{1,0:T(8,128)}), f32[32,40]{1,0:T(8,128)}) %reduce-scatter.23.cloned.1.call-update) | async-done | bytes 5136 | tf_op jit(solution)/shard_map/reduce_scatter | solution.py:388
  1267.0 137.2 %reduce-scatter.21.cloned.1.call-done = f32[32,512]{1,0:T(8,128)} async-done(((f32[1024,512]{1,0:T(8,128)}), f32[32,512]{1,0:T(8,128)}) %reduce-scatter.21.cloned.1.call-update) | async-done | bytes 65552 | tf_op jit(solution)/shard_map/reduce_scatter | solution.py:386
  1404.2 137.0 %reduce-scatter.19.cloned.1.call-done = f32[32,512]{1,0:T(8,128)} async-done(((f32[1024,512]{1,0:T(8,128)}), f32[32,512]{1,0:T(8,128)}) %reduce-scatter.19.cloned.1.call-update) | async-done | bytes 65552 | tf_op jit(solution)/shard_map/reduce_scatter | solution.py:385
  1541.2 176.5 %reduce-scatter.27.cloned.1.call-done = f32[16,64,128]{2,1,0:T(8,128)} async-done(((f32[16,1024,128]{2,1,0:T(8,128)}), f32[16,64,128]{2,1,0:T(8,128)}) %reduce-scatter.27.cloned.1.call-update) | async-done | bytes 524304 | tf_op jit(solution)/shard_map/reduce_scatter | solution.py:292
  1717.7 183.0 %reduce-scatter.29.cloned.1.call-done = f32[16,128,64]{1,2,0:T(8,128)} async-done(((f32[16,128,1024]{1,2,0:T(8,128)}), f32[16,128,64]{1,2,0:T(8,128)}) %reduce-scatter.29.cloned.1.call-update) | async-done | bytes 524304 | tf_op jit(solution)/shard_map/reduce_scatter | solution.py:293
  1900.7 158.3 %reduce-scatter.25.cloned.1.call-done = f32[2560,32]{0,1:T(8,128)} async-done(((f32[2560,1024]{0,1:T(8,128)}), f32[2560,32]{0,1:T(8,128)}) %reduce-scatter.25.cloned.1.call-update) | async-done | bytes 327696 | tf_op jit(solution)/shard_map/reduce_scatter | solution.py:389
  2059.1 152.9 %reduce-scatter.31.cloned.1.call-done = f32[32,2560]{1,0:T(8,128)} async-done(((f32[1024,2560]{1,0:T(8,128)}), f32[32,2560]{1,0:T(8,128)}) %reduce-scatter.31.cloned.1.call-update) | async-done | bytes 327696
  (461 shorter events, 95.6 us)
Async XLA Ops:
  7.2 90.1 %copy-start.17 = (bf16[512,1024]{1,0:T(8,128)(2,1)S(1)}, bf16[512,1024]{1,0:T(8,128)(2,1)}, u32[]{:S(2)}) copy-start(bf16[512,1024]{1,0:T(8,128)(2,1)} %param.17) | copy-start | bytes 3145732
  7.2 92.8 %all-gather.12.cloned.1.call-start = ((), (), s32[]{:S(2)}) async-start(), calls=%async_computation.11 | async-start | bytes 1081344 | tf_op jit(solution)/shard_map/all_gather | solution.py:136
  7.9 115.0 %all-gather.10.cloned.1.call-start = ((), (), s32[]{:S(2)}) async-start(), calls=%async_computation.10 | async-start | bytes 1081344 | tf_op jit(solution)/shard_map/all_gather | solution.py:135
  8.7 181.4 %all-gather.14.cloned.1.call-start = ((), (), s32[]{:S(2)}) async-start(), calls=%async_computation.12 | async-start | bytes 5406720 | tf_op jit(solution)/shard_map/all_gather | solution.py:137
  9.4 247.2 %all-gather.16.cloned.1.call-start = ((), (), s32[]{:S(2)}) async-start(), calls=%async_computation.13 | async-start | bytes 5406720 | tf_op jit(solution)/shard_map/all_gather | solution.py:139
  10.0 310.2 %all-gather.18.cloned.1.call-start = ((), (), s32[]{:S(2)}) async-start(), calls=%async_computation.14 | async-start | bytes 3145728 | tf_op jit(solution)/shard_map/all_gather | solution.py:228
  53.7 44.0 %copy-start.73 = (f32[1024]{0:T(1024)}, f32[1024]{0:T(1024)S(1)}, u32[]{:S(2)}) copy-start(f32[1024]{0:T(1024)S(1)} %convert_element_type.170) | copy-start | bytes 12292
  98.8 24.1 %copy-start.12 = (bf16[512,1024]{1,0:T(8,128)(2,1)}, bf16[512,1024]{1,0:T(8,128)(2,1)S(1)}, u32[]{:S(2)}) copy-start(bf16[512,1024]{1,0:T(8,128)(2,1)S(1)} %fusion.28) | copy-start | bytes 3145732
  99.4 28.2 %copy-start.68 = (pred[512,4,5]{0,1,2:T(4,128)(4,1)}, pred[512,4,5]{0,1,2:T(4,128)(4,1)S(1)}, u32[]{:S(2)}) copy-start(pred[512,4,5]{0,1,2:T(4,128)(4,1)S(1)} %fusion.78) | copy-start | bytes 30724
  99.9 25.0 %copy-start.43 = (f32[512,64]{0,1:T(8,128)}, f32[512,64]{0,1:T(8,128)S(1)}, u32[]{:S(2)}) copy-start(f32[512,64]{0,1:T(8,128)S(1)} %get-tuple-element.152) | copy-start | bytes 393220
  99.9 25.0 %copy-start.45 = (f32[512,64]{0,1:T(8,128)}, f32[512,64]{0,1:T(8,128)S(1)}, u32[]{:S(2)}) copy-start(f32[512,64]{0,1:T(8,128)S(1)} %get-tuple-element.153) | copy-start | bytes 393220
  125.4 3.6 collective-permute-start
  128.3 66.7 %copy-start.56 = (f32[512,4,5]{0,2,1:T(8,128)}, f32[512,4,5]{0,2,1:T(8,128)S(1)}, u32[]{:S(2)}) copy-start(f32[512,4,5]{0,2,1:T(8,128)S(1)} %copy.106) | copy-start | bytes 122884
  128.4 80.2 %copy-start.58 = (f32[512,4,5]{0,2,1:T(8,128)}, f32[512,4,5]{0,2,1:T(8,128)S(1)}, u32[]{:S(2)}) copy-start(f32[512,4,5]{0,2,1:T(8,128)S(1)} %copy.113) | copy-start | bytes 122884
  130.0 72.8 %copy-start.85 = (f32[512]{0:T(512)}, f32[512]{0:T(512)S(1)}, u32[]{:S(2)}) copy-start(f32[512]{0:T(512)S(1)} %get-tuple-element.154) | copy-start | bytes 6148
  131.8 71.0 %copy-start.87 = (f32[512]{0:T(512)}, f32[512]{0:T(512)S(1)}, u32[]{:S(2)}) copy-start(f32[512]{0:T(512)S(1)} %fusion.43) | copy-start | bytes 6148
  132.6 73.9 %copy-start.89 = (f32[512]{0:T(512)}, f32[512]{0:T(512)S(1)}, u32[]{:S(2)}) copy-start(f32[512]{0:T(512)S(1)} %get-tuple-element.156) | copy-start | bytes 6148
  134.5 72.1 %copy-start.91 = (f32[512]{0:T(512)}, f32[512]{0:T(512)S(1)}, u32[]{:S(2)}) copy-start(f32[512]{0:T(512)S(1)} %fusion.42) | copy-start | bytes 6148
  135.3 70.7 %copy-start.2 = (f32[512,1024]{1,0:T(8,128)}, f32[512,1024]{1,0:T(8,128)S(1)}, u32[]{:S(2)}) copy-start(f32[512,1024]{1,0:T(8,128)S(1)} %get-tuple-element.159) | copy-start | bytes 6291460
  135.3 70.7 %copy-start.93 = (f32[512]{0:T(512)}, f32[512]{0:T(512)S(1)}, u32[]{:S(2)}) copy-start(f32[512]{0:T(512)S(1)} %get-tuple-element.158) | copy-start | bytes 6148
  197.2 5.5 collective-permute-start.1
  208.5 55.9 %copy-start.21 = (f32[512,4,128]{0,2,1:T(8,128)}, f32[512,4,128]{0,2,1:T(8,128)S(1)}, u32[]{:S(2)}) copy-start(f32[512,4,128]{0,2,1:T(8,128)S(1)} %copy.111) | copy-start | bytes 3145732
  264.5 16.5 copy-start.101
  264.5 211.2 %all-gather.20.cloned.1.call-start = ((), (), s32[]{:S(2)}) async-start(), calls=%async_computation.15 | async-start | bytes 4456448 | tf_op jit(solution)/shard_map/all_gather | solution.py:144
  265.1 224.1 %all-gather.22.cloned.1.call-start = ((), (), s32[]{:S(2)}) async-start(), calls=%async_computation.16 | async-start | bytes 4456448 | tf_op jit(solution)/shard_map/all_gather | solution.py:145
  265.8 377.5 %reduce-scatter.15.cloned.1.call-start = ((), (), s32[]{:S(2)}) async-start(), calls=%async_computation.17 | async-start | bytes 6291456 | tf_op jit(solution)/shard_map/reduce_scatter | solution.py:254
  281.0 42.1 %copy-start.75 = (f32[1024]{0:T(1024)}, f32[1024]{0:T(1024)S(1)}, u32[]{:S(2)}) copy-start(f32[1024]{0:T(1024)S(1)} %convert_element_type.186) | copy-start | bytes 12292
  475.7 412.2 %copy-start.54 = (f32[16,768]{1,0:T(8,128)}, f32[16,768]{1,0:T(8,128)S(1)}, u32[]{:S(2)}) copy-start(f32[16,768]{1,0:T(8,128)S(1)} %broadcast_select_fusion) | copy-start | bytes 147460
  489.2 36.0 %copy-start.26 = (bf16[16,768,128]{2,1,0:T(8,128)(2,1)}, bf16[16,768,128]{2,1,0:T(8,128)(2,1)S(1)}, u32[]{:S(2)}) copy-start(bf16[16,768,128]{2,1,0:T(8,128)(2,1)S(1)} %get-tuple-element.168) | copy-start | bytes 9437188
  633.4 25.9 %all-gather.24.cloned.1.call-start = ((), (), s32[]{:S(2)}) async-start(), calls=%async_computation.18 | async-start | bytes 3145728 | tf_op jit(solution)/shard_map/all_gather | solution.py:260
  646.4 404.7 %reduce-scatter.17.cloned.1.call-start = ((), (), s32[]{:S(2)}) async-start(), calls=%async_computation.19 | async-start | bytes 6291456 | tf_op jit(solution)/shard_map/reduce_scatter | solution.py:289
  744.9 139.0 %copy-start.61 = (s32[16,8,128]{2,1,0:T(8,128)S(1)}, s32[16,8,128]{2,1,0:T(8,128)}, u32[]{:S(2)}) copy-start(s32[16,8,128]{2,1,0:T(8,128)} %copy-done.60) | copy-start | bytes 196612
  745.0 139.0 %copy-start.63 = (pred[1024,16]{0,1:T(8,128)(4,1)S(1)}, pred[1024,16]{0,1:T(8,128)(4,1)}, u32[]{:S(2)}) copy-start(pred[1024,16]{0,1:T(8,128)(4,1)} %copy-done.62) | copy-start | bytes 49156
  745.0 139.1 %copy-start.1 = (bf16[1024,1024]{1,0:T(8,128)(2,1)S(1)}, bf16[1024,1024]{1,0:T(8,128)(2,1)}, u32[]{:S(2)}) copy-start(bf16[1024,1024]{1,0:T(8,128)(2,1)} %all-gather.18.cloned.1.call-done) | copy-start | bytes 6291460
  745.0 139.1 %copy-start.65 = (bf16[1024,16]{0,1:T(8,128)(2,1)S(1)}, bf16[1024,16]{0,1:T(8,128)(2,1)}, u32[]{:S(2)}) copy-start(bf16[1024,16]{0,1:T(8,128)(2,1)} %copy-done.64) | copy-start | bytes 98308
  745.0 139.1 %copy-start.71 = (f32[1024]{0:T(1024)S(1)}, f32[1024]{0:T(1024)}, u32[]{:S(2)}) copy-start(f32[1024]{0:T(1024)} %copy-done.70) | copy-start | bytes 12292
  745.0 139.1 %copy-start.76 = (f32[1024]{0:T(1024)S(1)}, f32[1024]{0:T(1024)}, u32[]{:S(2)}) copy-start(f32[1024]{0:T(1024)} %copy-done.75) | copy-start | bytes 12292
  745.0 139.1 %copy-start.78 = (f32[1024]{0:T(1024)S(1)}, f32[1024]{0:T(1024)}, u32[]{:S(2)}) copy-start(f32[1024]{0:T(1024)} %copy-done.77) | copy-start | bytes 12292
  1037.7 131.8 %reduce-scatter.33.cloned.1.call-start = ((), (), s32[]{:S(2)}) async-start(), calls=%async_computation.27 | async-start | bytes 557056
  1041.0 226.0 %reduce-scatter.23.cloned.1.call-start = ((), (), s32[]{:S(2)}) async-start(), calls=%async_computation.22 | async-start | bytes 540672 | tf_op jit(solution)/shard_map/reduce_scatter | solution.py:388
  1083.0 9.0 collective-permute-start.3
  1088.2 12.1 collective-permute-start.2
  1100.3 303.9 %reduce-scatter.21.cloned.1.call-start = ((), (), s32[]{:S(2)}) async-start(), calls=%async_computation.21 | async-start | bytes 2162688 | tf_op jit(solution)/shard_map/reduce_scatter | solution.py:386
  1105.0 436.2 %reduce-scatter.19.cloned.1.call-start = ((), (), s32[]{:S(2)}) async-start(), calls=%async_computation.20 | async-start | bytes 2162688 | tf_op jit(solution)/shard_map/reduce_scatter | solution.py:385
  1108.1 609.6 %reduce-scatter.27.cloned.1.call-start = ((), (), s32[]{:S(2)}) async-start(), calls=%async_computation.24 | async-start | bytes 8912896 | tf_op jit(solution)/shard_map/reduce_scatter | solution.py:292
  1123.0 777.8 %reduce-scatter.29.cloned.1.call-start = ((), (), s32[]{:S(2)}) async-start(), calls=%async_computation.25 | async-start | bytes 8912896 | tf_op jit(solution)/shard_map/reduce_scatter | solution.py:293
  1140.7 918.3 %reduce-scatter.25.cloned.1.call-start = ((), (), s32[]{:S(2)}) async-start(), calls=%async_computation.23 | async-start | bytes 10813440 | tf_op jit(solution)/shard_map/reduce_scatter | solution.py:389
  1149.6 1062.3 %reduce-scatter.31.cloned.1.call-start = ((), (), s32[]{:S(2)}) async-start(), calls=%async_computation.26 | async-start | bytes 10813440
  (78 other events, 221.6 us)
Sparse Core Ops, SparseCore 0:
  10.9 56.4 all-gather.11
  70.2 52.5 all-gather.9
  125.7 64.2 all-gather.13
  192.8 63.7 all-gather.15
  264.6 9.1 all-gather.17
  276.4 77.3 all-gather.19
  356.5 75.4 all-gather.21
  633.5 7.8 reduce-scatter.14
  646.5 12.7 all-gather.23
  1037.8 13.1 reduce-scatter.16
  1053.3 78.7 reduce-scatter.32
  1134.8 132.1 reduce-scatter.22
  1269.8 134.3 reduce-scatter.20
  1406.9 134.2 reduce-scatter.18
  1543.9 173.7 reduce-scatter.26
  1720.4 180.2 reduce-scatter.28
  1903.4 155.5 reduce-scatter.24
  2061.8 150.0 reduce-scatter.30
where the time goes:
time: 2230 us; the launch traced here: 2220 us
  waiting for transfers between devices  1130 us (51%)
  local copies, waits for them, and re-layouts  401 us (18%)
  other arithmetic  291 us (13%)
  matrix products  193 us (9%)
  blocking collectives  173 us (8%)
    reduce_scatter x1, waiting for transfers between devices, shards(): lax.psum_scatter(down_grads, 'row', scatter_dimension=2, tiled=True)  183 us
    reduce_scatter x1, waiting for transfers between devices, shards(): lax.psum_scatter(up_grads, 'row', scatter_dimension=1, tiled=True)  176 us
    reduce_scatter x1, waiting for transfers between devices, shards(): lax.psum_scatter(output_grad, ('row', 'col'), scatter_dimension=1, tiled=...  158 us
    unnamed x20, waiting for transfers between devices  157 us
    gather x2, local copies, waits for them, and re-layouts, shards(): jnp.take_along_axis(slot_logit, token_rank, axis=1).T * member_float  139 us
    reduce_scatter x1, waiting for transfers between devices, shards(): lax.psum_scatter(key_grad, ('row', 'col'), scatter_dimension=0, tiled=True)  137 us
    reduce_scatter x1, waiting for transfers between devices, shards(): lax.psum_scatter(query_grad, ('row', 'col'), scatter_dimension=0, tiled=T...  137 us
    scatter-add x1, other arithmetic, shards(): grad_rows = jnp.zeros((group_size, width), jnp.float32).at[target_rows].a...  110 us
  transfers between devices with their start and end apart: 22, of which 13 were waited for; matrix products, arithmetic and copies ran while one was open for 15% of the time, Pallas kernels for 0%

commit v1 on v0

--- a/solution.py
+++ b/solution.py
@@ -9,7 +9,6 @@
 DH = 128
 AEXP = 5
 MAXLEN = 2048
-CAP = 768
 
 
 EPS = 1e-05
@@ -32,6 +31,114 @@
     return lax.dot_general(
         left, right, (((0,), (0,)), ((), ())), preferred_element_type=jnp.float32
     )
+
+
+GRID = (4, 2, 2)
+ORDER_A, ORDER_B, ORDER_C = ((0, 1, 2), (1, 2, 0), (2, 0, 1))
+
+
+def by_grid():
+    return lax.axis_size("row") == math.prod(GRID) and lax.axis_size("col") == 2
+
+
+def grid_place(dim):
+    row = lax.axis_index("row")
+    return (row // 4, (row // 2) % 2, row % 2)[dim]
+
+
+def grid_pairs(dim, steps):
+    pairs = []
+    for row in range(math.prod(GRID)):
+        place = [row // 4, (row // 2) % 2, row % 2]
+        place[dim] = (place[dim] + steps) % GRID[dim]
+        pairs.append((row, (place[0] * 2 + place[1]) * 2 + place[2]))
+    return pairs
+
+
+def sibling(value):
+    return lax.ppermute(value, "col", [(0, 1), (1, 0)])
+
+
+def gather_row(part, order):
+    if not by_grid():
+        return lax.all_gather(part, "row", axis=0, tiled=True)
+    held = part.reshape((1, 1, 1) + part.shape)
+    for dim in order:
+        size, place = (GRID[dim], grid_place(dim))
+        came = [lax.ppermute(held, "row", grid_pairs(dim, k)) for k in range(1, size)]
+        shape = list(held.shape)
+        shape[dim] = size
+        whole = lax.dynamic_update_slice_in_dim(jnp.zeros(shape, held.dtype), held, place, dim)
+        for k, block in zip(range(1, size), came):
+            whole = lax.dynamic_update_slice_in_dim(whole, block, (place - k) % size, dim)
+        held = whole
+    return held.reshape((-1,) + part.shape[1:])
+
+
+def gather_all(part, order):
+    if not by_grid():
+        return lax.all_gather(part, ("row", "col"), axis=0, tiled=True)
+    rows, wide = part.shape
+    mine = gather_row(part, order).reshape(-1, 1, rows, wide)
+    other = sibling(mine)
+    core = lax.axis_index("col")
+    whole = lax.dynamic_update_slice_in_dim(
+        jnp.zeros((mine.shape[0], 2, rows, wide), part.dtype), mine, core, 1
+    )
+    whole = lax.dynamic_update_slice_in_dim(whole, other, 1 - core, 1)
+    return whole.reshape(-1, wide)
+
+
+def scatter_row(total, order):
+    if not by_grid():
+        return lax.psum_scatter(total, "row", scatter_dimension=0, tiled=True)
+    rows = total.shape[0] // math.prod(GRID)
+    held = total.reshape(GRID + (rows, total.shape[1]))
+    for dim in order[::-1]:
+        size, place = (GRID[dim], grid_place(dim))
+        own = lax.dynamic_slice_in_dim(held, place, 1, dim).astype(jnp.float32)
+        for k in range(1, size):
+            leaving = lax.dynamic_slice_in_dim(held, (place + k) % size, 1, dim)
+            came = lax.ppermute(leaving.astype(jnp.bfloat16), "row", grid_pairs(dim, k))
+            own = own + came.astype(jnp.float32)
+        held = own
+    return held.reshape(rows, total.shape[1])
+
+
+def scatter_all(total, order):
+    if not by_grid():
+        return lax.psum_scatter(total, ("row", "col"), scatter_dimension=0, tiled=True)
+    rows = total.shape[0] // (2 * math.prod(GRID))
+    core = lax.axis_index("col")
+    split = total.reshape(-1, 2, rows, total.shape[1])
+    mine = lax.dynamic_slice_in_dim(split, core, 1, 1)
+    leaving = lax.dynamic_slice_in_dim(split, 1 - core, 1, 1).astype(jnp.bfloat16)
+    summed = mine + sibling(leaving).astype(jnp.float32)
+    return scatter_row(summed.reshape(-1, total.shape[1]), order)
+
+
+def gather_col(value):
+    if lax.axis_size("col") != 2:
+        return lax.all_gather(value, "col", axis=0, tiled=True)
+    core = lax.axis_index("col")
+    rows = value.shape[0]
+    whole = jnp.zeros((2 * rows,) + value.shape[1:], value.dtype)
+    whole = lax.dynamic_update_slice_in_dim(whole, value, core * rows, 0)
+    return lax.dynamic_update_slice_in_dim(whole, sibling(value), (1 - core) * rows, 0)
+
+
+def scatter_col(total):
+    if lax.axis_size("col") != 2:
+        return lax.psum_scatter(total, "col", scatter_dimension=0, tiled=True)
+    core = lax.axis_index("col")
+    rows = total.shape[0] // 2
+    leaving = lax.dynamic_slice_in_dim(total, (1 - core) * rows, rows, 0).astype(jnp.bfloat16)
+    mine = lax.dynamic_slice_in_dim(total, core * rows, rows, 0)
+    return mine + sibling(leaving).astype(jnp.float32)
+
+
+def padded(value, wide):
+    return jnp.pad(value, ((0, 0), (0, wide - value.shape[1])))
 
 
 def norm_parts(values, gain):
@@ -84,24 +191,6 @@
         ],
         axis=-1,
     )
-
-
-def router_parts(group_rows_in, gain_two, router_cols):
-    normed_two, hat_two, inv_two = norm_parts(group_rows_in.astype(jnp.float32), gain_two)
-    normed_low = normed_two.astype(jnp.bfloat16)
-    gates = jax.nn.sigmoid(jnp.dot(normed_low, router_cols, preferred_element_type=jnp.float32))
-    return (normed_low, hat_two, inv_two, gates)
-
-
-def expert_compute(rows_source, safe_rows, up_full, down_full):
-    local_experts = safe_rows.shape[0]
-    rows_in = rows_source[safe_rows.reshape(-1)].reshape(
-        local_experts, safe_rows.shape[1], rows_source.shape[1]
-    )
-    inner = jnp.einsum("ecd,edg->ecg", rows_in, up_full, preferred_element_type=jnp.float32)
-    active = jnp.maximum(inner, 0.0).astype(jnp.bfloat16)
-    expert_out = jnp.einsum("ecg,egd->ecd", active, down_full, preferred_element_type=jnp.float32)
-    return (rows_in, inner, active, expert_out)
 
 
 def shards(
@@ -130,23 +219,47 @@
     seq_length = min(MAXLEN, group_size)
     key_span = seq_length // tok_rows
     gated = H * AEXP
-    first_full, query_full, key_full, value_full, router_full, output_full, second_full = (
-        lax.all_gather(first_gain, ("row", "col"), axis=0, tiled=True),
-        lax.all_gather(query_weight, ("row", "col"), axis=0, tiled=True),
-        lax.all_gather(key_weight, ("row", "col"), axis=0, tiled=True),
-        lax.all_gather(value_weight, ("row", "col"), axis=0, tiled=True),
-        lax.all_gather(head_router, ("row", "col"), axis=0, tiled=True),
-        lax.all_gather(output_weight, ("row", "col"), axis=1, tiled=True),
-        lax.all_gather(second_gain, ("row", "col"), axis=0, tiled=True),
-    )
-    router_cols, up_full, down_full = (
-        lax.all_gather(expert_router, "row", axis=0, tiled=True),
-        lax.all_gather(expert_up, "row", axis=1, tiled=True),
-        lax.all_gather(expert_down, "row", axis=2, tiled=True),
-    )
-    token_count = lax.psum(jnp.sum(lengths), "row")
-    gain_one = first_full.astype(jnp.float32)
-    gain_two = second_full.astype(jnp.float32)
+    half_heads = gated * DH // 2
+    local_experts = expert_up.shape[0]
+    hidden_local = expert_up.shape[2]
+    hidden = local_experts * hidden_local
+    length_sum = jnp.sum(lengths)
+    small_parts = [
+        query_weight,
+        key_weight,
+        head_router,
+        first_gain[:, None],
+        second_gain[:, None],
+    ]
+    for digits in (length_sum // 64, length_sum % 64):
+        small_parts.append(
+            jnp.broadcast_to(digits.astype(jnp.bfloat16)[None, None], (first_gain.shape[0], 1))
+        )
+    lead_local = padded(jnp.concatenate(small_parts, axis=1), 2 * H * DH + 128)
+    lead_full = gather_all(lead_local, ORDER_B)
+    value_one = gather_all(value_weight[:, :half_heads], ORDER_A)
+    value_two = gather_all(value_weight[:, half_heads:], ORDER_C)
+    up_local = jnp.concatenate(
+        [
+            jnp.transpose(expert_up, (1, 0, 2)).reshape(-1, hidden),
+            padded(expert_router, 128),
+        ],
+        axis=1,
+    )
+    down_local = jnp.transpose(expert_down, (2, 0, 1)).reshape(-1, hidden)
+    output_turned = gather_all(output_weight.T, ORDER_B)
+    up_wide = gather_row(up_local, ORDER_A)
+    down_turned = gather_row(down_local, ORDER_C)
+    up_full = up_wide[:, :hidden]
+    router_cols = up_wide[:, hidden : hidden + local_experts]
+    query_full = lead_full[:, : H * DH]
+    key_full = lead_full[:, H * DH : 2 * H * DH]
+    router_full = lead_full[:, 2 * H * DH : 2 * H * DH + 2 * gated]
+    extra = lead_full[:, 2 * H * DH + 2 * gated :].astype(jnp.float32)
+    gain_one = extra[:, 0]
+    gain_two = extra[:, 1]
+    stride = first_gain.shape[0] * col_count
+    token_count = jnp.sum(extra[::stride, 2]) * 64.0 + jnp.sum(extra[::stride, 3])
     local_ids = jnp.arange(tok_rows, dtype=jnp.int32)
     group_ids = col_index * tok_rows + local_ids
     seq_pos = group_ids % seq_length
@@ -175,9 +288,13 @@
     output_sig = jax.nn.sigmoid(route_logits[:, gated:]).reshape(tok_rows, H, AEXP)
     value_gates = value_sig * chosen
     output_gates = output_sig * chosen
-    value_all = jnp.dot(block_input, value_full, preferred_element_type=jnp.float32).reshape(
-        tok_rows, H, AEXP, DH
-    )
+    value_all = jnp.concatenate(
+        [
+            jnp.dot(block_input, value_one, preferred_element_type=jnp.float32),
+            jnp.dot(block_input, value_two, preferred_element_type=jnp.float32),
+        ],
+        axis=1,
+    ).reshape(tok_rows, H, AEXP, DH)
     values_low = jnp.sum(value_all * value_gates[..., None], axis=2).astype(jnp.bfloat16)
     key_parts = [key_rot]
     value_parts = [values_low]
@@ -223,80 +340,57 @@
         .astype(jnp.bfloat16)
         .reshape(tok_rows, gated * DH)
     )
-    resid = inputs_full + jnp.dot(mixed_low, output_full, preferred_element_type=jnp.float32)
+    resid = inputs_full + contract_last(mixed_low, output_turned)
     resid_low = resid.astype(jnp.bfloat16)
-    group_in = lax.all_gather(resid_low, "col", axis=0, tiled=True)
-    normed_two, hat_two, inv_two, expert_gates = router_parts(group_in, gain_two, router_cols)
-    local_experts = router_cols.shape[1]
+    group_in = gather_col(resid_low)
+    normed_two, hat_two, inv_two = norm_parts(group_in.astype(jnp.float32), gain_two)
+    normed_two_low = normed_two.astype(jnp.bfloat16)
+    gates = jax.nn.sigmoid(jnp.dot(normed_two_low, router_cols, preferred_element_type=jnp.float32))
     expert_ids = col_index * local_experts + jnp.arange(local_experts, dtype=jnp.int32)
     member = jnp.any(expert_routes[:, :, None] == expert_ids[None, None, :], axis=1)
-    member_float = member.astype(jnp.float32)
-    counts_cum = jnp.cumsum(member.astype(jnp.int32), axis=0)
-    slot_ids = jnp.arange(CAP, dtype=jnp.int32)
-
-    def count_below(cum_column):
-        return jnp.sum((cum_column[None, :] <= slot_ids[:, None]).astype(jnp.int32), axis=1)
-
-    slot_rows = lax.map(count_below, counts_cum.T)
-    live_slot = slot_rows < group_size
-    live_float = live_slot.astype(jnp.float32)
-    safe_rows = jnp.minimum(slot_rows, group_size - 1)
-    target_rows = jnp.where(live_slot, slot_rows, group_size).reshape(-1)
-    token_rank = jnp.clip(counts_cum.T - 1, 0, CAP - 1)
-    rows_in, inner, active, expert_out = expert_compute(group_in, safe_rows, up_full, down_full)
-    gate_slots = jnp.take_along_axis(expert_gates.T, safe_rows, axis=1)
-    weighted = expert_out * (gate_slots * live_float)[..., None]
-    partial_value = (
-        jnp.zeros((group_size, width), jnp.float32)
-        .at[target_rows]
-        .add(weighted.reshape(-1, width), mode="drop")
-    )
-    expert_sum = lax.psum_scatter(partial_value, "col", scatter_dimension=0, tiled=True)
+    used_gates = gates * member.astype(jnp.float32)
+
+    def spread(columns):
+        return jnp.repeat(columns, hidden_local, axis=1)
+
+    inner = jnp.dot(group_in, up_full, preferred_element_type=jnp.float32)
+    active = jnp.maximum(inner, 0.0).astype(jnp.bfloat16)
+    gated_active = (active.astype(jnp.float32) * spread(used_gates)).astype(jnp.bfloat16)
+    expert_sum = scatter_col(contract_last(gated_active, down_turned))
     output_full_rows = resid + expert_sum
     block_output = output_full_rows.astype(jnp.bfloat16)
-    ratio = total_rows / token_count.astype(jnp.float32)
+    ratio = total_rows / token_count
     grad_output = ratio * (output_full_rows - teacher.astype(jnp.float32)) * valid[:, None]
     grad_output_low = grad_output.astype(jnp.bfloat16)
-    group_grad = lax.all_gather(grad_output_low, "col", axis=0, tiled=True)
-    normed_back, hat_back, inv_back = (normed_two, hat_two, inv_two)
-    rows_back, inner_back, active_back, out_back = (rows_in, inner, active, expert_out)
-    grad_slot = (
-        group_grad[safe_rows.reshape(-1)].reshape(local_experts, CAP, width).astype(jnp.float32)
-    )
-    grad_expert = (grad_slot * (gate_slots * live_float)[..., None]).astype(jnp.bfloat16)
-    gate_grad = jnp.sum(out_back * grad_slot, axis=2) * live_float
-    grad_active = jnp.einsum(
-        "ecd,egd->ecg", grad_expert, down_full, preferred_element_type=jnp.float32
-    )
-    grad_inner = jnp.where(inner_back > 0, grad_active, 0.0).astype(jnp.bfloat16)
-    down_grads = jnp.einsum(
-        "ecg,ecd->egd", active_back, grad_expert, preferred_element_type=jnp.float32
-    )
-    up_grads = jnp.einsum("ecd,ecg->edg", rows_back, grad_inner, preferred_element_type=jnp.float32)
-    slot_back = jnp.einsum("ecg,edg->ecd", grad_inner, up_full, preferred_element_type=jnp.float32)
-    grad_rows = (
-        jnp.zeros((group_size, width), jnp.float32)
-        .at[target_rows]
-        .add(slot_back.reshape(-1, width), mode="drop")
-    )
-    slot_logit = gate_grad * gate_slots * (1.0 - gate_slots)
-    logit_grads = jnp.take_along_axis(slot_logit, token_rank, axis=1).T * member_float
-    logit_low = logit_grads.astype(jnp.bfloat16)
-    router_grad = contract_first(normed_back, logit_low)
+    group_grad = gather_col(grad_output_low)
+    grad_hidden = jnp.dot(group_grad, down_turned, preferred_element_type=jnp.float32)
+    gate_grad = jnp.sum(
+        (active.astype(jnp.float32) * grad_hidden).reshape(group_size, local_experts, hidden_local),
+        axis=2,
+    )
+    grad_inner = jnp.where(active > 0, grad_hidden * spread(used_gates), 0.0).astype(jnp.bfloat16)
+    down_grad = contract_first(group_grad, gated_active)
+    up_grad = contract_first(group_in, grad_inner)
+    slot_back = contract_last(grad_inner, up_full)
+    logit_low = (gate_grad * used_gates * (1.0 - gates)).astype(jnp.bfloat16)
+    router_grad = contract_first(normed_two_low, logit_low)
     grad_norm_two = contract_last(logit_low, router_cols)
-    second_gain_part = jnp.sum(grad_norm_two * hat_back, axis=0)
-    grad_rows = grad_rows + norm_back(grad_norm_two, gain_two, hat_back, inv_back)
-    moe_grad = lax.psum_scatter(grad_rows, "col", scatter_dimension=0, tiled=True)
-    router_sum, up_sum, down_sum = (
-        lax.psum_scatter(router_grad, "row", scatter_dimension=0, tiled=True),
-        lax.psum_scatter(up_grads, "row", scatter_dimension=1, tiled=True),
-        lax.psum_scatter(down_grads, "row", scatter_dimension=2, tiled=True),
-    )
+    second_gain_part = jnp.sum(grad_norm_two * hat_two, axis=0)
+    grad_rows = slot_back + norm_back(grad_norm_two, gain_two, hat_two, inv_two)
+    moe_grad = scatter_col(grad_rows)
+    up_sum = scatter_row(jnp.concatenate([up_grad, padded(router_grad, 128)], axis=1), ORDER_A)
+    down_sum = scatter_row(down_grad, ORDER_C)
+    router_sum = up_sum[:, hidden : hidden + local_experts]
+    up_out = jnp.transpose(
+        up_sum[:, :hidden].reshape(-1, local_experts, hidden_local), (1, 0, 2)
+    )
+    down_out = jnp.transpose(down_sum.reshape(-1, local_experts, hidden_local), (1, 2, 0))
     grad_resid = grad_output + moe_grad
     grad_branch = grad_resid.astype(jnp.bfloat16)
-    output_grad = contract_first(mixed_low, grad_branch)
+    output_grad = contract_first(grad_branch, mixed_low)
+    output_sum = scatter_all(output_grad, ORDER_B).T
     grad_mixed = (
-        contract_last(grad_branch, output_full)
+        jnp.dot(grad_branch, output_turned, preferred_element_type=jnp.float32)
         .astype(jnp.bfloat16)
         .astype(jnp.float32)
         .reshape(tok_rows, H, AEXP, DH)
@@ -368,7 +462,8 @@
     query_grad = contract_first(normed_low, grad_query_raw)
     key_grad = contract_first(normed_low, grad_key_raw)
     router_head_grad = contract_first(normed_low, grad_route)
-    value_grad = contract_first(block_input, grad_value_all)
+    value_grad_one = contract_first(block_input, grad_value_all[:, :half_heads])
+    value_grad_two = contract_first(block_input, grad_value_all[:, half_heads:])
     grad_norm_one = (
         contract_last(grad_query_raw, query_full)
         + contract_last(grad_key_raw, key_full)
@@ -378,17 +473,32 @@
     input_grad = (
         grad_resid
         + norm_back(grad_norm_one, gain_one, hat_one, inv_one)
-        + contract_last(grad_value_all, value_full)
-    )
-    first_sum, query_sum, key_sum, value_sum, router_head_sum, output_sum, second_sum = (
-        lax.psum_scatter(first_gain_part, ("row", "col"), scatter_dimension=0, tiled=True),
-        lax.psum_scatter(query_grad, ("row", "col"), scatter_dimension=0, tiled=True),
-        lax.psum_scatter(key_grad, ("row", "col"), scatter_dimension=0, tiled=True),
-        lax.psum_scatter(value_grad, ("row", "col"), scatter_dimension=0, tiled=True),
-        lax.psum_scatter(router_head_grad, ("row", "col"), scatter_dimension=0, tiled=True),
-        lax.psum_scatter(output_grad, ("row", "col"), scatter_dimension=1, tiled=True),
-        lax.psum_scatter(second_gain_part, ("row", "col"), scatter_dimension=0, tiled=True),
-    )
+        + contract_last(grad_value_all[:, :half_heads], value_one)
+        + contract_last(grad_value_all[:, half_heads:], value_two)
+    )
+    lead_grad = padded(
+        jnp.concatenate(
+            [
+                query_grad,
+                key_grad,
+                router_head_grad,
+                first_gain_part[:, None],
+                second_gain_part[:, None],
+            ],
+            axis=1,
+        ),
+        2 * H * DH + 128,
+    )
+    lead_sum = scatter_all(lead_grad, ORDER_B)
+    value_sum = jnp.concatenate(
+        [scatter_all(value_grad_one, ORDER_A), scatter_all(value_grad_two, ORDER_C)], axis=1
+    )
+    query_sum = lead_sum[:, : H * DH]
+    key_sum = lead_sum[:, H * DH : 2 * H * DH]
+    extra_at = 2 * H * DH + 2 * gated
+    router_head_sum = lead_sum[:, 2 * H * DH : extra_at]
+    first_sum = lead_sum[:, extra_at]
+    second_sum = lead_sum[:, extra_at + 1]
     return (
         block_output,
         input_grad,
@@ -400,8 +510,8 @@
         output_sum,
         second_sum,
         router_sum,
-        up_sum,
-        down_sum,
+        up_out,
+        down_out,
     )
 
 

time: 2230 us -> 761 us (0.34)
  waiting for transfers between devices: 1130 us -> 233 us
  local copies, waits for them, and re-layouts: 401 us -> 155 us
  other arithmetic: 291 us -> 66.8 us
  blocking collectives: 173 us -> 0 us
  starting transfers between devices: 8.66 us -> 153 us
  matrix products: 193 us -> 135 us
    reduce_scatter x8 -> x0, waiting for transfers between devices: 843 us -> none  [the longest x1 183 us: shards(): lax.psum_scatter(down_grads, 'row', scatter_dimension=2, tiled=True)]
    gather x7 -> x0, local copies, waits for them, and re-layouts: 351 us -> none  [the longest x2 139 us: shards(): jnp.take_along_axis(slot_logit, token_rank, axis=1).T * member_float]
    ppermute x0 -> x72, waiting for transfers between devices: none -> 233 us  [the longest x30 147 us: scatter_row(): came = lax.ppermute(leaving.astype(jnp.bfloat16), 'row', grid_pairs(dim, k))]
    scatter-add x2 -> x0, other arithmetic: 218 us -> none  [the longest x1 110 us: shards(): grad_rows = jnp.zeros((group_size, width), jnp.float32).at[target_rows].a...]
    unnamed x20 -> x0, waiting for transfers between devices: 157 us -> none
    ppermute x0 -> x72, starting transfers between devices: none -> 145 us  [the longest x30 76.4 us: scatter_row(): came = lax.ppermute(leaving.astype(jnp.bfloat16), 'row', grid_pairs(dim, k))]
    all_gather x8 -> x0, waiting for transfers between devices: 133 us -> none  [the longest x1 54.8 us: shards(): lax.all_gather(value_weight, ('row', 'col'), axis=0, tiled=True)]
    dot_general x9 -> x6, matrix products: 129 us -> 29.9 us  [the longest x1 14.5 us: shards(): jnp.dot(group_grad, down_turned, preferred_element_type=jnp.float32)]
  transfers between devices with their start and end apart: 22 -> 76, of which waited for: 13 -> 25; matrix products, arithmetic and copies ran while one was open for 15% -> 33% of each run, Pallas kernels for 0% -> 0%
where the time goes in v1:
time: 761 us; the launch traced here: 748 us
  waiting for transfers between devices  233 us (31%)
  local copies, waits for them, and re-layouts  155 us (20%)
  starting transfers between devices  153 us (20%)
  matrix products  135 us (18%)
  other arithmetic  66.8 us (9%)
    ppermute x30, waiting for transfers between devices, scatter_row(): came = lax.ppermute(leaving.astype(jnp.bfloat16), 'row', grid_pairs(dim, k))  147 us
    ppermute x30, waiting for transfers between devices, gather_row(): lax.ppermute(held, 'row', grid_pairs(dim, k))  85.9 us
    ppermute x30, starting transfers between devices, scatter_row(): came = lax.ppermute(leaving.astype(jnp.bfloat16), 'row', grid_pairs(dim, k))  76.4 us
    ppermute x30, starting transfers between devices, gather_row(): lax.ppermute(held, 'row', grid_pairs(dim, k))  65.8 us
    dot_general x9, matrix products, contract_last(): lax.dot_general(left, right, (((1,), (1,)), ((), ())), preferred_element_...  46.1 us
    dot_general x17, matrix products, contract_first(): lax.dot_general(left, right, (((0,), (0,)), ((), ())), preferred_element_...  41.9 us
    unnamed x300, local copies, waits for them, and re-layouts  36.1 us
    dynamic_update_slice x30, local copies, waits for them, and re-layouts, gather_row(): lax.dynamic_update_slice_in_dim(whole, block, (place - k) % size, dim)  19.5 us
  transfers between devices with their start and end apart: 76, of which 25 were waited for; matrix products, arithmetic and copies ran while one was open for 33% of the time, Pallas kernels for 0%

profile of v1, /device:TPU:0, one launch (start us, length us, event | category | flops | bytes accessed | tf_op | source)
XLA Modules:
  0.0 748.4 jit_solution(5920786648247049233)
XLA Ops:
  33.0 5.4 collective-permute-done.8
  42.3 6.0 collective-permute-done.13
  59.2 7.6 %collective-permute-done.14 = bf16[1,1,2,32,1280]{4,3,2,1,0:T(8,128)(2,1)S(1)} collective-permute-done((bf16[1,1,2,32,1280]{4,3,2,1,0:T(8,128)(2,1)S(1)}, bf16[1,1,2,32,1280]{4,3,2,1,0:T(8,128)(2,1)S(1)}, u32[]{:S(2)}, u32[]{:S(2)}) %collective-permute-start.14) | collective-permute-done | bytes 163872 | tf_op jit(solution)/shard_map/ppermute | solution.py:68
  68.1 6.3 collective-permute-done.15
  74.4 5.3 collective-permute-done.16
  105.3 17.0 %collective-permute-done.3 = bf16[1,2,2,32,1152]{4,3,2,1,0:T(8,128)(2,1)S(1)} collective-permute-done((bf16[1,2,2,32,1152]{4,3,2,1,0:T(8,128)(2,1)S(1)}, bf16[1,2,2,32,1152]{4,3,2,1,0:T(8,128)(2,1)S(1)}, u32[]{:S(2)}, u32[]{:S(2)}) %collective-permute-start.3) | collective-permute-done | bytes 294944 | tf_op jit(solution)/shard_map/ppermute | solution.py:68
  124.4 20.8 %collective-permute-done.34 = bf16[1,1,2,64,2048]{4,3,2,1,0:T(8,128)(2,1)S(1)} collective-permute-done((bf16[1,1,2,64,2048]{4,3,2,1,0:T(8,128)(2,1)S(1)}, bf16[1,1,2,64,2048]{4,3,2,1,0:T(8,128)(2,1)S(1)}, u32[]{:S(2)}, u32[]{:S(2)}) %collective-permute-start.34) | collective-permute-done | bytes 524320 | tf_op jit(solution)/shard_map/ppermute | solution.py:68
  145.3 11.5 %collective-permute-start.22 = (bf16[1,2,2,32,2560]{4,3,2,1,0:T(8,128)(2,1)S(1)}, bf16[1,2,2,32,2560]{4,3,2,1,0:T(8,128)(2,1)S(1)}, u32[]{:S(2)}, u32[]{:S(2)}) collective-permute-start(bf16[1,2,2,32,2560]{4,3,2,1,0:T(8,128)(2,1)S(1)} %constant_dynamic-update-slice_fusion.26), channel_id=1, source_target_pairs={{0,8},{2,10},{4,12},{6,14},{8,16},{10,18},{12,20},{14,22},{16,24},... | collective-permute-start | bytes 1966088 | tf_op jit(solution)/shard_map/ppermute | solution.py:68
  157.6 19.3 %collective-permute-start.23 = (bf16[1,2,2,32,2560]{4,3,2,1,0:T(8,128)(2,1)S(1)}, bf16[1,2,2,32,2560]{4,3,2,1,0:T(8,128)(2,1)S(1)}, u32[]{:S(2)}, u32[]{:S(2)}) collective-permute-start(bf16[1,2,2,32,2560]{4,3,2,1,0:T(8,128)(2,1)S(1)} %constant_dynamic-update-slice_fusion.26), channel_id=1, source_target_pairs={{0,16},{2,18},{4,20},{6,22},{8,24},{10,26},{12,28},{14,30},{16,0},... | collective-permute-start | bytes 1966088 | tf_op jit(solution)/shard_map/ppermute | solution.py:68
  190.6 9.0 %collective-permute-done.23 = bf16[1,2,2,32,2560]{4,3,2,1,0:T(8,128)(2,1)S(1)} collective-permute-done((bf16[1,2,2,32,2560]{4,3,2,1,0:T(8,128)(2,1)S(1)}, bf16[1,2,2,32,2560]{4,3,2,1,0:T(8,128)(2,1)S(1)}, u32[]{:S(2)}, u32[]{:S(2)}) %collective-permute-start.23) | collective-permute-done | bytes 655392 | tf_op jit(solution)/shard_map/ppermute | solution.py:68
  244.8 4.4 constant_dynamic-update-slice_fusion.20
  249.5 6.7 constant_dynamic-update-slice_fusion.19
  266.3 6.3 maximum_convert_fusion
  280.6 7.8 %fusion.126 = f32[1024,1024]{1,0:T(8,128)} fusion(bf16[1024,2048]{1,0:T(8,128)(2,1)S(1)} %bitcast.359, bf16[1024,2048]{1,0:T(8,128)(2,1)S(1)} %copy-done.43, f32[128,8,16,128]{3,2,1,0:T(8,128)S(1)} %bitcast.311), kind=kOutput, calls=%fused_computation.394 | convolution fusion | flops 4301258752 | bytes 20971520 | tf_op jit(solution)/shard_map/dot_general | solution.py:25
  298.1 5.2 constant_dynamic-update-slice_fusion.1
  308.7 13.8 %fusion.124 = f32[1024,2048]{1,0:T(8,128)} fusion(bf16[1024,1024]{1,0:T(8,128)(2,1)} %constant_dynamic-update-slice_fusion, bf16[1024,2048]{1,0:T(8,128)(2,1)} %maximum_convert_fusion, f32[128,8,16,128]{3,2,1,0:T(8,128)} %bitcast.312), kind=kOutput, calls=%fused_computation.393 | convolution fusion | flops 4301258752 | bytes 23068672 | tf_op jit(solution)/shard_map/dot_general | solution.py:31
  322.5 14.5 %fusion.3 = (bf16[1024,2048]{1,0:T(8,128)(2,1)}, f32[128,8,16,128]{3,1,2,0:T(8,128)S(1)}) fusion(bf16[1024,2048]{1,0:T(8,128)(2,1)} %maximum_convert_fusion, f32[128,8,16,128]{3,2,1,0:T(8,128)S(1)} %bitcast.315, bf16[1024,1024]{1,0:T(8,128)(2,1)} %constant_dynamic-update-slice_fusion, bf16[1024,2048]{1,0:T(8,128)(2,1)} %bitcast.358), kind=kOutput, calls=%fused_computation.8 | convolution fusion | flops 4307550208 | bytes 31457280 | tf_op jit(solution)/shard_map/dot_general | solution.py:366
  337.0 5.2 copy.188
  342.3 6.4 reduce_sum.244
  354.7 4.4 fusion.16
  363.5 4.7 fusion.135
  368.3 8.2 %fusion.15 = f32[1024,1024]{1,0:T(8,128)S(1)} fusion(bf16[1024,1024]{1,0:T(8,128)(2,1)S(1)} %copy-done.11, f32[1024,1024]{1,0:T(8,128)} %get-tuple-element.144, f32[1024]{0:T(1024)S(1)} %broadcast_multiply_fusion, f32[1024]{0:T(1024)S(1)} %broadcast_multiply_fusion.1, f32[1024]{0:T(1024)S(1)} %copy-done.104, f32[1024]{0:T(1024)S(1)} %copy-done.106, ...), kind=kOutput, calls=%fused_computation.35 | convolution fusion | flops 4304404480 | bytes 18894848 | tf_op jit(solution)/shard_map/dot_general | solution.py:25
  383.8 6.7 convert_bitcast_fusion
  391.8 4.6 fusion.10
  396.4 6.3 copy.161
  422.7 5.0 fusion.134
  464.3 4.9 fusion.34
  469.1 10.2 %concatenate.80 = f32[1024,1066]{0,1:T(8,128)} concatenate(f32[1024,512]{0,1:T(8,128)} %fusion.137, f32[1024,512]{0,1:T(8,128)S(1)} %copy-done.23, f32[1024,40]{0,1:T(8,128)S(1)} %fusion.108, f32[1024,1]{0,1:T(1,128)S(1)} %bitcast.383, f32[1024,1]{0,1:T(1,128)S(1)} %bitcast.384), dimensions={1} | concatenate | bytes 8732672 | tf_op jit(solution)/shard_map/concatenate | solution.py:480
  479.3 5.8 copy.185
  497.0 6.9 fusion.33
  506.8 13.5 %collective-permute-start.72 = (bf16[1,1,2,64,2048]{4,3,2,1,0:T(8,128)(2,1)S(1)}, bf16[1,1,2,64,2048]{4,3,2,1,0:T(8,128)(2,1)S(1)}, u32[]{:S(2)}, u32[]{:S(2)}) collective-permute-start(bf16[1,1,2,64,2048]{4,3,2,1,0:T(8,128)(2,1)S(1)} %get-tuple-element.84), channel_id=1, source_target_pairs={{0,8},{2,10},{4,12},{6,14},{8,16},{10,18},{12,20},{14,22},{16,24},... | collective-permute-start | bytes 1572872 | tf_op jit(solution)/shard_map/ppermute | solution.py:102
  526.1 9.9 %collective-permute-done.72 = bf16[1,1,2,64,2048]{4,3,2,1,0:T(8,128)(2,1)S(1)} collective-permute-done((bf16[1,1,2,64,2048]{4,3,2,1,0:T(8,128)(2,1)S(1)}, bf16[1,1,2,64,2048]{4,3,2,1,0:T(8,128)(2,1)S(1)}, u32[]{:S(2)}, u32[]{:S(2)}) %collective-permute-start.72) | collective-permute-done | bytes 524320 | tf_op jit(solution)/shard_map/ppermute | solution.py:102
  536.0 21.8 %collective-permute-done.73 = bf16[1,1,2,64,2048]{4,3,2,1,0:T(8,128)(2,1)S(1)} collective-permute-done((bf16[1,1,2,64,2048]{4,3,2,1,0:T(8,128)(2,1)S(1)}, bf16[1,1,2,64,2048]{4,3,2,1,0:T(8,128)(2,1)S(1)}, u32[]{:S(2)}, u32[]{:S(2)}) %collective-permute-start.73) | collective-permute-done | bytes 524320 | tf_op jit(solution)/shard_map/ppermute | solution.py:102
  560.1 11.7 %collective-permute-start.43 = (bf16[1,2,2,32,1152]{4,3,2,1,0:T(8,128)(2,1)S(1)}, bf16[1,2,2,32,1152]{4,3,2,1,0:T(8,128)(2,1)S(1)}, u32[]{:S(2)}, u32[]{:S(2)}) collective-permute-start(bf16[1,2,2,32,1152]{4,3,2,1,0:T(8,128)(2,1)S(1)} %get-tuple-element.87), channel_id=1, source_target_pairs={{0,8},{2,10},{4,12},{6,14},{8,16},{10,18},{12,20},{14,22},{16,24},... | collective-permute-start | bytes 884744 | tf_op jit(solution)/shard_map/ppermute | solution.py:102
  575.0 4.2 collective-permute-done.43
  580.6 10.5 %collective-permute-done.44 = bf16[1,2,2,32,1152]{4,3,2,1,0:T(8,128)(2,1)S(1)} collective-permute-done((bf16[1,2,2,32,1152]{4,3,2,1,0:T(8,128)(2,1)S(1)}, bf16[1,2,2,32,1152]{4,3,2,1,0:T(8,128)(2,1)S(1)}, u32[]{:S(2)}, u32[]{:S(2)}) %collective-permute-start.44) | collective-permute-done | bytes 294944 | tf_op jit(solution)/shard_map/ppermute | solution.py:102
  593.5 17.4 %collective-permute-done.46 = bf16[1,2,1,32,1152]{4,3,2,1,0:T(8,128)(2,1)S(1)} collective-permute-done((bf16[1,2,1,32,1152]{4,3,2,1,0:T(8,128)(2,1)S(1)}, bf16[1,2,1,32,1152]{4,3,2,1,0:T(8,128)(2,1)S(1)}, u32[]{:S(2)}, u32[]{:S(2)}) %collective-permute-start.46) | collective-permute-done | bytes 147488 | tf_op jit(solution)/shard_map/ppermute | solution.py:102
  614.1 14.0 %collective-permute-done.47 = bf16[1,1,1,32,1152]{4,3,2,1,0:T(8,128)(2,1)S(1)} collective-permute-done((bf16[1,1,1,32,1152]{4,3,2,1,0:T(8,128)(2,1)S(1)}, bf16[1,1,1,32,1152]{4,3,2,1,0:T(8,128)(2,1)S(1)}, u32[]{:S(2)}, u32[]{:S(2)}) %collective-permute-start.47) | collective-permute-done | bytes 73760 | tf_op jit(solution)/shard_map/ppermute | solution.py:102
  630.5 5.1 collective-permute-start.68
  641.8 4.1 collective-permute-done.68
  645.9 6.5 collective-permute-start.56
  652.4 4.2 collective-permute-done.69
  656.6 11.6 %collective-permute-start.58 = (bf16[1,1,2,32,1280]{4,3,2,1,0:T(8,128)(2,1)S(1)}, bf16[1,1,2,32,1280]{4,3,2,1,0:T(8,128)(2,1)}, u32[]{:S(2)}, u32[]{:S(2)}) collective-permute-start(bf16[1,1,2,32,1280]{4,3,2,1,0:T(8,128)(2,1)S(1)} %get-tuple-element.95), channel_id=1, source_target_pairs={{0,24},{2,26},{4,28},{6,30},{8,0},{10,2},{12,4},{14,6},{16,8},{18,... | collective-permute-start | bytes 491528 | tf_op jit(solution)/shard_map/ppermute | solution.py:102
  670.1 4.1 convert_add_fusion
  683.6 13.2 %collective-permute-done.61 = bf16[1,2,2,32,2560]{4,3,2,1,0:T(8,128)(2,1)S(1)} collective-permute-done((bf16[1,2,2,32,2560]{4,3,2,1,0:T(8,128)(2,1)S(1)}, bf16[1,2,2,32,2560]{4,3,2,1,0:T(8,128)(2,1)S(1)}, u32[]{:S(2)}, u32[]{:S(2)}) %collective-permute-start.61) | collective-permute-done | bytes 655392 | tf_op jit(solution)/shard_map/ppermute | solution.py:102
  696.8 26.7 %collective-permute-done.62 = bf16[1,2,2,32,2560]{4,3,2,1,0:T(8,128)(2,1)S(1)} collective-permute-done((bf16[1,2,2,32,2560]{4,3,2,1,0:T(8,128)(2,1)S(1)}, bf16[1,2,2,32,2560]{4,3,2,1,0:T(8,128)(2,1)S(1)}, u32[]{:S(2)}, u32[]{:S(2)}) %collective-permute-start.62) | collective-permute-done | bytes 655392 | tf_op jit(solution)/shard_map/ppermute | solution.py:102
  725.3 15.8 %collective-permute-done.52 = bf16[1,1,1,32,1280]{4,3,2,1,0:T(8,128)(2,1)S(1)} collective-permute-done((bf16[1,1,1,32,1280]{4,3,2,1,0:T(8,128)(2,1)S(1)}, bf16[1,1,1,32,1280]{4,3,2,1,0:T(8,128)(2,1)S(1)}, u32[]{:S(2)}, u32[]{:S(2)}) %collective-permute-start.52) | collective-permute-done | bytes 81952 | tf_op jit(solution)/shard_map/ppermute | solution.py:102
  743.0 4.3 collective-permute-done.65
  (693 shorter events, 297.6 us)
Async XLA Ops:
  3.2 84.0 %collective-permute-start.27 = (bf16[1,1,1,64,2176]{4,3,2,1,0:T(8,128)(2,1)}, bf16[1,1,1,64,2176]{4,3,2,1,0:T(8,128)(2,1)}, u32[]{:S(2)}, u32[]{:S(2)}) collective-permute-start(bf16[1,1,1,64,2176]{4,3,2,1,0:T(8,128)(2,1)} %fusion.80), channel_id=1, source_target_pairs={{0,8},{2,10},{4,12},{6,14},{8,16},{10,18},{12,20},{14,22},{16,24},... | collective-permute-start | bytes 835592 | tf_op jit(solution)/shard_map/ppermute | solution.py:68
  6.2 82.0 %collective-permute-start.28 = (bf16[1,1,1,64,2176]{4,3,2,1,0:T(8,128)(2,1)}, bf16[1,1,1,64,2176]{4,3,2,1,0:T(8,128)(2,1)}, u32[]{:S(2)}, u32[]{:S(2)}) collective-permute-start(bf16[1,1,1,64,2176]{4,3,2,1,0:T(8,128)(2,1)} %fusion.80), channel_id=1, source_target_pairs={{0,16},{2,18},{4,20},{6,22},{8,24},{10,26},{12,28},{14,30},{16,0},... | collective-permute-start | bytes 835592 | tf_op jit(solution)/shard_map/ppermute | solution.py:68
  8.8 82.8 %collective-permute-start.29 = (bf16[1,1,1,64,2176]{4,3,2,1,0:T(8,128)(2,1)}, bf16[1,1,1,64,2176]{4,3,2,1,0:T(8,128)(2,1)}, u32[]{:S(2)}, u32[]{:S(2)}) collective-permute-start(bf16[1,1,1,64,2176]{4,3,2,1,0:T(8,128)(2,1)} %fusion.80), channel_id=1, source_target_pairs={{0,24},{2,26},{4,28},{6,30},{8,0},{10,2},{12,4},{14,6},{16,8},{18,... | collective-permute-start | bytes 835592 | tf_op jit(solution)/shard_map/ppermute | solution.py:68
  38.4 44.8 %collective-permute-start.32 = (bf16[1,1,1,64,2048]{4,3,2,1,0:T(8,128)(2,1)S(1)}, bf16[1,1,1,64,2048]{4,3,2,1,0:T(8,128)(2,1)S(1)}, u32[]{:S(2)}, u32[]{:S(2)}) collective-permute-start(bf16[1,1,1,64,2048]{4,3,2,1,0:T(8,128)(2,1)S(1)} %reshape_reshape.34), channel_id=1, source_target_pairs={{0,2},{2,0},{4,6},{6,4},{8,10},{10,8},{12,14},{14,12},{16,18},{18,... | collective-permute-start | bytes 786440 | tf_op jit(solution)/shard_map/ppermute | solution.py:68
  79.7 17.8 %collective-permute-start.10 = (bf16[4,1,1,32,1280]{4,3,2,1,0:T(8,128)(2,1)S(1)}, bf16[4,1,1,32,1280]{4,3,2,1,0:T(8,128)(2,1)S(1)}, u32[]{:S(2)}, u32[]{:S(2)}) collective-permute-start(bf16[4,1,1,32,1280]{4,3,2,1,0:T(8,128)(2,1)S(1)} %constant_dynamic-update-slice_fusion.46), channel_id=1, source_target_pairs={{0,4},{2,6},{4,0},{6,2},{8,12},{10,14},{12,8},{14,10},{16,20},{18,... | collective-permute-start | bytes 983048 | tf_op jit(solution)/shard_map/ppermute | solution.py:68
  88.2 34.1 %collective-permute-start.3 = (bf16[1,2,2,32,1152]{4,3,2,1,0:T(8,128)(2,1)S(1)}, bf16[1,2,2,32,1152]{4,3,2,1,0:T(8,128)(2,1)S(1)}, u32[]{:S(2)}, u32[]{:S(2)}) collective-permute-start(bf16[1,2,2,32,1152]{4,3,2,1,0:T(8,128)(2,1)S(1)} %constant_dynamic-update-slice_fusion.56), channel_id=1, source_target_pairs={{0,16},{2,18},{4,20},{6,22},{8,24},{10,26},{12,28},{14,30},{16,0},... | collective-permute-start | bytes 884744 | tf_op jit(solution)/shard_map/ppermute | solution.py:68
  91.6 30.8 %collective-permute-start.4 = (bf16[1,2,2,32,1152]{4,3,2,1,0:T(8,128)(2,1)S(1)}, bf16[1,2,2,32,1152]{4,3,2,1,0:T(8,128)(2,1)S(1)}, u32[]{:S(2)}, u32[]{:S(2)}) collective-permute-start(bf16[1,2,2,32,1152]{4,3,2,1,0:T(8,128)(2,1)S(1)} %constant_dynamic-update-slice_fusion.56), channel_id=1, source_target_pairs={{0,24},{2,26},{4,28},{6,30},{8,0},{10,2},{12,4},{14,6},{16,8},{18,... | collective-permute-start | bytes 884744 | tf_op jit(solution)/shard_map/ppermute | solution.py:68
  97.6 82.6 %collective-permute-start.17 = (bf16[4,1,2,32,1280]{4,3,2,1,0:T(8,128)(2,1)S(1)}, bf16[4,1,2,32,1280]{4,3,2,1,0:T(8,128)(2,1)S(1)}, u32[]{:S(2)}, u32[]{:S(2)}) collective-permute-start(bf16[4,1,2,32,1280]{4,3,2,1,0:T(8,128)(2,1)S(1)} %constant_dynamic-update-slice_fusion.34), channel_id=1, source_target_pairs={{0,4},{2,6},{4,0},{6,2},{8,12},{10,14},{12,8},{14,10},{16,20},{18,... | collective-permute-start | bytes 1966088 | tf_op jit(solution)/shard_map/ppermute | solution.py:68
  99.9 23.0 %collective-permute-start.33 = (bf16[1,1,2,64,2048]{4,3,2,1,0:T(8,128)(2,1)S(1)}, bf16[1,1,2,64,2048]{4,3,2,1,0:T(8,128)(2,1)S(1)}, u32[]{:S(2)}, u32[]{:S(2)}) collective-permute-start(bf16[1,1,2,64,2048]{4,3,2,1,0:T(8,128)(2,1)S(1)} %constant_dynamic-update-slice_fusion.8), channel_id=1, source_target_pairs={{0,8},{2,10},{4,12},{6,14},{8,16},{10,18},{12,20},{14,22},{16,24},... | collective-permute-start | bytes 1572872 | tf_op jit(solution)/shard_map/ppermute | solution.py:68
  102.8 42.4 %collective-permute-start.34 = (bf16[1,1,2,64,2048]{4,3,2,1,0:T(8,128)(2,1)S(1)}, bf16[1,1,2,64,2048]{4,3,2,1,0:T(8,128)(2,1)S(1)}, u32[]{:S(2)}, u32[]{:S(2)}) collective-permute-start(bf16[1,1,2,64,2048]{4,3,2,1,0:T(8,128)(2,1)S(1)} %constant_dynamic-update-slice_fusion.8), channel_id=1, source_target_pairs={{0,16},{2,18},{4,20},{6,22},{8,24},{10,26},{12,28},{14,30},{16,0},... | collective-permute-start | bytes 1572872 | tf_op jit(solution)/shard_map/ppermute | solution.py:68
  122.3 35.3 %collective-permute-start.35 = (bf16[1,1,2,64,2048]{4,3,2,1,0:T(8,128)(2,1)S(1)}, bf16[1,1,2,64,2048]{4,3,2,1,0:T(8,128)(2,1)S(1)}, u32[]{:S(2)}, u32[]{:S(2)}) collective-permute-start(bf16[1,1,2,64,2048]{4,3,2,1,0:T(8,128)(2,1)S(1)} %constant_dynamic-update-slice_fusion.8), channel_id=1, source_target_pairs={{0,24},{2,26},{4,28},{6,30},{8,0},{10,2},{12,4},{14,6},{16,8},{18,... | collective-permute-start | bytes 1572872 | tf_op jit(solution)/shard_map/ppermute | solution.py:68
  122.4 82.2 %collective-permute-start.30 = (bf16[4,1,1,64,2176]{4,3,2,1,0:T(8,128)(2,1)S(1)}, bf16[4,1,1,64,2176]{4,3,2,1,0:T(8,128)(2,1)S(1)}, u32[]{:S(2)}, u32[]{:S(2)}) collective-permute-start(bf16[4,1,1,64,2176]{4,3,2,1,0:T(8,128)(2,1)S(1)} %constant_dynamic-update-slice_fusion.14), channel_id=1, source_target_pairs={{0,4},{2,6},{4,0},{6,2},{8,12},{10,14},{12,8},{14,10},{16,20},{18,... | collective-permute-start | bytes 3342344 | tf_op jit(solution)/shard_map/ppermute | solution.py:68
  123.0 63.6 %collective-permute-start.11 = (bf16[4,2,1,32,1280]{4,3,2,1,0:T(8,128)(2,1)S(1)}, bf16[4,2,1,32,1280]{4,3,2,1,0:T(8,128)(2,1)S(1)}, u32[]{:S(2)}, u32[]{:S(2)}) collective-permute-start(bf16[4,2,1,32,1280]{4,3,2,1,0:T(8,128)(2,1)S(1)} %constant_dynamic-update-slice_fusion.44), channel_id=1, source_target_pairs={{0,2},{2,0},{4,6},{6,4},{8,10},{10,8},{12,14},{14,12},{16,18},{18,... | collective-permute-start | bytes 1966088 | tf_op jit(solution)/shard_map/ppermute | solution.py:68
  145.3 44.2 %collective-permute-start.22 = (bf16[1,2,2,32,2560]{4,3,2,1,0:T(8,128)(2,1)S(1)}, bf16[1,2,2,32,2560]{4,3,2,1,0:T(8,128)(2,1)S(1)}, u32[]{:S(2)}, u32[]{:S(2)}) collective-permute-start(bf16[1,2,2,32,2560]{4,3,2,1,0:T(8,128)(2,1)S(1)} %constant_dynamic-update-slice_fusion.26), channel_id=1, source_target_pairs={{0,8},{2,10},{4,12},{6,14},{8,16},{10,18},{12,20},{14,22},{16,24},... | collective-permute-start | bytes 1966088 | tf_op jit(solution)/shard_map/ppermute | solution.py:68
  157.6 41.9 %collective-permute-start.23 = (bf16[1,2,2,32,2560]{4,3,2,1,0:T(8,128)(2,1)S(1)}, bf16[1,2,2,32,2560]{4,3,2,1,0:T(8,128)(2,1)S(1)}, u32[]{:S(2)}, u32[]{:S(2)}) collective-permute-start(bf16[1,2,2,32,2560]{4,3,2,1,0:T(8,128)(2,1)S(1)} %constant_dynamic-update-slice_fusion.26), channel_id=1, source_target_pairs={{0,16},{2,18},{4,20},{6,22},{8,24},{10,26},{12,28},{14,30},{16,0},... | collective-permute-start | bytes 1966088 | tf_op jit(solution)/shard_map/ppermute | solution.py:68
  180.2 20.3 %collective-permute-start.24 = (bf16[1,2,2,32,2560]{4,3,2,1,0:T(8,128)(2,1)S(1)}, bf16[1,2,2,32,2560]{4,3,2,1,0:T(8,128)(2,1)S(1)}, u32[]{:S(2)}, u32[]{:S(2)}) collective-permute-start(bf16[1,2,2,32,2560]{4,3,2,1,0:T(8,128)(2,1)S(1)} %constant_dynamic-update-slice_fusion.26), channel_id=1, source_target_pairs={{0,24},{2,26},{4,28},{6,30},{8,0},{10,2},{12,4},{14,6},{16,8},{18,... | collective-permute-start | bytes 1966088 | tf_op jit(solution)/shard_map/ppermute | solution.py:68
  186.6 19.3 %collective-permute-start.5 = (bf16[16,1,32,1152]{3,2,1,0:T(8,128)(2,1)S(1)}, bf16[16,1,32,1152]{3,2,1,0:T(8,128)(2,1)S(1)}, u32[]{:S(2)}, u32[]{:S(2)}) collective-permute-start(bf16[16,1,32,1152]{3,2,1,0:T(8,128)(2,1)S(1)} %bitcast.357), channel_id=1, source_target_pairs={{0,1},{1,0},{2,3},{3,2},{4,5},{5,4},{6,7},{7,6},{8,9},{9,8},{10,11... | collective-permute-start | bytes 3538952 | tf_op jit(solution)/shard_map/ppermute | solution.py:59
  189.5 69.4 %collective-permute-start.36 = (bf16[4,1,2,64,2048]{4,3,2,1,0:T(8,128)(2,1)}, bf16[4,1,2,64,2048]{4,3,2,1,0:T(8,128)(2,1)}, u32[]{:S(2)}, u32[]{:S(2)}) collective-permute-start(bf16[4,1,2,64,2048]{4,3,2,1,0:T(8,128)(2,1)} %constant_dynamic-update-slice_fusion.4), channel_id=1, source_target_pairs={{0,4},{2,6},{4,0},{6,2},{8,12},{10,14},{12,8},{14,10},{16,20},{18,... | collective-permute-start | bytes 6291464 | tf_op jit(solution)/shard_map/ppermute | solution.py:68
  200.5 24.4 %collective-permute-start.12 = (bf16[16,1,32,1280]{3,2,1,0:T(8,128)(2,1)}, bf16[16,1,32,1280]{3,2,1,0:T(8,128)(2,1)}, u32[]{:S(2)}, u32[]{:S(2)}) collective-permute-start(bf16[16,1,32,1280]{3,2,1,0:T(8,128)(2,1)} %bitcast.11), channel_id=1, source_target_pairs={{0,1},{1,0},{2,3},{3,2},{4,5},{5,4},{6,7},{7,6},{8,9},{9,8},{10,11... | collective-permute-start | bytes 3932168 | tf_op jit(solution)/shard_map/ppermute | solution.py:59
  204.6 40.2 %collective-permute-start.25 = (bf16[16,1,32,2560]{3,2,1,0:T(8,128)(2,1)}, bf16[16,1,32,2560]{3,2,1,0:T(8,128)(2,1)}, u32[]{:S(2)}, u32[]{:S(2)}) collective-permute-start(bf16[16,1,32,2560]{3,2,1,0:T(8,128)(2,1)} %bitcast.37), channel_id=1, source_target_pairs={{0,1},{1,0},{2,3},{3,2},{4,5},{5,4},{6,7},{7,6},{8,9},{9,8},{10,11... | collective-permute-start | bytes 7864328 | tf_op jit(solution)/shard_map/ppermute | solution.py:59
  205.9 55.6 %collective-permute-start.31 = (bf16[4,2,1,64,2176]{4,3,2,1,0:T(8,128)(2,1)}, bf16[4,2,1,64,2176]{4,3,2,1,0:T(8,128)(2,1)}, u32[]{:S(2)}, u32[]{:S(2)}) collective-permute-start(bf16[4,2,1,64,2176]{4,3,2,1,0:T(8,128)(2,1)} %constant_dynamic-update-slice_fusion.12), channel_id=1, source_target_pairs={{0,2},{2,0},{4,6},{6,4},{8,10},{10,8},{12,14},{14,12},{16,18},{18,... | collective-permute-start | bytes 6684680 | tf_op jit(solution)/shard_map/ppermute | solution.py:68
  363.1 140.8 %collective-permute-start.71 = (bf16[4,1,2,64,2048]{4,3,2,1,0:T(8,128)(2,1)}, bf16[4,1,2,64,2048]{4,3,2,1,0:T(8,128)(2,1)}, u32[]{:S(2)}, u32[]{:S(2)}) collective-permute-start(bf16[4,1,2,64,2048]{4,3,2,1,0:T(8,128)(2,1)} %dynamic-slice_convert_fusion.2), channel_id=1, source_target_pairs={{0,4},{2,6},{4,0},{6,2},{8,12},{10,14},{12,8},{14,10},{16,20},{18,... | collective-permute-start | bytes 6291464 | tf_op jit(solution)/shard_map/ppermute | solution.py:102
  382.3 141.3 %collective-permute-start.66 = (bf16[4,2,1,64,2176]{4,3,2,1,0:T(8,128)(2,1)}, bf16[4,2,1,64,2176]{4,3,2,1,0:T(8,128)(2,1)}, u32[]{:S(2)}, u32[]{:S(2)}) collective-permute-start(bf16[4,2,1,64,2176]{4,3,2,1,0:T(8,128)(2,1)} %dynamic-slice_convert_fusion.1), channel_id=1, source_target_pairs={{0,2},{2,0},{4,6},{6,4},{8,10},{10,8},{12,14},{14,12},{16,18},{18,... | collective-permute-start | bytes 6684680 | tf_op jit(solution)/shard_map/ppermute | solution.py:102
  429.5 240.6 %collective-permute-start.60 = (bf16[16,1,32,2560]{3,2,1,0:T(8,128)(2,1)}, bf16[16,1,32,2560]{3,2,1,0:T(8,128)(2,1)}, u32[]{:S(2)}, u32[]{:S(2)}) collective-permute-start(bf16[16,1,32,2560]{3,2,1,0:T(8,128)(2,1)} %dynamic-slice_convert_fusion), channel_id=1, source_target_pairs={{0,1},{1,0},{2,3},{3,2},{4,5},{5,4},{6,7},{7,6},{8,9},{9,8},{10,11... | collective-permute-start | bytes 7864328 | tf_op jit(solution)/shard_map/ppermute | solution.py:59
  489.1 69.2 %collective-permute-start.42 = (bf16[16,1,32,1152]{3,2,1,0:T(8,128)(2,1)}, bf16[16,1,32,1152]{3,2,1,0:T(8,128)(2,1)}, u32[]{:S(2)}, u32[]{:S(2)}) collective-permute-start(bf16[16,1,32,1152]{3,2,1,0:T(8,128)(2,1)} %dynamic-slice_convert_fusion.5), channel_id=1, source_target_pairs={{0,1},{1,0},{2,3},{3,2},{4,5},{5,4},{6,7},{7,6},{8,9},{9,8},{10,11... | collective-permute-start | bytes 3538952 | tf_op jit(solution)/shard_map/ppermute | solution.py:59
  506.8 29.2 %collective-permute-start.72 = (bf16[1,1,2,64,2048]{4,3,2,1,0:T(8,128)(2,1)S(1)}, bf16[1,1,2,64,2048]{4,3,2,1,0:T(8,128)(2,1)S(1)}, u32[]{:S(2)}, u32[]{:S(2)}) collective-permute-start(bf16[1,1,2,64,2048]{4,3,2,1,0:T(8,128)(2,1)S(1)} %get-tuple-element.84), channel_id=1, source_target_pairs={{0,8},{2,10},{4,12},{6,14},{8,16},{10,18},{12,20},{14,22},{16,24},... | collective-permute-start | bytes 1572872 | tf_op jit(solution)/shard_map/ppermute | solution.py:102
  520.3 37.5 %collective-permute-start.73 = (bf16[1,1,2,64,2048]{4,3,2,1,0:T(8,128)(2,1)S(1)}, bf16[1,1,2,64,2048]{4,3,2,1,0:T(8,128)(2,1)S(1)}, u32[]{:S(2)}, u32[]{:S(2)}) collective-permute-start(bf16[1,1,2,64,2048]{4,3,2,1,0:T(8,128)(2,1)S(1)} %get-tuple-element.86), channel_id=1, source_target_pairs={{0,16},{2,18},{4,20},{6,22},{8,24},{10,26},{12,28},{14,30},{16,0},... | collective-permute-start | bytes 1572872 | tf_op jit(solution)/shard_map/ppermute | solution.py:102
  523.6 34.1 %collective-permute-start.74 = (bf16[1,1,2,64,2048]{4,3,2,1,0:T(8,128)(2,1)S(1)}, bf16[1,1,2,64,2048]{4,3,2,1,0:T(8,128)(2,1)S(1)}, u32[]{:S(2)}, u32[]{:S(2)}) collective-permute-start(bf16[1,1,2,64,2048]{4,3,2,1,0:T(8,128)(2,1)S(1)} %get-tuple-element.85), channel_id=1, source_target_pairs={{0,24},{2,26},{4,28},{6,30},{8,0},{10,2},{12,4},{14,6},{16,8},{18,... | collective-permute-start | bytes 1572872 | tf_op jit(solution)/shard_map/ppermute | solution.py:102
  536.0 35.8 %collective-permute-start.48 = (bf16[16,1,32,1280]{3,2,1,0:T(8,128)(2,1)S(1)}, bf16[16,1,32,1280]{3,2,1,0:T(8,128)(2,1)S(1)}, u32[]{:S(2)}, u32[]{:S(2)}) collective-permute-start(bf16[16,1,32,1280]{3,2,1,0:T(8,128)(2,1)S(1)} %copy-done.68), channel_id=1, source_target_pairs={{0,1},{1,0},{2,3},{3,2},{4,5},{5,4},{6,7},{7,6},{8,9},{9,8},{10,11... | collective-permute-start | bytes 3932168 | tf_op jit(solution)/shard_map/ppermute | solution.py:59
  557.8 72.4 %collective-permute-start.67 = (bf16[4,1,1,64,2176]{4,3,2,1,0:T(8,128)(2,1)S(1)}, bf16[4,1,1,64,2176]{4,3,2,1,0:T(8,128)(2,1)S(1)}, u32[]{:S(2)}, u32[]{:S(2)}) collective-permute-start(bf16[4,1,1,64,2176]{4,3,2,1,0:T(8,128)(2,1)S(1)} %dynamic-slice_convert_fusion.6), channel_id=1, source_target_pairs={{0,4},{2,6},{4,0},{6,2},{8,12},{10,14},{12,8},{14,10},{16,20},{18,... | collective-permute-start | bytes 3342344 | tf_op jit(solution)/shard_map/ppermute | solution.py:102
  560.1 19.1 %collective-permute-start.43 = (bf16[1,2,2,32,1152]{4,3,2,1,0:T(8,128)(2,1)S(1)}, bf16[1,2,2,32,1152]{4,3,2,1,0:T(8,128)(2,1)S(1)}, u32[]{:S(2)}, u32[]{:S(2)}) collective-permute-start(bf16[1,2,2,32,1152]{4,3,2,1,0:T(8,128)(2,1)S(1)} %get-tuple-element.87), channel_id=1, source_target_pairs={{0,8},{2,10},{4,12},{6,14},{8,16},{10,18},{12,20},{14,22},{16,24},... | collective-permute-start | bytes 884744 | tf_op jit(solution)/shard_map/ppermute | solution.py:102
  571.8 19.3 %collective-permute-start.44 = (bf16[1,2,2,32,1152]{4,3,2,1,0:T(8,128)(2,1)S(1)}, bf16[1,2,2,32,1152]{4,3,2,1,0:T(8,128)(2,1)S(1)}, u32[]{:S(2)}, u32[]{:S(2)}) collective-permute-start(bf16[1,2,2,32,1152]{4,3,2,1,0:T(8,128)(2,1)S(1)} %get-tuple-element.89), channel_id=1, source_target_pairs={{0,16},{2,18},{4,20},{6,22},{8,24},{10,26},{12,28},{14,30},{16,0},... | collective-permute-start | bytes 884744 | tf_op jit(solution)/shard_map/ppermute | solution.py:102
  572.1 20.4 %collective-permute-start.45 = (bf16[1,2,2,32,1152]{4,3,2,1,0:T(8,128)(2,1)S(1)}, bf16[1,2,2,32,1152]{4,3,2,1,0:T(8,128)(2,1)S(1)}, u32[]{:S(2)}, u32[]{:S(2)}) collective-permute-start(bf16[1,2,2,32,1152]{4,3,2,1,0:T(8,128)(2,1)S(1)} %get-tuple-element.88), channel_id=1, source_target_pairs={{0,24},{2,26},{4,28},{6,30},{8,0},{10,2},{12,4},{14,6},{16,8},{18,... | collective-permute-start | bytes 884744 | tf_op jit(solution)/shard_map/ppermute | solution.py:102
  579.2 33.5 %collective-permute-start.75 = (bf16[1,1,1,64,2048]{4,3,2,1,0:T(8,128)(2,1)S(1)}, bf16[1,1,1,64,2048]{4,3,2,1,0:T(8,128)(2,1)S(1)}, u32[]{:S(2)}, u32[]{:S(2)}) collective-permute-start(bf16[1,1,1,64,2048]{4,3,2,1,0:T(8,128)(2,1)S(1)} %dynamic-slice_convert_fusion.25), channel_id=1, source_target_pairs={{0,2},{2,0},{4,6},{6,4},{8,10},{10,8},{12,14},{14,12},{16,18},{18,... | collective-permute-start | bytes 786440 | tf_op jit(solution)/shard_map/ppermute | solution.py:102
  591.1 47.8 %collective-permute-start.49 = (bf16[4,2,1,32,1280]{4,3,2,1,0:T(8,128)(2,1)S(1)}, bf16[4,2,1,32,1280]{4,3,2,1,0:T(8,128)(2,1)S(1)}, u32[]{:S(2)}, u32[]{:S(2)}) collective-permute-start(bf16[4,2,1,32,1280]{4,3,2,1,0:T(8,128)(2,1)S(1)} %dynamic-slice_convert_fusion.13), channel_id=1, source_target_pairs={{0,2},{2,0},{4,6},{6,4},{8,10},{10,8},{12,14},{14,12},{16,18},{18,... | collective-permute-start | bytes 1966088 | tf_op jit(solution)/shard_map/ppermute | solution.py:102
  592.8 18.1 %collective-permute-start.46 = (bf16[1,2,1,32,1152]{4,3,2,1,0:T(8,128)(2,1)S(1)}, bf16[1,2,1,32,1152]{4,3,2,1,0:T(8,128)(2,1)S(1)}, u32[]{:S(2)}, u32[]{:S(2)}) collective-permute-start(bf16[1,2,1,32,1152]{4,3,2,1,0:T(8,128)(2,1)S(1)} %dynamic-slice_convert_fusion.30), channel_id=1, source_target_pairs={{0,2},{2,0},{4,6},{6,4},{8,10},{10,8},{12,14},{14,12},{16,18},{18,... | collective-permute-start | bytes 442376 | tf_op jit(solution)/shard_map/ppermute | solution.py:102
  610.8 28.5 %collective-permute-start.55 = (bf16[4,1,2,32,1280]{4,3,2,1,0:T(8,128)(2,1)S(1)}, bf16[4,1,2,32,1280]{4,3,2,1,0:T(8,128)(2,1)S(1)}, u32[]{:S(2)}, u32[]{:S(2)}) collective-permute-start(bf16[4,1,2,32,1280]{4,3,2,1,0:T(8,128)(2,1)S(1)} %dynamic-slice_convert_fusion.12), channel_id=1, source_target_pairs={{0,4},{2,6},{4,0},{6,2},{8,12},{10,14},{12,8},{14,10},{16,20},{18,... | collective-permute-start | bytes 1966088 | tf_op jit(solution)/shard_map/ppermute | solution.py:102
  635.6 21.0 %collective-permute-start.69 = (bf16[1,1,1,64,2176]{4,3,2,1,0:T(8,128)(2,1)S(1)}, bf16[1,1,1,64,2176]{4,3,2,1,0:T(8,128)(2,1)S(1)}, u32[]{:S(2)}, u32[]{:S(2)}) collective-permute-start(bf16[1,1,1,64,2176]{4,3,2,1,0:T(8,128)(2,1)S(1)} %get-tuple-element.92), channel_id=1, source_target_pairs={{0,16},{2,18},{4,20},{6,22},{8,24},{10,26},{12,28},{14,30},{16,0},... | collective-permute-start | bytes 835592 | tf_op jit(solution)/shard_map/ppermute | solution.py:102
  639.4 42.9 %collective-permute-start.50 = (bf16[4,1,1,32,1280]{4,3,2,1,0:T(8,128)(2,1)S(1)}, bf16[4,1,1,32,1280]{4,3,2,1,0:T(8,128)(2,1)S(1)}, u32[]{:S(2)}, u32[]{:S(2)}) collective-permute-start(bf16[4,1,1,32,1280]{4,3,2,1,0:T(8,128)(2,1)S(1)} %dynamic-slice_convert_fusion.18), channel_id=1, source_target_pairs={{0,4},{2,6},{4,0},{6,2},{8,12},{10,14},{12,8},{14,10},{16,20},{18,... | collective-permute-start | bytes 983048 | tf_op jit(solution)/shard_map/ppermute | solution.py:102
  645.9 28.4 %collective-permute-start.56 = (bf16[1,1,2,32,1280]{4,3,2,1,0:T(8,128)(2,1)}, bf16[1,1,2,32,1280]{4,3,2,1,0:T(8,128)(2,1)}, u32[]{:S(2)}, u32[]{:S(2)}) collective-permute-start(bf16[1,1,2,32,1280]{4,3,2,1,0:T(8,128)(2,1)} %get-tuple-element.94), channel_id=1, source_target_pairs={{0,8},{2,10},{4,12},{6,14},{8,16},{10,18},{12,20},{14,22},{16,24},... | collective-permute-start | bytes 491528 | tf_op jit(solution)/shard_map/ppermute | solution.py:102
  656.6 17.7 %collective-permute-start.57 = (bf16[1,1,2,32,1280]{4,3,2,1,0:T(8,128)(2,1)}, bf16[1,1,2,32,1280]{4,3,2,1,0:T(8,128)(2,1)}, u32[]{:S(2)}, u32[]{:S(2)}) collective-permute-start(bf16[1,1,2,32,1280]{4,3,2,1,0:T(8,128)(2,1)} %get-tuple-element.96), channel_id=1, source_target_pairs={{0,16},{2,18},{4,20},{6,22},{8,24},{10,26},{12,28},{14,30},{16,0},... | collective-permute-start | bytes 491528 | tf_op jit(solution)/shard_map/ppermute | solution.py:102
  656.6 17.7 %collective-permute-start.58 = (bf16[1,1,2,32,1280]{4,3,2,1,0:T(8,128)(2,1)S(1)}, bf16[1,1,2,32,1280]{4,3,2,1,0:T(8,128)(2,1)}, u32[]{:S(2)}, u32[]{:S(2)}) collective-permute-start(bf16[1,1,2,32,1280]{4,3,2,1,0:T(8,128)(2,1)S(1)} %get-tuple-element.95), channel_id=1, source_target_pairs={{0,24},{2,26},{4,28},{6,30},{8,0},{10,2},{12,4},{14,6},{16,8},{18,... | collective-permute-start | bytes 491528 | tf_op jit(solution)/shard_map/ppermute | solution.py:102
  677.2 19.6 %collective-permute-start.61 = (bf16[1,2,2,32,2560]{4,3,2,1,0:T(8,128)(2,1)S(1)}, bf16[1,2,2,32,2560]{4,3,2,1,0:T(8,128)(2,1)S(1)}, u32[]{:S(2)}, u32[]{:S(2)}) collective-permute-start(bf16[1,2,2,32,2560]{4,3,2,1,0:T(8,128)(2,1)S(1)} %get-tuple-element.81), channel_id=1, source_target_pairs={{0,8},{2,10},{4,12},{6,14},{8,16},{10,18},{12,20},{14,22},{16,24},... | collective-permute-start | bytes 1966088 | tf_op jit(solution)/shard_map/ppermute | solution.py:102
  678.4 45.1 %collective-permute-start.62 = (bf16[1,2,2,32,2560]{4,3,2,1,0:T(8,128)(2,1)S(1)}, bf16[1,2,2,32,2560]{4,3,2,1,0:T(8,128)(2,1)S(1)}, u32[]{:S(2)}, u32[]{:S(2)}) collective-permute-start(bf16[1,2,2,32,2560]{4,3,2,1,0:T(8,128)(2,1)S(1)} %get-tuple-element.83), channel_id=1, source_target_pairs={{0,16},{2,18},{4,20},{6,22},{8,24},{10,26},{12,28},{14,30},{16,0},... | collective-permute-start | bytes 1966088 | tf_op jit(solution)/shard_map/ppermute | solution.py:102
  680.0 43.5 %collective-permute-start.63 = (bf16[1,2,2,32,2560]{4,3,2,1,0:T(8,128)(2,1)S(1)}, bf16[1,2,2,32,2560]{4,3,2,1,0:T(8,128)(2,1)S(1)}, u32[]{:S(2)}, u32[]{:S(2)}) collective-permute-start(bf16[1,2,2,32,2560]{4,3,2,1,0:T(8,128)(2,1)S(1)} %get-tuple-element.82), channel_id=1, source_target_pairs={{0,24},{2,26},{4,28},{6,30},{8,0},{10,2},{12,4},{14,6},{16,8},{18,... | collective-permute-start | bytes 1966088 | tf_op jit(solution)/shard_map/ppermute | solution.py:102
  682.4 42.9 %collective-permute-start.51 = (bf16[1,1,1,32,1280]{4,3,2,1,0:T(8,128)(2,1)S(1)}, bf16[1,1,1,32,1280]{4,3,2,1,0:T(8,128)(2,1)S(1)}, u32[]{:S(2)}, u32[]{:S(2)}) collective-permute-start(bf16[1,1,1,32,1280]{4,3,2,1,0:T(8,128)(2,1)S(1)} %get-tuple-element.107), channel_id=1, source_target_pairs={{0,8},{2,10},{4,12},{6,14},{8,16},{10,18},{12,20},{14,22},{16,24},... | collective-permute-start | bytes 245768 | tf_op jit(solution)/shard_map/ppermute | solution.py:102
  682.5 58.6 %collective-permute-start.52 = (bf16[1,1,1,32,1280]{4,3,2,1,0:T(8,128)(2,1)S(1)}, bf16[1,1,1,32,1280]{4,3,2,1,0:T(8,128)(2,1)S(1)}, u32[]{:S(2)}, u32[]{:S(2)}) collective-permute-start(bf16[1,1,1,32,1280]{4,3,2,1,0:T(8,128)(2,1)S(1)} %get-tuple-element.109), channel_id=1, source_target_pairs={{0,16},{2,18},{4,20},{6,22},{8,24},{10,26},{12,28},{14,30},{16,0},... | collective-permute-start | bytes 245768 | tf_op jit(solution)/shard_map/ppermute | solution.py:102
  696.8 44.3 %collective-permute-start.53 = (bf16[1,1,1,32,1280]{4,3,2,1,0:T(8,128)(2,1)S(1)}, bf16[1,1,1,32,1280]{4,3,2,1,0:T(8,128)(2,1)S(1)}, u32[]{:S(2)}, u32[]{:S(2)}) collective-permute-start(bf16[1,1,1,32,1280]{4,3,2,1,0:T(8,128)(2,1)S(1)} %get-tuple-element.108), channel_id=1, source_target_pairs={{0,24},{2,26},{4,28},{6,30},{8,0},{10,2},{12,4},{14,6},{16,8},{18,... | collective-permute-start | bytes 245768 | tf_op jit(solution)/shard_map/ppermute | solution.py:102
  (173 other events, 1385.5 us)

commit v2 on v1

--- a/solution.py
+++ b/solution.py
@@ -1,8 +1,11 @@
+import functools
 import math
 
 import jax
 import jax.numpy as jnp
 from jax import lax
+from jax.experimental import pallas as pl
+from jax.experimental.pallas import tpu as pltpu
 from jax.sharding import PartitionSpec as P
 
 H = 4
@@ -34,87 +37,368 @@
 
 
 GRID = (4, 2, 2)
-ORDER_A, ORDER_B, ORDER_C = ((0, 1, 2), (1, 2, 0), (2, 0, 1))
+MESH = pl.DeviceIdType.MESH
+GATHER_PLAN = (
+    (
+        (3, 0, 1152, (2, 0, 1)),
+        (4, 0, 768, (2, 1, 0)),
+        (1, 0, 1280, (0, 1, 2)),
+        (2, 0, 768, (0, 2, 1)),
+        (3, 1152, 1024, (0, 1, 2)),
+        (1, 1280, 1280, (0, 2, 1)),
+        (2, 768, 1792, (0, 1, 2)),
+        (0, 0, 1152, (0, 2, 1)),
+        (4, 768, 1280, (0, 1, 2)),
+    ),
+    (
+        (0, 0),
+        (1, 0),
+        (2, 0),
+        (3, 0),
+        (4, 0),
+        (5, 0),
+        (6, 0),
+        (7, 0),
+        (8, 0),
+        (0, 1),
+        (1, 1),
+        (2, 1),
+        (3, 1),
+        (1, 2),
+        (3, 2),
+        (2, 2),
+        (4, 1),
+        (3, 3),
+        (5, 1),
+        (2, 3),
+        (4, 2),
+        (6, 1),
+        (5, 2),
+        (7, 1),
+        (6, 2),
+        (8, 1),
+        (5, 3),
+        (7, 2),
+        (8, 2),
+        (0, 2),
+        (6, 3),
+        (7, 3),
+    ),
+)
+SCATTER_PLAN = (
+    (
+        (2, 0, 1664, (1, 2, 0)),
+        (2, 1664, 896, (2, 0, 1)),
+        (5, 0, 1152, (2, 0, 1)),
+        (1, 0, 896, (2, 1, 0)),
+        (4, 0, 128, (2, 0, 1)),
+        (1, 896, 1664, (1, 2, 0)),
+        (5, 1152, 896, (1, 2, 0)),
+        (3, 0, 1408, (1, 2, 0)),
+        (0, 0, 1152, (1, 2, 0)),
+        (3, 1408, 640, (0, 1, 2)),
+    ),
+    (
+        (2, 0),
+        (4, 0),
+        (6, 0),
+        (7, 0),
+        (9, 0),
+        (0, 0),
+        (1, 0),
+        (3, 0),
+        (5, 0),
+        (8, 0),
+        (6, 1),
+        (2, 1),
+        (4, 1),
+        (9, 1),
+        (1, 1),
+        (3, 1),
+        (7, 1),
+        (2, 2),
+        (4, 2),
+        (6, 2),
+        (1, 2),
+        (0, 1),
+        (7, 2),
+        (0, 2),
+        (5, 1),
+        (5, 2),
+        (8, 1),
+        (9, 2),
+        (3, 2),
+        (8, 2),
+    ),
+)
 
 
 def by_grid():
     return lax.axis_size("row") == math.prod(GRID) and lax.axis_size("col") == 2
 
 
-def grid_place(dim):
+def places():
     row = lax.axis_index("row")
-    return (row // 4, (row // 2) % 2, row % 2)[dim]
-
-
-def grid_pairs(dim, steps):
-    pairs = []
-    for row in range(math.prod(GRID)):
-        place = [row // 4, (row // 2) % 2, row % 2]
-        place[dim] = (place[dim] + steps) % GRID[dim]
-        pairs.append((row, (place[0] * 2 + place[1]) * 2 + place[2]))
-    return pairs
+    return (row // 4, (row // 2) % 2, row % 2)
+
+
+def row_of(place):
+    return (place[0] * 2 + place[1]) * 2 + place[2]
+
+
+def moved(place, dim, steps):
+    there = list(place)
+    there[dim] = lax.rem(place[dim] + steps, GRID[dim])
+    return row_of(there)
+
+
+def greet(place, core):
+    barrier = pltpu.get_barrier_semaphore()
+    partners = [(moved(place, dim, k), core) for dim in range(3) for k in range(1, GRID[dim])]
+    partners.append((row_of(place), 1 - core))
+    for row, col in partners:
+        pl.semaphore_signal(barrier, inc=1, device_id={"row": row, "col": col}, device_id_type=MESH)
+    pl.semaphore_wait(barrier, len(partners))
+
+
+def push(source, target, send, recv, row, core):
+    copy = pltpu.make_async_remote_copy(
+        source, target, send, recv, device_id={"row": row, "col": core}, device_id_type=MESH
+    )
+    copy.start()
+    return copy
+
+
+def gather_kernel(chunks, events, shared, *refs):
+    count = len(shared)
+    ins, outs = (refs[:count], refs[count : 2 * count])
+    send, recv, local = refs[2 * count :]
+    place, core = (places(), lax.axis_index("col"))
+    greet(place, core)
+    owns = []
+    for n in range(count):
+        at = tuple(place) + ((core,) if shared[n] else ())
+        owns.append(pltpu.make_async_copy(ins[n], outs[n].at[at], local.at[n]))
+        owns[-1].start()
+    sent, flying = ([], {})
+    waited = False
+    for i, phase in events:
+        which, start, wide, order = chunks[i]
+        if phase == 1 and not waited:
+            for copy in owns:
+                copy.wait()
+            waited = True
+        for copy in flying.pop(i, []):
+            copy.wait_recv()
+        held = order[:phase]
+        at = [slice(None) if dim in held else place[dim] for dim in range(3)]
+        at += [core] if shared[which] else []
+        block = outs[which].at[tuple(at) + (slice(None), pl.ds(start, wide))]
+        if phase == 3:
+            flying[i] = [push(block, block, send.at[i, 5], recv.at[i, 5], row_of(place), 1 - core)]
+        else:
+            dim = order[phase]
+            source = ins[which].at[:, pl.ds(start, wide)] if phase == 0 else block
+            slot = (0, 3, 4)[dim]
+            flying[i] = [
+                push(
+                    source,
+                    block,
+                    send.at[i, slot + k - 1],
+                    recv.at[i, slot + k - 1],
+                    moved(place, dim, k),
+                    core,
+                )
+                for k in range(1, GRID[dim])
+            ]
+        sent += flying[i]
+    for copies in flying.values():
+        for copy in copies:
+            copy.wait_recv()
+    for copy in sent:
+        copy.wait_send()
+
+
+def gather_parts(parts, shared, plan, collective_id):
+    if not by_grid():
+        return [
+            lax.all_gather(part, ("row", "col") if both else "row", axis=0, tiled=True)
+            for part, both in zip(parts, shared)
+        ]
+    chunks, events = plan
+    count = len(parts)
+    outs = pl.pallas_call(
+        functools.partial(gather_kernel, chunks, events, shared),
+        out_shape=[
+            jax.ShapeDtypeStruct(GRID + ((2,) if both else ()) + part.shape, part.dtype)
+            for part, both in zip(parts, shared)
+        ],
+        in_specs=[pl.BlockSpec(memory_space=pltpu.VMEM)] * count,
+        out_specs=[pl.BlockSpec(memory_space=pl.ANY)] * count,
+        scratch_shapes=[
+            pltpu.SemaphoreType.DMA((len(chunks), 6)),
+            pltpu.SemaphoreType.DMA((len(chunks), 6)),
+            pltpu.SemaphoreType.DMA((count,)),
+        ],
+        compiler_params=pltpu.CompilerParams(collective_id=collective_id, has_side_effects=True),
+    )(*parts)
+    return [out.reshape(-1, part.shape[1]) for out, part in zip(outs, parts)]
+
+
+def add_blocks(target, terms, lead, rows):
+    steps = rows // 16
+
+    def body(step, carry):
+        block, part = (step // steps, (step % steps) * 16)
+        at = []
+        for size in lead[::-1]:
+            at.insert(0, block % size)
+            block = block // size
+        at = tuple(at) + (pl.ds(pl.multiple_of(part, 16), 16),)
+        total = terms[0][at].astype(jnp.float32)
+        for term in terms[1:]:
+            total = total + term[at].astype(jnp.float32)
+        target[at] = total.astype(target.dtype)
+        return carry
+
+    lax.fori_loop(0, math.prod(lead) * steps, body, 0)
+
+
+def scatter_kernel(chunks, events, shared, *refs):
+    count = len(shared)
+    ins, outs = (refs[:count], refs[count : 2 * count])
+    send, recv, local = refs[2 * count : 2 * count + 3]
+    slots = list(refs[2 * count + 3 :])
+    place, core = (places(), lax.axis_index("col"))
+    held = {}
+    for i in range(len(chunks)):
+        held[i] = [slots.pop(0) for _ in range(5 if shared[chunks[i][0]] else 4)]
+    greet(place, core)
+    sent, flying, owns = ([], {}, {})
+
+    def lead_of(order, phase):
+        return [GRID[dim] for dim in range(3) if dim not in order[: phase + 1]]
+
+    for i in dict.fromkeys(i for i, _ in events):
+        which, start, wide, order = chunks[i]
+        cols = pl.ds(start, wide)
+        if shared[which]:
+            own = ins[which].at[:, :, :, core, :, cols]
+            other = ins[which].at[:, :, :, 1 - core, :, cols]
+            flying[i] = [push(other, held[i][1], send.at[i, 5], recv.at[i, 5], row_of(place), 1 - core)]
+            sent += flying[i]
+        else:
+            at = [slice(None)] * 3
+            at[order[0]] = place[order[0]]
+            own = ins[which].at[tuple(at) + (slice(None), cols)]
+        owns[i] = pltpu.make_async_copy(own, held[i][0], local.at[i])
+        owns[i].start()
+
+    def source_of(i, phase):
+        which, start, wide, order = chunks[i]
+        if phase == 0:
+            return held[i][1] if shared[which] else ins[which].at[:, :, :, :, pl.ds(start, wide)]
+        return held[i][-3 + phase - 1].at[0]
+
+    def landed(i, phase):
+        which, start, wide, order = chunks[i]
+        rows = outs[which].shape[0]
+        for copy in flying.pop(i):
+            copy.wait_recv()
+        if phase < 0:
+            owns[i].wait()
+            add_blocks(held[i][1], [held[i][0], held[i][1]], list(GRID), rows)
+            return
+        dim = order[phase]
+        came = held[i][-3 + phase]
+        if phase == 0 and not shared[which]:
+            owns[i].wait()
+            own = held[i][0]
+        else:
+            left = [d for d in range(3) if d not in order[:phase]]
+            at = tuple(place[dim] if d == dim else slice(None) for d in left)
+            own = source_of(i, phase).at[at]
+        target = outs[which].at[:, pl.ds(start, wide)] if phase == 2 else came.at[0]
+        terms = [own] + [came.at[k] for k in range(GRID[dim] - 1)]
+        add_blocks(target, terms, lead_of(order, phase), rows)
+
+    for i, phase in events:
+        which, start, wide, order = chunks[i]
+        if phase > 0 or shared[which]:
+            landed(i, phase - 1)
+        dim = order[phase]
+        left = [d for d in range(3) if d not in order[:phase]]
+        slot = (0, 3, 4)[dim]
+        flying[i] = []
+        for k in range(1, GRID[dim]):
+            there = lax.rem(place[dim] + k, GRID[dim])
+            at = tuple(there if d == dim else slice(None) for d in left)
+            flying[i].append(
+                push(
+                    source_of(i, phase).at[at],
+                    held[i][-3 + phase].at[k - 1],
+                    send.at[i, slot + k - 1],
+                    recv.at[i, slot + k - 1],
+                    moved(place, dim, k),
+                    core,
+                )
+            )
+        sent += flying[i]
+    for i in list(flying):
+        landed(i, 2)
+    for copy in sent:
+        copy.wait_send()
+
+
+def scatter_parts(parts, shared, plan, collective_id):
+    if not by_grid():
+        return [
+            lax.psum_scatter(
+                part.astype(jnp.float32),
+                ("row", "col") if both else "row",
+                scatter_dimension=0,
+                tiled=True,
+            )
+            for part, both in zip(parts, shared)
+        ]
+    chunks, events = plan
+    count = len(parts)
+    views = []
+    for part, both in zip(parts, shared):
+        rows = part.shape[0] // (math.prod(GRID) * (2 if both else 1))
+        views.append(part.reshape(GRID + ((2,) if both else ()) + (rows, part.shape[1])))
+    scratch = []
+    for which, _, wide, order in chunks:
+        rows = views[which].shape[-2]
+        if shared[which]:
+            scratch += [pltpu.VMEM(GRID + (rows, wide), jnp.bfloat16)] * 2
+        else:
+            lead = tuple(GRID[dim] for dim in range(3) if dim != order[0])
+            scratch.append(pltpu.VMEM(lead + (rows, wide), jnp.bfloat16))
+        for phase in range(3):
+            lead = tuple(GRID[dim] for dim in range(3) if dim not in order[: phase + 1])
+            scratch.append(
+                pltpu.VMEM((GRID[order[phase]] - 1,) + lead + (rows, wide), jnp.bfloat16)
+            )
+    return pl.pallas_call(
+        functools.partial(scatter_kernel, chunks, events, shared),
+        out_shape=[jax.ShapeDtypeStruct(view.shape[-2:], jnp.float32) for view in views],
+        in_specs=[pl.BlockSpec(memory_space=pl.ANY)] * count,
+        out_specs=[pl.BlockSpec(memory_space=pltpu.VMEM)] * count,
+        scratch_shapes=[
+            pltpu.SemaphoreType.DMA((len(chunks), 6)),
+            pltpu.SemaphoreType.DMA((len(chunks), 6)),
+            pltpu.SemaphoreType.DMA((len(chunks),)),
+        ]
+        + scratch,
+        compiler_params=pltpu.CompilerParams(
+            collective_id=collective_id, has_side_effects=True, vmem_limit_bytes=60 * 1024 * 1024
+        ),
+    )(*views)
 
 
 def sibling(value):
     return lax.ppermute(value, "col", [(0, 1), (1, 0)])
-
-
-def gather_row(part, order):
-    if not by_grid():
-        return lax.all_gather(part, "row", axis=0, tiled=True)
-    held = part.reshape((1, 1, 1) + part.shape)
-    for dim in order:
-        size, place = (GRID[dim], grid_place(dim))
-        came = [lax.ppermute(held, "row", grid_pairs(dim, k)) for k in range(1, size)]
-        shape = list(held.shape)
-        shape[dim] = size
-        whole = lax.dynamic_update_slice_in_dim(jnp.zeros(shape, held.dtype), held, place, dim)
-        for k, block in zip(range(1, size), came):
-            whole = lax.dynamic_update_slice_in_dim(whole, block, (place - k) % size, dim)
-        held = whole
-    return held.reshape((-1,) + part.shape[1:])
-
-
-def gather_all(part, order):
-    if not by_grid():
-        return lax.all_gather(part, ("row", "col"), axis=0, tiled=True)
-    rows, wide = part.shape
-    mine = gather_row(part, order).reshape(-1, 1, rows, wide)
-    other = sibling(mine)
-    core = lax.axis_index("col")
-    whole = lax.dynamic_update_slice_in_dim(
-        jnp.zeros((mine.shape[0], 2, rows, wide), part.dtype), mine, core, 1
-    )
-    whole = lax.dynamic_update_slice_in_dim(whole, other, 1 - core, 1)
-    return whole.reshape(-1, wide)
-
-
-def scatter_row(total, order):
-    if not by_grid():
-        return lax.psum_scatter(total, "row", scatter_dimension=0, tiled=True)
-    rows = total.shape[0] // math.prod(GRID)
-    held = total.reshape(GRID + (rows, total.shape[1]))
-    for dim in order[::-1]:
-        size, place = (GRID[dim], grid_place(dim))
-        own = lax.dynamic_slice_in_dim(held, place, 1, dim).astype(jnp.float32)
-        for k in range(1, size):
-            leaving = lax.dynamic_slice_in_dim(held, (place + k) % size, 1, dim)
-            came = lax.ppermute(leaving.astype(jnp.bfloat16), "row", grid_pairs(dim, k))
-            own = own + came.astype(jnp.float32)
-        held = own
-    return held.reshape(rows, total.shape[1])
-
-
-def scatter_all(total, order):
-    if not by_grid():
-        return lax.psum_scatter(total, ("row", "col"), scatter_dimension=0, tiled=True)
-    rows = total.shape[0] // (2 * math.prod(GRID))
-    core = lax.axis_index("col")
-    split = total.reshape(-1, 2, rows, total.shape[1])
-    mine = lax.dynamic_slice_in_dim(split, core, 1, 1)
-    leaving = lax.dynamic_slice_in_dim(split, 1 - core, 1, 1).astype(jnp.bfloat16)
-    summed = mine + sibling(leaving).astype(jnp.float32)
-    return scatter_row(summed.reshape(-1, total.shape[1]), order)
 
 
 def gather_col(value):
@@ -219,7 +503,6 @@
     seq_length = min(MAXLEN, group_size)
     key_span = seq_length // tok_rows
     gated = H * AEXP
-    half_heads = gated * DH // 2
     local_experts = expert_up.shape[0]
     hidden_local = expert_up.shape[2]
     hidden = local_experts * hidden_local
@@ -236,9 +519,6 @@
             jnp.broadcast_to(digits.astype(jnp.bfloat16)[None, None], (first_gain.shape[0], 1))
         )
     lead_local = padded(jnp.concatenate(small_parts, axis=1), 2 * H * DH + 128)
-    lead_full = gather_all(lead_local, ORDER_B)
-    value_one = gather_all(value_weight[:, :half_heads], ORDER_A)
-    value_two = gather_all(value_weight[:, half_heads:], ORDER_C)
     up_local = jnp.concatenate(
         [
             jnp.transpose(expert_up, (1, 0, 2)).reshape(-1, hidden),
@@ -247,15 +527,16 @@
         axis=1,
     )
     down_local = jnp.transpose(expert_down, (2, 0, 1)).reshape(-1, hidden)
-    output_turned = gather_all(output_weight.T, ORDER_B)
-    up_wide = gather_row(up_local, ORDER_A)
-    down_turned = gather_row(down_local, ORDER_C)
+    lead_full, value_full, output_turned, up_wide, down_turned = gather_parts(
+        [lead_local, value_weight, output_weight.T, up_local, down_local],
+        [True, True, True, False, False],
+        GATHER_PLAN,
+        1,
+    )
     up_full = up_wide[:, :hidden]
     router_cols = up_wide[:, hidden : hidden + local_experts]
-    query_full = lead_full[:, : H * DH]
-    key_full = lead_full[:, H * DH : 2 * H * DH]
-    router_full = lead_full[:, 2 * H * DH : 2 * H * DH + 2 * gated]
-    extra = lead_full[:, 2 * H * DH + 2 * gated :].astype(jnp.float32)
+    extra_at = 2 * H * DH + 2 * gated
+    extra = lead_full[:, extra_at : extra_at + 4].astype(jnp.float32)
     gain_one = extra[:, 0]
     gain_two = extra[:, 1]
     stride = first_gain.shape[0] * col_count
@@ -272,15 +553,16 @@
     inputs_full = block_input.astype(jnp.float32)
     normed_one, hat_one, inv_one = norm_parts(inputs_full, gain_one)
     normed_low = normed_one.astype(jnp.bfloat16)
-    query_raw = jnp.dot(normed_low, query_full, preferred_element_type=jnp.float32)
-    key_raw = jnp.dot(normed_low, key_full, preferred_element_type=jnp.float32)
+    lead_raw = jnp.dot(normed_low, lead_full, preferred_element_type=jnp.float32)
+    query_raw = lead_raw[:, : H * DH]
+    key_raw = lead_raw[:, H * DH : 2 * H * DH]
+    route_logits = lead_raw[:, 2 * H * DH : extra_at]
     cosine, sines = rope_tables(seq_pos, DH)
     query_scale = DH ** (-0.5)
     query_rot = (rotate(query_raw.reshape(tok_rows, H, DH), cosine, sines) * query_scale).astype(
         jnp.bfloat16
     )
     key_rot = rotate(key_raw.reshape(tok_rows, H, DH), cosine, sines).astype(jnp.bfloat16)
-    route_logits = jnp.dot(normed_low, router_full, preferred_element_type=jnp.float32)
     chosen = jnp.any(
         head_routes[:, :, :, None] == jnp.arange(AEXP, dtype=jnp.int32)[None, None, None, :], axis=2
     ).astype(jnp.float32)
@@ -288,13 +570,9 @@
     output_sig = jax.nn.sigmoid(route_logits[:, gated:]).reshape(tok_rows, H, AEXP)
     value_gates = value_sig * chosen
     output_gates = output_sig * chosen
-    value_all = jnp.concatenate(
-        [
-            jnp.dot(block_input, value_one, preferred_element_type=jnp.float32),
-            jnp.dot(block_input, value_two, preferred_element_type=jnp.float32),
-        ],
-        axis=1,
-    ).reshape(tok_rows, H, AEXP, DH)
+    value_all = jnp.dot(block_input, value_full, preferred_element_type=jnp.float32).reshape(
+        tok_rows, H, AEXP, DH
+    )
     values_low = jnp.sum(value_all * value_gates[..., None], axis=2).astype(jnp.bfloat16)
     key_parts = [key_rot]
     value_parts = [values_low]
@@ -369,26 +647,18 @@
         axis=2,
     )
     grad_inner = jnp.where(active > 0, grad_hidden * spread(used_gates), 0.0).astype(jnp.bfloat16)
-    down_grad = contract_first(group_grad, gated_active)
-    up_grad = contract_first(group_in, grad_inner)
+    down_grad = contract_first(group_grad, gated_active).astype(jnp.bfloat16)
+    up_grad = contract_first(group_in, grad_inner).astype(jnp.bfloat16)
     slot_back = contract_last(grad_inner, up_full)
     logit_low = (gate_grad * used_gates * (1.0 - gates)).astype(jnp.bfloat16)
-    router_grad = contract_first(normed_two_low, logit_low)
+    router_grad = contract_first(normed_two_low, padded(logit_low, 128)).astype(jnp.bfloat16)
     grad_norm_two = contract_last(logit_low, router_cols)
     second_gain_part = jnp.sum(grad_norm_two * hat_two, axis=0)
     grad_rows = slot_back + norm_back(grad_norm_two, gain_two, hat_two, inv_two)
     moe_grad = scatter_col(grad_rows)
-    up_sum = scatter_row(jnp.concatenate([up_grad, padded(router_grad, 128)], axis=1), ORDER_A)
-    down_sum = scatter_row(down_grad, ORDER_C)
-    router_sum = up_sum[:, hidden : hidden + local_experts]
-    up_out = jnp.transpose(
-        up_sum[:, :hidden].reshape(-1, local_experts, hidden_local), (1, 0, 2)
-    )
-    down_out = jnp.transpose(down_sum.reshape(-1, local_experts, hidden_local), (1, 2, 0))
     grad_resid = grad_output + moe_grad
     grad_branch = grad_resid.astype(jnp.bfloat16)
-    output_grad = contract_first(grad_branch, mixed_low)
-    output_sum = scatter_all(output_grad, ORDER_B).T
+    output_grad = contract_first(grad_branch, mixed_low).astype(jnp.bfloat16)
     grad_mixed = (
         jnp.dot(grad_branch, output_turned, preferred_element_type=jnp.float32)
         .astype(jnp.bfloat16)
@@ -459,43 +729,35 @@
         ],
         axis=1,
     ).astype(jnp.bfloat16)
-    query_grad = contract_first(normed_low, grad_query_raw)
-    key_grad = contract_first(normed_low, grad_key_raw)
-    router_head_grad = contract_first(normed_low, grad_route)
-    value_grad_one = contract_first(block_input, grad_value_all[:, :half_heads])
-    value_grad_two = contract_first(block_input, grad_value_all[:, half_heads:])
-    grad_norm_one = (
-        contract_last(grad_query_raw, query_full)
-        + contract_last(grad_key_raw, key_full)
-        + contract_last(grad_route, router_full)
-    )
+    lead_back = padded(
+        jnp.concatenate([grad_query_raw, grad_key_raw, grad_route], axis=1), 2 * H * DH + 128
+    )
+    value_grad = contract_first(block_input, grad_value_all).astype(jnp.bfloat16)
+    grad_norm_one = contract_last(lead_back, lead_full)
     first_gain_part = jnp.sum(grad_norm_one * hat_one, axis=0)
     input_grad = (
         grad_resid
         + norm_back(grad_norm_one, gain_one, hat_one, inv_one)
-        + contract_last(grad_value_all[:, :half_heads], value_one)
-        + contract_last(grad_value_all[:, half_heads:], value_two)
-    )
-    lead_grad = padded(
-        jnp.concatenate(
-            [
-                query_grad,
-                key_grad,
-                router_head_grad,
-                first_gain_part[:, None],
-                second_gain_part[:, None],
-            ],
-            axis=1,
-        ),
-        2 * H * DH + 128,
-    )
-    lead_sum = scatter_all(lead_grad, ORDER_B)
-    value_sum = jnp.concatenate(
-        [scatter_all(value_grad_one, ORDER_A), scatter_all(value_grad_two, ORDER_C)], axis=1
-    )
+        + contract_last(grad_value_all, value_full)
+    )
+    lead_cols = jnp.arange(2 * H * DH + 128, dtype=jnp.int32)[None, :]
+    lead_grad = (
+        contract_first(normed_low, lead_back)
+        + jnp.where(lead_cols == extra_at, first_gain_part[:, None], 0.0)
+        + jnp.where(lead_cols == extra_at + 1, second_gain_part[:, None], 0.0)
+    ).astype(jnp.bfloat16)
+    lead_sum, value_sum, output_turned_sum, up_sum, router_sum, down_sum = scatter_parts(
+        [lead_grad, value_grad, output_grad, up_grad, router_grad, down_grad],
+        [True, True, True, False, False, False],
+        SCATTER_PLAN,
+        2,
+    )
+    output_sum = output_turned_sum.T
+    router_sum = router_sum[:, :local_experts]
+    up_out = jnp.transpose(up_sum.reshape(-1, local_experts, hidden_local), (1, 0, 2))
+    down_out = jnp.transpose(down_sum.reshape(-1, local_experts, hidden_local), (1, 2, 0))
     query_sum = lead_sum[:, : H * DH]
     key_sum = lead_sum[:, H * DH : 2 * H * DH]
-    extra_at = 2 * H * DH + 2 * gated
     router_head_sum = lead_sum[:, 2 * H * DH : extra_at]
     first_sum = lead_sum[:, extra_at]
     second_sum = lead_sum[:, extra_at + 1]

time: 761 us -> 549 us (0.72)
  Pallas kernels: 0 us -> 277 us
  waiting for transfers between devices: 233 us -> 1.96 us
  starting transfers between devices: 153 us -> 7.02 us
  local copies, waits for them, and re-layouts: 155 us -> 65.9 us
  other arithmetic: 66.8 us -> 57.6 us
  matrix products: 135 us -> 126 us
    pallas_call x0 -> x2, Pallas kernels: none -> 277 us  [the longest x1 148 us: gather_parts(): pl.pallas_call(functools.partial(gather_kernel, chunks, events, shared),...]
    ppermute x60 -> x0, waiting for transfers between devices: 233 us -> none  [the longest x30 147 us: scatter_row(): came = lax.ppermute(leaving.astype(jnp.bfloat16), 'row', grid_pairs(dim, k))]
    ppermute x60 -> x0, starting transfers between devices: 142 us -> none  [the longest x30 76.4 us: scatter_row(): came = lax.ppermute(leaving.astype(jnp.bfloat16), 'row', grid_pairs(dim, k))]
    dynamic_update_slice x54 -> x0, local copies, waits for them, and re-layouts: 43.4 us -> none  [the longest x30 19.5 us: gather_row(): lax.dynamic_update_slice_in_dim(whole, block, (place - k) % size, dim)]
    unnamed x300 -> x205, local copies, waits for them, and re-layouts: 36.1 us -> 20.1 us
    convert_element_type x22 -> x0, local copies, waits for them, and re-layouts: 13.1 us -> none  [the longest x18 7.68 us: scatter_row(): came = lax.ppermute(leaving.astype(jnp.bfloat16), 'row', grid_pairs(dim, k))]
    add x16 -> x1, other arithmetic: 13.8 us -> 1.67 us  [shards(): grad_resid = grad_output + moe_grad]
    concatenate x1, local copies, waits for them, and re-layouts: 10.2 us -> 0.49 us  [shards(): jnp.concatenate([grad_query_raw, grad_key_raw, grad_route], axis=1)]
  transfers between devices with their start and end apart: 76 -> 8, of which waited for: 25 -> 1; matrix products, arithmetic and copies ran while one was open for 33% -> 10% of each run, Pallas kernels for 0% -> 0%
where the time goes in v2:
time: 549 us; the launch traced here: 540 us
  Pallas kernels  277 us (50%)
  matrix products  126 us (23%)
  local copies, waits for them, and re-layouts  65.9 us (12%)
  other arithmetic  57.6 us (10%)
  starting transfers between devices  7.02 us (1%)
    pallas_call x1, Pallas kernels, gather_parts(): pl.pallas_call(functools.partial(gather_kernel, chunks, events, shared),...  148 us
    pallas_call x1, Pallas kernels, scatter_parts(): pl.pallas_call(functools.partial(scatter_kernel, chunks, events, shared),...  129 us
    dot_general x6, matrix products, contract_last(): lax.dot_general(left, right, (((1,), (1,)), ((), ())), preferred_element_...  43.4 us
    dot_general x14, matrix products, contract_first(): lax.dot_general(left, right, (((0,), (0,)), ((), ())), preferred_element_...  35.7 us
    unnamed x205, local copies, waits for them, and re-layouts  20.1 us
    dot_general x1, matrix products, shards(): jnp.dot(group_grad, down_turned, preferred_element_type=jnp.float32)  12.3 us
  transfers between devices with their start and end apart: 8, of which 1 were waited for; matrix products, arithmetic and copies ran while one was open for 10% of the time, Pallas kernels for 0%

profile of v2, /device:TPU:0, one launch (start us, length us, event | category | flops | bytes accessed | tf_op | source)
XLA Modules:
  0.0 539.8 jit_solution(15168679204004832334)
XLA Ops:
  3.0 1.6 fusion.34
  7.3 147.9 %shard_map.238 = (bf16[4,2,2,2,32,1152]{5,4,3,2,1,0:T(8,128)(2,1)}, bf16[4,2,2,2,32,2560]{5,4,3,2,1,0:T(8,128)(2,1)}, bf16[4,2,2,2,32,2560]{5,4,3,2,1,0:T(8,128)...) custom-call(bf16[32,1152]{1,0:T(8,128)(2,1)} %pad.16.refs_0_, bf16[32,2560]{1,0:T(8,128)(2,1)} %refs_1_.1, ...), custom_call_target="tpu_custom_call" | custom-call | tf_op jit(solution)/shard_map/pallas_call | solution.py:230
  157.0 3.3 fusion.96
  160.4 1.5 fusion.102
  162.4 1.6 copy.237
  166.7 2.1 collective-permute-start
  170.4 4.9 fusion.110
  176.2 1.5 copy-done.8
  177.7 1.5 collective-permute-start.1
  189.4 2.5 copy.214
  192.0 1.9 multiply_convert_fusion.1
  193.9 1.8 broadcast.475.clone
  195.6 7.2 %constant_dynamic-update-slice_fusion.3 = (bf16[1024,1024]{1,0:T(8,128)(2,1)}, bf16[512,1024]{1,0:T(8,128)(2,1)}, f32[512,1024]{1,0:T(8,128)}) fusion(bf16[1024,1024]{1,0:T(8,128)(2,1)} %broadcast.475.clone, s32[]{:T(128)S(6)} %select_n.127, bf16[512,2560]{0,1:T(8,128)(2,1)S(1)} %bitcast.270, bf16[1024,2560]{1,0:T(8,128)(2,1)} %bitcast.299, ...), kind=kOutput, calls=%fused_computation.237 | convolution fusion | flops 2685927424 | bytes 13107204 | tf_op jit(solution)/shard_map/dot_general | solution.py:28
  203.9 1.9 collective-permute-done.2
  205.9 2.3 constant_dynamic-update-slice_fusion.2
  208.2 1.9 convert_reduce_fusion
  210.1 2.3 fusion.17
  212.4 9.3 %maximum_convert_fusion = bf16[1024,2048]{1,0:T(8,128)(2,1)} fusion(bf16[1024,1024]{1,0:T(8,128)(2,1)} %constant_dynamic-update-slice_fusion.2, bf16[1024,2176]{1,0:T(8,128)(2,1)} %bitcast.287), kind=kOutput, calls=%fused_computation.7 | convolution fusion | flops 4299161600 | bytes 10485760 | tf_op jit(solution)/shard_map/dot_general | solution.py:634
  221.7 2.3 fusion.11
  225.3 2.3 broadcast_select_fusion
  227.6 1.8 copy.218
  229.4 3.9 broadcast_in_dim.66
  233.3 10.9 %fusion.99 = f32[1024,1024]{1,0:T(8,128)S(1)} fusion(bf16[1024,2048]{1,0:T(8,128)(2,1)S(1)} %bitcast.304, bf16[1024,2048]{1,0:T(8,128)(2,1)} %maximum_convert_fusion, f32[128,8,16,128]{3,2,1,0:T(8,128)S(1)} %bitcast.261), kind=kOutput, calls=%fused_computation.255 | convolution fusion | flops 4301258752 | bytes 20971520 | tf_op jit(solution)/shard_map/dot_general | solution.py:28
  254.5 4.6 constant_dynamic-update-slice_fusion.1
  262.6 8.7 %convolution_convert_fusion.3 = bf16[1024,2048]{1,0:T(8,128)(2,1)} fusion(bf16[1024,1024]{1,0:T(8,128)(2,1)S(1)} %constant_dynamic-update-slice_fusion, bf16[1024,2048]{1,0:T(8,128)(2,1)S(1)} %copy-done.94, f32[128,8,16,128]{3,2,1,0:T(8,128)S(1)} %bitcast.262), kind=kOutput, calls=%fused_computation.35 | convolution fusion | flops 4303355904 | bytes 18874368 | tf_op jit(solution)/shard_map/dot_general | solution.py:34
  271.3 12.3 %fusion.1 = (f32[128,8,16,128]{3,1,2,0:T(8,128)S(1)}, bf16[1024,2048]{1,0:T(8,128)(2,1)}) fusion(bf16[1024,2048]{1,0:T(8,128)(2,1)} %maximum_convert_fusion, f32[128,8,16,128]{3,2,1,0:T(8,128)S(1)} %bitcast.263, bf16[1024,1024]{1,0:T(8,128)(2,1)S(1)} %constant_dynamic-update-slice_fusion, bf16[1024,2048]{1,0:T(8,128)(2,1)} %bitcast.303), kind=kOutput, calls=%fused_computation.3 | convolution fusion | flops 4307550208 | bytes 31457280 | tf_op jit(solution)/shard_map/dot_general | solution.py:644
  283.6 5.3 copy.246
  288.9 6.4 %reduce_sum.244 = f32[1024,16]{1,0:T(8,128)} reduce(f32[1024,16,128]{2,1,0:T(8,128)} %bitcast.257, f32[]{:T(128)} %constant.112.clone.1), dimensions={2}, to_apply=%region_17.18 | reduce | flops 2080768 | bytes 8454148 | tf_op jit(solution)/shard_map/reduce_sum | solution.py:645
  295.3 1.8 copy.219
  298.1 3.7 fusion.16
  301.9 7.8 %fusion.15 = f32[1024,1024]{1,0:T(8,128)S(1)} fusion(bf16[1024,1024]{1,0:T(8,128)(2,1)} %constant_dynamic-update-slice_fusion.2, f32[1024,1024]{1,0:T(8,128)S(1)} %get-tuple-element.167, f32[1024]{0:T(1024)S(1)} %broadcast_multiply_fusion, f32[1024]{0:T(1024)S(1)} %broadcast_multiply_fusion.1, f32[1024]{0:T(1024)S(1)} %bitcast.286, ...), kind=kOutput, calls=%fused_computation.32 | convolution fusion | flops 4304404480 | bytes 18894848 | tf_op jit(solution)/shard_map/dot_general | solution.py:28
  312.7 8.4 %convolution_convert_fusion.4 = bf16[1024,2048]{1,0:T(8,128)(2,1)} fusion(bf16[1024,1024]{1,0:T(8,128)(2,1)} %constant_dynamic-update-slice_fusion.2, bf16[1024,2048]{1,0:T(8,128)(2,1)S(1)} %copy-done.95), kind=kOutput, calls=%fused_computation.36 | convolution fusion | flops 4297064448 | bytes 10485760 | tf_op jit(solution)/shard_map/dot_general | solution.py:34
  321.1 1.7 add_add_fusion
  324.1 4.6 fusion.10
  328.7 5.9 %copy.221 = f32[512,2560]{0,1:T(8,128)} copy(f32[512,2560]{1,0:T(8,128)} %fusion.10) | data formatting | bytes 10485760 | tf_op jit(solution)/shard_map/reshape | solution.py:666
  334.7 4.5 multiply_reduce_fusion
  356.7 4.9 convolution_convert_fusion
  362.7 1.6 copy.226
  364.3 5.0 multiply_reduce_fusion.1
  376.6 5.1 fusion.33
  381.7 4.8 convolution_convert_fusion.1
  386.5 3.8 add_convert_fusion
  390.3 129.3 %shard_map.239 = (f32[32,1152]{1,0:T(8,128)}, f32[32,2560]{1,0:T(8,128)}, f32[32,2560]{1,0:T(8,128)}, f32[64,2048]{1,0:T(8,128)}, f32[64,128]{1,0:T(8,128)}, /*index=5*/f32[64,2048]{1,0:T(8,128)}) custom-call(bf16[4,2,2,2,32,1152]{5,4,3,2,1,0:T(8,128)(2,1)} %bitcast.274, bf16[4,2,2,2,32,2560]{5,4,3,2,1,0:T(8,128)(2,1)} %bitcast.265, ...), custom_call_target="tpu_custom_call" | custom-call | tf_op jit(solution)/shard_map/pallas_call | solution.py:383
  519.7 1.6 slice_reduce_fusion
  522.6 1.5 fusion.104
  525.5 1.9 bitcast_bitcast_fusion.1
  527.4 1.9 bitcast_bitcast_fusion
  529.3 8.8 %fusion.32 = f32[512,1024]{1,0:T(8,128)} fusion(f32[512,1024]{1,0:T(8,128)S(1)} %copy-done.33, bf16[512,1024]{1,0:T(8,128)(2,1)S(1)} %copy-done.16, f32[512,1024]{1,0:T(8,128)} %get-tuple-element.176, f32[512]{0:T(512)S(1)} %broadcast_multiply_fusion.3, f32[512]{0:T(512)S(1)} %broadcast_multiply_fusion.4, f32[1024]{0:T(1024)S(1)} %bitcast.294, ...), kind=kOutput, calls=%fused_computation.55 | convolution fusion | flops 2689597440 | bytes 15216640 | tf_op jit(solution)/shard_map/dot_general | solution.py:28
  (329 shorter events, 71.3 us)
Async XLA Ops:
  0.7 5.1 copy-start.67
  3.0 154.0 %copy-start.65 = (f32[512]{0:T(512)}, f32[512]{0:T(512)S(1)}, u32[]{:S(2)}) copy-start(f32[512]{0:T(512)S(1)} %broadcast_multiply_fusion.5) | copy-start | bytes 6148
  4.6 152.4 %copy-start.14 = (bf16[512,1024]{1,0:T(8,128)(2,1)S(1)}, bf16[512,1024]{1,0:T(8,128)(2,1)}, u32[]{:S(2)}) copy-start(bf16[512,1024]{1,0:T(8,128)(2,1)} %param.15) | copy-start | bytes 3145732
  4.7 155.7 %copy-start.87 = (f32[512]{0:T(512)}, f32[512]{0:T(512)S(1)}, u32[]{:S(2)}) copy-start(f32[512]{0:T(512)S(1)} %add_rsqrt_fusion.1) | copy-start | bytes 6148
  164.6 5.4 copy-start.64
  166.7 12.8 %collective-permute-start = (bf16[512,4,128]{0,2,1:T(8,128)(2,1)S(1)}, bf16[512,4,128]{0,2,1:T(8,128)(2,1)}, u32[]{:S(2)}, u32[]{:S(2)}) collective-permute-start(bf16[512,4,128]{0,2,1:T(8,128)(2,1)S(1)} %pad_maximum_fusion.4), channel_id=1, source_target_pairs={{0,1},{2,3},{4,5},{6,7},{8,9},{10,11},{12,13},{14,15},{16,17},{18,... | collective-permute-start | bytes 1572872 | tf_op jit(solution)/shard_map/ppermute | solution.py:24
  170.0 5.4 copy-start.47
  170.1 5.3 copy-start.40
  170.2 5.2 copy-start.42
  177.7 8.4 %collective-permute-start.1 = (bf16[512,4,128]{0,2,1:T(8,128)(2,1)S(1)}, bf16[512,4,128]{0,2,1:T(8,128)(2,1)S(1)}, u32[]{:S(2)}, u32[]{:S(2)}) collective-permute-start(bf16[512,4,128]{0,2,1:T(8,128)(2,1)S(1)} %multiply_reduce_fusion.3), channel_id=1, source_target_pairs={{0,1},{2,3},{4,5},{6,7},{8,9},{10,11},{12,13},{14,15},{16,17},{18,... | collective-permute-start | bytes 1572872 | tf_op jit(solution)/shard_map/ppermute | solution.py:24
  179.5 5.3 copy-start.34
  182.4 5.4 %copy-start.4 = (f32[512,1024]{1,0:T(8,128)}, f32[512,1024]{1,0:T(8,128)S(1)}, u32[]{:S(2)}) copy-start(f32[512,1024]{1,0:T(8,128)S(1)} %get-tuple-element.159) | copy-start | bytes 6291460
  182.4 5.4 %copy-start.70 = (f32[512]{0:T(512)}, f32[512]{0:T(512)S(1)}, u32[]{:S(2)}) copy-start(f32[512]{0:T(512)S(1)} %get-tuple-element.158) | copy-start | bytes 6148
  193.9 9.0 %copy-start.23 = (bf16[512,4,5,128]{0,3,2,1:T(8,128)(2,1)}, bf16[512,4,5,128]{0,3,2,1:T(8,128)(2,1)S(1)}, u32[]{:S(2)}) copy-start(bf16[512,4,5,128]{0,3,2,1:T(8,128)(2,1)S(1)} %multiply_convert_fusion.1) | copy-start | bytes 7864324
  202.9 3.0 collective-permute-start.2
  210.1 11.6 %copy-start.49 = (f32[1024]{0:T(1024)}, f32[1024]{0:T(1024)S(1)}, u32[]{:S(2)}) copy-start(f32[1024]{0:T(1024)S(1)} %broadcast_multiply_fusion.2) | copy-start | bytes 12292
  212.4 9.3 %copy-start.60 = (f32[1024]{0:T(1024)}, f32[1024]{0:T(1024)S(1)}, u32[]{:S(2)}) copy-start(f32[1024]{0:T(1024)S(1)} %add_rsqrt_fusion) | copy-start | bytes 12292
  212.4 9.3 %copy-start.62 = (f32[1024,1]{0,1:T(1,128)S(1)}, f32[1024,1]{0,1:T(1,128)}, u32[]{:S(2)}) copy-start(f32[1024,1]{0,1:T(1,128)} %get-tuple-element.149) | copy-start | bytes 12292
  233.3 10.9 %copy-start.11 = (f32[1024,16,128]{2,1,0:T(8,128)}, f32[1024,16,128]{2,1,0:T(8,128)S(1)}, u32[]{:S(2)}) copy-start(f32[1024,16,128]{2,1,0:T(8,128)S(1)} %broadcast_in_dim.66) | copy-start | bytes 25165828
  246.6 6.7 %collective-permute-start.3 = (bf16[512,1024]{1,0:T(8,128)(2,1)}, bf16[512,1024]{1,0:T(8,128)(2,1)}, u32[]{:S(2)}, u32[]{:S(2)}) collective-permute-start(bf16[512,1024]{1,0:T(8,128)(2,1)} %dynamic-slice_convert_fusion.1), channel_id=1, source_target_pairs={{0,1},{1,0},{2,3},{3,2},{4,5},{5,4},{6,7},{7,6},{8,9},{9,8},{10,11... | collective-permute-start | bytes 3145736 | tf_op jit(solution)/shard_map/ppermute | solution.py:401
  253.2 5.8 %copy-start.58 = (f32[512]{0:T(512)}, f32[512]{0:T(512)S(1)}, u32[]{:S(2)}) copy-start(f32[512]{0:T(512)S(1)} %compare_convert_fusion) | copy-start | bytes 6148
  254.4 5.6 %copy-start.69 = (f32[512]{0:T(512)S(1)}, f32[512]{0:T(512)}, u32[]{:S(2)}) copy-start(f32[512]{0:T(512)} %copy-done.68) | copy-start | bytes 6148
  254.4 5.6 %copy-start.81 = (f32[512]{0:T(512)S(1)}, f32[512]{0:T(512)}, u32[]{:S(2)}) copy-start(f32[512]{0:T(512)} %copy-done.80) | copy-start | bytes 6148
  254.4 6.2 %copy-start.71 = (f32[512]{0:T(512)S(1)}, f32[512]{0:T(512)}, u32[]{:S(2)}) copy-start(f32[512]{0:T(512)} %copy-done.70) | copy-start | bytes 6148
  254.5 6.2 %copy-start.79 = (f32[512]{0:T(512)S(1)}, f32[512]{0:T(512)}, u32[]{:S(2)}) copy-start(f32[512]{0:T(512)} %copy-done.78) | copy-start | bytes 6148
  254.5 6.8 %copy-start.73 = (f32[512]{0:T(512)S(1)}, f32[512]{0:T(512)}, u32[]{:S(2)}) copy-start(f32[512]{0:T(512)} %copy-done.72) | copy-start | bytes 6148
  254.5 6.8 %copy-start.75 = (f32[512]{0:T(512)S(1)}, f32[512]{0:T(512)}, u32[]{:S(2)}) copy-start(f32[512]{0:T(512)} %copy-done.74) | copy-start | bytes 6148
  254.5 7.4 %copy-start.77 = (f32[512]{0:T(512)S(1)}, f32[512]{0:T(512)}, u32[]{:S(2)}) copy-start(f32[512]{0:T(512)} %copy-done.76) | copy-start | bytes 6148
  254.5 7.4 %copy-start.83 = (f32[512]{0:T(512)S(1)}, f32[512]{0:T(512)}, u32[]{:S(2)}) copy-start(f32[512]{0:T(512)} %copy-done.82) | copy-start | bytes 6148
  254.5 8.1 %copy-start.12 = (f32[1024,16,128]{2,1,0:T(8,128)S(1)}, f32[1024,16,128]{2,1,0:T(8,128)}, u32[]{:S(2)}) copy-start(f32[1024,16,128]{2,1,0:T(8,128)} %copy-done.11) | copy-start | bytes 25165828
  254.5 8.1 %copy-start.94 = (bf16[1024,2048]{1,0:T(8,128)(2,1)S(1)}, bf16[1024,2048]{1,0:T(8,128)(2,1)}, u32[]{:S(2)}) copy-start(bf16[1024,2048]{1,0:T(8,128)(2,1)} %maximum_convert_fusion) | copy-start | bytes 12582916
  259.1 3.4 collective-permute-start.4
  309.7 14.5 %slice-start = ((s8[5242880]{0:T(1024)(128)(4,1)}), s8[1048576]{0:T(1024)(128)(4,1)S(1)}, s32[]{:S(2)}) async-start(s8[5242880]{0:T(1024)(128)(4,1)} %bitcast.300), calls=%async_computation | async-start | bytes 2097152
  309.8 11.3 %collective-permute-start.5 = (bf16[512,1024]{1,0:T(8,128)(2,1)S(1)}, bf16[512,1024]{1,0:T(8,128)(2,1)S(1)}, u32[]{:S(2)}, u32[]{:S(2)}) collective-permute-start(bf16[512,1024]{1,0:T(8,128)(2,1)S(1)} %dynamic-slice_convert_fusion), channel_id=1, source_target_pairs={{0,1},{1,0},{2,3},{3,2},{4,5},{5,4},{6,7},{7,6},{8,9},{9,8},{10,11... | collective-permute-start | bytes 3145736 | tf_op jit(solution)/shard_map/ppermute | solution.py:401
  312.7 8.4 %copy-start.13 = (f32[512,1024]{1,0:T(8,128)S(1)}, f32[512,1024]{1,0:T(8,128)}, u32[]{:S(2)}) copy-start(f32[512,1024]{1,0:T(8,128)} %get-tuple-element.118) | copy-start | bytes 6291460
  312.7 8.4 %copy-start.21 = (bf16[512,1024]{1,0:T(8,128)(2,1)S(1)}, bf16[512,1024]{1,0:T(8,128)(2,1)}, u32[]{:S(2)}) copy-start(bf16[512,1024]{1,0:T(8,128)(2,1)} %param.16) | copy-start | bytes 3145732
  312.7 8.4 %copy-start.59 = (f32[512]{0:T(512)S(1)}, f32[512]{0:T(512)}, u32[]{:S(2)}) copy-start(f32[512]{0:T(512)} %copy-done.58) | copy-start | bytes 6148
  312.7 11.4 %slice-start.1 = ((s8[5242880]{0:T(1024)(128)(4,1)}), s8[4194304]{0:T(1024)(128)(4,1)S(1)}, s32[]{:S(2)}) async-start(s8[5242880]{0:T(1024)(128)(4,1)} %bitcast.300), calls=%async_computation.1 | async-start | bytes 8388608
  351.9 9.7 %collective-permute-start.7 = (bf16[512,4,128]{2,0,1:T(8,128)(2,1)S(1)}, bf16[512,4,128]{2,0,1:T(8,128)(2,1)S(1)}, u32[]{:S(2)}, u32[]{:S(2)}) collective-permute-start(bf16[512,4,128]{2,0,1:T(8,128)(2,1)S(1)} %slice.350), channel_id=1, source_target_pairs={{1,0},{3,2},{5,4},{7,6},{9,8},{11,10},{13,12},{15,14},{17,16},{19,... | collective-permute-start | bytes 1572872 | tf_op jit(solution)/shard_map/ppermute | solution.py:24
  354.2 19.6 %collective-permute-start.6 = (bf16[512,4,128]{0,2,1:T(8,128)(2,1)}, bf16[512,4,128]{0,2,1:T(8,128)(2,1)}, u32[]{:S(2)}, u32[]{:S(2)}) collective-permute-start(bf16[512,4,128]{0,2,1:T(8,128)(2,1)} %slice.351), channel_id=1, source_target_pairs={{1,0},{3,2},{5,4},{7,6},{9,8},{11,10},{13,12},{15,14},{17,16},{19,... | collective-permute-start | bytes 1572872 | tf_op jit(solution)/shard_map/ppermute | solution.py:24
  364.3 8.6 %copy-start.41 = (f32[512,20]{0,1:T(8,128)S(1)}, f32[512,20]{0,1:T(8,128)}, u32[]{:S(2)}) copy-start(f32[512,20]{0,1:T(8,128)} %copy-done.40) | copy-start | bytes 122884
  369.3 5.7 %copy-start.17 = (f32[512,4,128]{0,2,1:T(8,128)S(1)}, f32[512,4,128]{0,2,1:T(8,128)}, u32[]{:S(2)}) copy-start(f32[512,4,128]{0,2,1:T(8,128)} %maximum_multiply_fusion.1) | copy-start | bytes 3145732
  369.3 5.7 %copy-start.37 = (f32[512,64]{0,1:T(8,128)S(1)}, f32[512,64]{0,1:T(8,128)}, u32[]{:S(2)}) copy-start(f32[512,64]{0,1:T(8,128)} %copy-done.36) | copy-start | bytes 393220
  369.3 5.7 %copy-start.39 = (f32[512,64]{0,1:T(8,128)S(1)}, f32[512,64]{0,1:T(8,128)}, u32[]{:S(2)}) copy-start(f32[512,64]{0,1:T(8,128)} %copy-done.38) | copy-start | bytes 393220
  519.7 9.7 %copy-start.33 = (f32[512,1024]{1,0:T(8,128)S(1)}, f32[512,1024]{1,0:T(8,128)}, u32[]{:S(2)}) copy-start(f32[512,1024]{1,0:T(8,128)} %copy-done.31) | copy-start | bytes 6291460
  529.3 8.8 %copy-start.44 = (f32[32,2560]{1,0:T(8,128)S(1)}, f32[32,2560]{1,0:T(8,128)}, u32[]{:S(2)}) copy-start(f32[32,2560]{1,0:T(8,128)} %get-tuple-element.200) | copy-start | bytes 983044
  529.3 9.5 %copy-start.43 = (f32[32,2560]{1,0:T(8,128)S(1)}, f32[32,2560]{1,0:T(8,128)}, u32[]{:S(2)}) copy-start(f32[32,2560]{1,0:T(8,128)} %get-tuple-element.30) | copy-start | bytes 983044
  529.3 10.3 %copy-start.1 = (bf16[16,64,128]{2,1,0:T(8,128)(2,1)S(1)}, bf16[16,64,128]{2,1,0:T(8,128)(2,1)}, u32[]{:S(2)}) copy-start(bf16[16,64,128]{2,1,0:T(8,128)(2,1)} %param.28) | copy-start | bytes 786436
  (58 other events, 176.7 us)

commit v3 on v2

--- a/solution.py
+++ b/solution.py
@@ -38,17 +38,53 @@
 
 GRID = (4, 2, 2)
 MESH = pl.DeviceIdType.MESH
-GATHER_PLAN = (
+LEAD_GATHER = (
     (
-        (3, 0, 1152, (2, 0, 1)),
-        (4, 0, 768, (2, 1, 0)),
-        (1, 0, 1280, (0, 1, 2)),
-        (2, 0, 768, (0, 2, 1)),
-        (3, 1152, 1024, (0, 1, 2)),
-        (1, 1280, 1280, (0, 2, 1)),
-        (2, 768, 1792, (0, 1, 2)),
-        (0, 0, 1152, (0, 2, 1)),
-        (4, 768, 1280, (0, 1, 2)),
+        (0, 0, 384, (0, 1, 2)),
+        (1, 0, 512, (2, 1, 0)),
+        (1, 512, 768, (1, 0, 2)),
+        (1, 1280, 640, (0, 2, 1)),
+        (1, 1920, 640, (0, 1, 2)),
+        (0, 384, 768, (0, 2, 1)),
+    ),
+    (
+        (0, 0),
+        (1, 0),
+        (2, 0),
+        (3, 0),
+        (4, 0),
+        (5, 0),
+        (1, 1),
+        (2, 1),
+        (0, 1),
+        (1, 2),
+        (3, 1),
+        (0, 2),
+        (4, 1),
+        (3, 2),
+        (5, 1),
+        (4, 2),
+        (0, 3),
+        (5, 2),
+        (3, 3),
+        (2, 2),
+        (4, 3),
+        (5, 3),
+        (1, 3),
+        (2, 3),
+    ),
+)
+REST_GATHER = (
+    (
+        (0, 0, 1024, (0, 2, 1)),
+        (0, 1024, 512, (0, 1, 2)),
+        (2, 0, 896, (1, 0, 2)),
+        (1, 0, 384, (0, 1, 2)),
+        (0, 1536, 1024, (0, 2, 1)),
+        (2, 896, 512, (1, 2, 0)),
+        (1, 384, 1152, (0, 2, 1)),
+        (1, 1536, 640, (0, 1, 2)),
+        (2, 1408, 640, (0, 2, 1)),
     ),
     (
         (0, 0),
@@ -60,75 +96,99 @@
         (6, 0),
         (7, 0),
         (8, 0),
+        (2, 1),
+        (5, 1),
         (0, 1),
         (1, 1),
+        (5, 2),
+        (3, 1),
+        (1, 2),
+        (0, 2),
+        (4, 1),
+        (3, 2),
+        (1, 3),
+        (4, 2),
+        (0, 3),
+        (6, 1),
+        (7, 1),
+        (4, 3),
+        (8, 1),
+        (6, 2),
+        (7, 2),
+        (8, 2),
+        (2, 2),
+    ),
+)
+REST_SCATTER = (
+    (
+        (0, 0, 1536, (1, 2, 0)),
+        (3, 0, 1024, (1, 2, 0)),
+        (1, 0, 768, (1, 2, 0)),
+        (2, 0, 128, (1, 2, 0)),
+        (3, 1024, 640, (2, 0, 1)),
+        (1, 768, 768, (2, 0, 1)),
+        (1, 1536, 512, (0, 1, 2)),
+        (0, 1536, 1024, (1, 2, 0)),
+        (3, 1664, 384, (2, 1, 0)),
+    ),
+    (
+        (1, 0),
+        (2, 0),
+        (3, 0),
+        (4, 0),
+        (5, 0),
+        (6, 0),
+        (8, 0),
+        (0, 0),
+        (7, 0),
+        (4, 1),
+        (6, 1),
+        (1, 1),
+        (5, 1),
+        (4, 2),
+        (8, 1),
         (2, 1),
         (3, 1),
         (1, 2),
+        (5, 2),
+        (2, 2),
+        (0, 1),
         (3, 2),
-        (2, 2),
-        (4, 1),
-        (3, 3),
-        (5, 1),
-        (2, 3),
-        (4, 2),
-        (6, 1),
-        (5, 2),
+        (0, 2),
         (7, 1),
         (6, 2),
-        (8, 1),
-        (5, 3),
         (7, 2),
         (8, 2),
-        (0, 2),
-        (6, 3),
-        (7, 3),
     ),
 )
-SCATTER_PLAN = (
+LEAD_SCATTER = (
     (
-        (2, 0, 1664, (1, 2, 0)),
-        (2, 1664, 896, (2, 0, 1)),
-        (5, 0, 1152, (2, 0, 1)),
-        (1, 0, 896, (2, 1, 0)),
-        (4, 0, 128, (2, 0, 1)),
-        (1, 896, 1664, (1, 2, 0)),
-        (5, 1152, 896, (1, 2, 0)),
-        (3, 0, 1408, (1, 2, 0)),
-        (0, 0, 1152, (1, 2, 0)),
-        (3, 1408, 640, (0, 1, 2)),
+        (0, 0, 512, (0, 2, 1)),
+        (1, 0, 640, (1, 0, 2)),
+        (1, 640, 896, (2, 1, 0)),
+        (0, 512, 640, (1, 0, 2)),
+        (1, 1536, 640, (2, 1, 0)),
+        (1, 2176, 384, (2, 1, 0)),
     ),
     (
-        (2, 0),
-        (4, 0),
-        (6, 0),
-        (7, 0),
-        (9, 0),
         (0, 0),
         (1, 0),
+        (2, 0),
         (3, 0),
+        (4, 0),
+        (1, 1),
         (5, 0),
-        (8, 0),
-        (6, 1),
+        (0, 1),
         (2, 1),
+        (3, 1),
+        (1, 2),
         (4, 1),
-        (9, 1),
-        (1, 1),
-        (3, 1),
-        (7, 1),
         (2, 2),
+        (3, 2),
+        (5, 1),
+        (0, 2),
         (4, 2),
-        (6, 2),
-        (1, 2),
-        (0, 1),
-        (7, 2),
-        (0, 2),
-        (5, 1),
         (5, 2),
-        (8, 1),
-        (9, 2),
-        (3, 2),
-        (8, 2),
     ),
 )
 
@@ -169,20 +229,38 @@
     return copy
 
 
-def gather_kernel(chunks, events, shared, *refs):
-    count = len(shared)
-    ins, outs = (refs[:count], refs[count : 2 * count])
-    send, recv, local = refs[2 * count :]
-    place, core = (places(), lax.axis_index("col"))
-    greet(place, core)
+def head_cols(head):
+    return slice(head * DH, (head + 1) * DH)
+
+
+def half_turned(values, cosine, sines):
+    return values * cosine + pltpu.roll(values, DH // 2, 1) * sines
+
+
+def masked_pair(queries, keys, others, limits, core):
+    rows = queries.shape[0]
+    query_at = core * rows + lax.broadcasted_iota(jnp.int32, (rows, rows), 0)
+    key_at = lax.broadcasted_iota(jnp.int32, (rows, rows), 1)
+    scores = []
+    for block, start in ((keys, core * rows), (others, (1 - core) * rows)):
+        place = start + key_at
+        allowed = (place <= query_at) & (place < limits)
+        scores.append(jnp.where(allowed, contract_last(queries, block), MASKED))
+    return scores
+
+
+def gather_run(chunks, events, shared, ins, outs, send, recv, local, place, core, tasks):
     owns = []
-    for n in range(count):
+    for n in range(len(shared)):
         at = tuple(place) + ((core,) if shared[n] else ())
         owns.append(pltpu.make_async_copy(ins[n], outs[n].at[at], local.at[n]))
         owns[-1].start()
-    sent, flying = ([], {})
+    sent, flying, left = ([], {}, list(tasks))
+    early = sum(1 for _, phase in events if phase == 0)
     waited = False
-    for i, phase in events:
+    for step, (i, phase) in enumerate(events):
+        if left and step >= early and (step - early) % 2 == 0:
+            left.pop(0)()
         which, start, wide, order = chunks[i]
         if phase == 1 and not waited:
             for copy in owns:
@@ -212,11 +290,110 @@
                 for k in range(1, GRID[dim])
             ]
         sent += flying[i]
+    for task in left:
+        task()
     for copies in flying.values():
         for copy in copies:
             copy.wait_recv()
     for copy in sent:
         copy.wait_send()
+
+
+def gather_kernel(chunks, events, shared, *refs):
+    count = len(shared)
+    place, core = (places(), lax.axis_index("col"))
+    greet(place, core)
+    gather_run(
+        chunks, events, shared, refs[:count], refs[count : 2 * count], *refs[2 * count :], place, core, ()
+    )
+
+
+def attend_kernel(chunks, events, shared, *refs):
+    count = len(shared)
+    ins, refs = (refs[:count], refs[count:])
+    lead, value_all, gates, cosine, sines, limits = refs[:6]
+    outs, refs = (refs[6 : 6 + count], refs[6 + count :])
+    query, key, value, key_other, value_other, attended, lse, mixed = refs[:8]
+    send, recv, local, side_send, side_recv = refs[8:]
+    place, core = (places(), lax.axis_index("col"))
+    greet(place, core)
+    side = []
+
+    def make_keys():
+        for head in range(H):
+            at = head_cols(head)
+            shift = slice(H * DH + head * DH, H * DH + (head + 1) * DH)
+            key[:, at] = half_turned(lead[:, shift], cosine[...], sines[...]).astype(key.dtype)
+
+    def make_values():
+        for head in range(H):
+            total = None
+            for one in range(head * AEXP, (head + 1) * AEXP):
+                term = value_all[:, head_cols(one)] * gates[:, one : one + 1]
+                total = term if total is None else total + term
+            value[:, head_cols(head)] = total.astype(value.dtype)
+
+    def make_queries():
+        row, col = (row_of(place), 1 - core)
+        side.append(push(key, key_other, side_send.at[0], side_recv.at[0], row, col))
+        side.append(push(value, value_other, side_send.at[1], side_recv.at[1], row, col))
+        for head in range(H):
+            at = head_cols(head)
+            turned = half_turned(lead[:, at], cosine[...], sines[...]) * DH ** (-0.5)
+            query[:, at] = turned.astype(query.dtype)
+
+    def arrive():
+        for copy in side:
+            copy.wait()
+
+    def attend(head):
+        at = head_cols(head)
+        near, far = masked_pair(query[:, at], key[:, at], key_other[:, at], limits[0:1, 0:1], core)
+        top = jnp.maximum(
+            jnp.max(near, axis=1, keepdims=True), jnp.max(far, axis=1, keepdims=True)
+        )
+        near, far = (jnp.exp(near - top), jnp.exp(far - top))
+        total = jnp.sum(near, axis=1, keepdims=True) + jnp.sum(far, axis=1, keepdims=True)
+        near, far = ((near / total).astype(jnp.bfloat16), (far / total).astype(jnp.bfloat16))
+        out = jnp.dot(near, value[:, at], preferred_element_type=jnp.float32) + jnp.dot(
+            far, value_other[:, at], preferred_element_type=jnp.float32
+        )
+        attended[:, at] = out
+        lse[:, at] = jnp.broadcast_to(top + jnp.log(total), out.shape)
+        for one in range(head * AEXP, (head + 1) * AEXP):
+            gate = gates[:, H * AEXP + one : H * AEXP + one + 1]
+            mixed[:, head_cols(one)] = (out * gate).astype(mixed.dtype)
+
+    tasks = [make_keys, make_values, make_queries, arrive]
+    tasks += [functools.partial(attend, head) for head in range(H)]
+    gather_run(chunks, events, shared, ins, outs, send, recv, local, place, core, tasks)
+
+
+def gather_call(kernel, parts, shared, plan, collective_id, more, made, scratch):
+    chunks, events = plan
+    count = len(parts)
+    outs = pl.pallas_call(
+        functools.partial(kernel, chunks, events, shared),
+        out_shape=[
+            jax.ShapeDtypeStruct(GRID + ((2,) if both else ()) + part.shape, part.dtype)
+            for part, both in zip(parts, shared)
+        ]
+        + made,
+        in_specs=[pl.BlockSpec(memory_space=pltpu.VMEM)] * (count + len(more)),
+        out_specs=[pl.BlockSpec(memory_space=pl.ANY)] * count
+        + [pl.BlockSpec(memory_space=pltpu.VMEM)] * len(made),
+        scratch_shapes=[
+            pltpu.SemaphoreType.DMA((len(chunks), 6)),
+            pltpu.SemaphoreType.DMA((len(chunks), 6)),
+            pltpu.SemaphoreType.DMA((count,)),
+        ]
+        + scratch,
+        compiler_params=pltpu.CompilerParams(
+            collective_id=collective_id, has_side_effects=True, vmem_limit_bytes=60 * 1024 * 1024
+        ),
+    )(*parts, *more)
+    whole = [out.reshape(-1, part.shape[1]) for out, part in zip(outs, parts)]
+    return (whole, outs[count:])
 
 
 def gather_parts(parts, shared, plan, collective_id):
@@ -225,24 +402,7 @@
             lax.all_gather(part, ("row", "col") if both else "row", axis=0, tiled=True)
             for part, both in zip(parts, shared)
         ]
-    chunks, events = plan
-    count = len(parts)
-    outs = pl.pallas_call(
-        functools.partial(gather_kernel, chunks, events, shared),
-        out_shape=[
-            jax.ShapeDtypeStruct(GRID + ((2,) if both else ()) + part.shape, part.dtype)
-            for part, both in zip(parts, shared)
-        ],
-        in_specs=[pl.BlockSpec(memory_space=pltpu.VMEM)] * count,
-        out_specs=[pl.BlockSpec(memory_space=pl.ANY)] * count,
-        scratch_shapes=[
-            pltpu.SemaphoreType.DMA((len(chunks), 6)),
-            pltpu.SemaphoreType.DMA((len(chunks), 6)),
-            pltpu.SemaphoreType.DMA((count,)),
-        ],
-        compiler_params=pltpu.CompilerParams(collective_id=collective_id, has_side_effects=True),
-    )(*parts)
-    return [out.reshape(-1, part.shape[1]) for out, part in zip(outs, parts)]
+    return gather_call(gather_kernel, parts, shared, plan, collective_id, [], [], [])[0]
 
 
 def add_blocks(target, terms, lead, rows):
@@ -264,20 +424,12 @@
     lax.fori_loop(0, math.prod(lead) * steps, body, 0)
 
 
-def scatter_kernel(chunks, events, shared, *refs):
-    count = len(shared)
-    ins, outs = (refs[:count], refs[count : 2 * count])
-    send, recv, local = refs[2 * count : 2 * count + 3]
-    slots = list(refs[2 * count + 3 :])
-    place, core = (places(), lax.axis_index("col"))
+def scatter_run(chunks, events, shared, ins, outs, send, recv, local, slots, place, core, tasks):
+    slots, rest = (list(slots), list(tasks))
     held = {}
     for i in range(len(chunks)):
         held[i] = [slots.pop(0) for _ in range(5 if shared[chunks[i][0]] else 4)]
-    greet(place, core)
     sent, flying, owns = ([], {}, {})
-
-    def lead_of(order, phase):
-        return [GRID[dim] for dim in range(3) if dim not in order[: phase + 1]]
 
     for i in dict.fromkeys(i for i, _ in events):
         which, start, wide, order = chunks[i]
@@ -285,7 +437,9 @@
         if shared[which]:
             own = ins[which].at[:, :, :, core, :, cols]
             other = ins[which].at[:, :, :, 1 - core, :, cols]
-            flying[i] = [push(other, held[i][1], send.at[i, 5], recv.at[i, 5], row_of(place), 1 - core)]
+            flying[i] = [
+                push(other, held[i][1], send.at[i, 5], recv.at[i, 5], row_of(place), 1 - core)
+            ]
             sent += flying[i]
         else:
             at = [slice(None)] * 3
@@ -316,13 +470,16 @@
             own = held[i][0]
         else:
             left = [d for d in range(3) if d not in order[:phase]]
-            at = tuple(place[dim] if d == dim else slice(None) for d in left)
-            own = source_of(i, phase).at[at]
+            own = source_of(i, phase).at[tuple(place[dim] if d == dim else slice(None) for d in left)]
         target = outs[which].at[:, pl.ds(start, wide)] if phase == 2 else came.at[0]
         terms = [own] + [came.at[k] for k in range(GRID[dim] - 1)]
-        add_blocks(target, terms, lead_of(order, phase), rows)
-
-    for i, phase in events:
+        lead = [GRID[d] for d in range(3) if d not in order[: phase + 1]]
+        add_blocks(target, terms, lead, rows)
+
+    early = sum(1 for i, phase in events if phase == 0 and not shared[chunks[i][0]])
+    for step, (i, phase) in enumerate(events):
+        if rest and step >= early and (step - early) % 2 == 0:
+            rest.pop(0)()
         which, start, wide, order = chunks[i]
         if phase > 0 or shared[which]:
             landed(i, phase - 1)
@@ -344,10 +501,145 @@
                 )
             )
         sent += flying[i]
+    for task in rest:
+        task()
     for i in list(flying):
         landed(i, 2)
     for copy in sent:
         copy.wait_send()
+
+
+def scatter_kernel(chunks, events, shared, *refs):
+    count = len(shared)
+    ins, outs = (refs[:count], refs[count : 2 * count])
+    send, recv, local = refs[2 * count : 2 * count + 3]
+    place, core = (places(), lax.axis_index("col"))
+    greet(place, core)
+    slots = refs[2 * count + 3 :]
+    scatter_run(chunks, events, shared, ins, outs, send, recv, local, slots, place, core, ())
+
+
+def attend_back_kernel(chunks, events, shared, *refs):
+    count = len(shared)
+    ins, refs = (refs[:count], refs[count:])
+    query, key, value, key_other, value_other, attended, lse, grad_mixed = refs[:8]
+    value_all, gates, sigs, cosine, sines, limits = refs[8:14]
+    outs, refs = (refs[14 : 14 + count], refs[14 + count :])
+    lead_back, grad_value_all = refs[:2]
+    send, recv, local, side_send, side_recv = refs[2:7]
+    grad_key, grad_value, grad_gates, key_leave, value_leave, key_came, value_came = refs[7:14]
+    slots = refs[14:]
+    place, core = (places(), lax.axis_index("col"))
+    greet(place, core)
+    side = []
+    gated = H * AEXP
+
+    def put_gate(one, column):
+        lanes = lax.broadcasted_iota(jnp.int32, grad_gates.shape, 1)
+        grad_gates[...] = jnp.where(lanes == one, column, grad_gates[...])
+
+    def attend_back(head):
+        at = head_cols(head)
+        if head == 0:
+            grad_gates[...] = jnp.zeros_like(grad_gates)
+        total = None
+        for one in range(head * AEXP, (head + 1) * AEXP):
+            gate = gates[:, gated + one : gated + one + 1]
+            piece = grad_mixed[:, head_cols(one)].astype(jnp.float32)
+            put_gate(gated + one, jnp.sum(piece * attended[:, at], axis=1, keepdims=True))
+            total = piece * gate if total is None else total + piece * gate
+        grad_out = total.astype(jnp.bfloat16)
+        queries, keys, others = (query[:, at], key[:, at], key_other[:, at])
+        near, far = masked_pair(queries, keys, others, limits[0:1, 0:1], core)
+        level = lse[:, head * DH : head * DH + 1]
+        near, far = (jnp.exp(near - level), jnp.exp(far - level))
+        near_grad = contract_last(grad_out, value[:, at])
+        far_grad = contract_last(grad_out, value_other[:, at])
+        mean = jnp.sum(near * near_grad, axis=1, keepdims=True) + jnp.sum(
+            far * far_grad, axis=1, keepdims=True
+        )
+        near_grad = (near * (near_grad - mean)).astype(jnp.bfloat16)
+        far_grad = (far * (far_grad - mean)).astype(jnp.bfloat16)
+        near, far = (near.astype(jnp.bfloat16), far.astype(jnp.bfloat16))
+        grad_query = jnp.dot(near_grad, keys, preferred_element_type=jnp.float32) + jnp.dot(
+            far_grad, others, preferred_element_type=jnp.float32
+        )
+        turned = half_turned(grad_query * DH ** (-0.5), cosine[...], -sines[...])
+        lead_back[:, at] = turned.astype(lead_back.dtype)
+        grad_key[:, at] = contract_first(near_grad, queries)
+        grad_value[:, at] = contract_first(near, grad_out)
+        key_leave[:, at] = contract_first(far_grad, queries).astype(key_leave.dtype)
+        value_leave[:, at] = contract_first(far, grad_out).astype(value_leave.dtype)
+
+    def leave():
+        row, col = (row_of(place), 1 - core)
+        side.append(push(key_leave, key_came, side_send.at[0], side_recv.at[0], row, col))
+        side.append(push(value_leave, value_came, side_send.at[1], side_recv.at[1], row, col))
+
+    def arrive():
+        for copy in side:
+            copy.wait()
+
+    def finish(head):
+        at = head_cols(head)
+        turned = half_turned(
+            grad_key[:, at] + key_came[:, at].astype(jnp.float32), cosine[...], -sines[...]
+        )
+        lead_back[:, H * DH + head * DH : H * DH + (head + 1) * DH] = turned.astype(lead_back.dtype)
+        whole = grad_value[:, at] + value_came[:, at].astype(jnp.float32)
+        for one in range(head * AEXP, (head + 1) * AEXP):
+            grad_value_all[:, head_cols(one)] = (whole * gates[:, one : one + 1]).astype(
+                grad_value_all.dtype
+            )
+            put_gate(one, jnp.sum(value_all[:, head_cols(one)] * whole, axis=1, keepdims=True))
+        if head == H - 1:
+            lead_back[:, 2 * H * DH :] = (
+                grad_gates[...] * gates[...] * (1.0 - sigs[...])
+            ).astype(lead_back.dtype)
+
+    tasks = [functools.partial(attend_back, head) for head in range(H)]
+    tasks += [leave, arrive] + [functools.partial(finish, head) for head in range(H)]
+    scatter_run(chunks, events, shared, ins, outs, send, recv, local, slots, place, core, tasks)
+
+
+def scatter_call(kernel, parts, shared, plan, collective_id, more, made, scratch):
+    chunks, events = plan
+    count = len(parts)
+    views = []
+    for part, both in zip(parts, shared):
+        rows = part.shape[0] // (math.prod(GRID) * (2 if both else 1))
+        views.append(part.reshape(GRID + ((2,) if both else ()) + (rows, part.shape[1])))
+    slots = []
+    for which, _, wide, order in chunks:
+        rows = views[which].shape[-2]
+        if shared[which]:
+            slots += [pltpu.VMEM(GRID + (rows, wide), jnp.bfloat16)] * 2
+        else:
+            lead = tuple(GRID[dim] for dim in range(3) if dim != order[0])
+            slots.append(pltpu.VMEM(lead + (rows, wide), jnp.bfloat16))
+        for phase in range(3):
+            lead = tuple(GRID[dim] for dim in range(3) if dim not in order[: phase + 1])
+            slots.append(
+                pltpu.VMEM((GRID[order[phase]] - 1,) + lead + (rows, wide), jnp.bfloat16)
+            )
+    outs = pl.pallas_call(
+        functools.partial(kernel, chunks, events, shared),
+        out_shape=[jax.ShapeDtypeStruct(view.shape[-2:], jnp.float32) for view in views] + made,
+        in_specs=[pl.BlockSpec(memory_space=pl.ANY)] * count
+        + [pl.BlockSpec(memory_space=pltpu.VMEM)] * len(more),
+        out_specs=[pl.BlockSpec(memory_space=pltpu.VMEM)] * (count + len(made)),
+        scratch_shapes=[
+            pltpu.SemaphoreType.DMA((len(chunks), 6)),
+            pltpu.SemaphoreType.DMA((len(chunks), 6)),
+            pltpu.SemaphoreType.DMA((len(chunks),)),
+        ]
+        + scratch
+        + slots,
+        compiler_params=pltpu.CompilerParams(
+            collective_id=collective_id, has_side_effects=True, vmem_limit_bytes=62 * 1024 * 1024
+        ),
+    )(*views, *more)
+    return (outs[:count], outs[count:])
 
 
 def scatter_parts(parts, shared, plan, collective_id):
@@ -361,40 +653,7 @@
             )
             for part, both in zip(parts, shared)
         ]
-    chunks, events = plan
-    count = len(parts)
-    views = []
-    for part, both in zip(parts, shared):
-        rows = part.shape[0] // (math.prod(GRID) * (2 if both else 1))
-        views.append(part.reshape(GRID + ((2,) if both else ()) + (rows, part.shape[1])))
-    scratch = []
-    for which, _, wide, order in chunks:
-        rows = views[which].shape[-2]
-        if shared[which]:
-            scratch += [pltpu.VMEM(GRID + (rows, wide), jnp.bfloat16)] * 2
-        else:
-            lead = tuple(GRID[dim] for dim in range(3) if dim != order[0])
-            scratch.append(pltpu.VMEM(lead + (rows, wide), jnp.bfloat16))
-        for phase in range(3):
-            lead = tuple(GRID[dim] for dim in range(3) if dim not in order[: phase + 1])
-            scratch.append(
-                pltpu.VMEM((GRID[order[phase]] - 1,) + lead + (rows, wide), jnp.bfloat16)
-            )
-    return pl.pallas_call(
-        functools.partial(scatter_kernel, chunks, events, shared),
-        out_shape=[jax.ShapeDtypeStruct(view.shape[-2:], jnp.float32) for view in views],
-        in_specs=[pl.BlockSpec(memory_space=pl.ANY)] * count,
-        out_specs=[pl.BlockSpec(memory_space=pltpu.VMEM)] * count,
-        scratch_shapes=[
-            pltpu.SemaphoreType.DMA((len(chunks), 6)),
-            pltpu.SemaphoreType.DMA((len(chunks), 6)),
-            pltpu.SemaphoreType.DMA((len(chunks),)),
-        ]
-        + scratch,
-        compiler_params=pltpu.CompilerParams(
-            collective_id=collective_id, has_side_effects=True, vmem_limit_bytes=60 * 1024 * 1024
-        ),
-    )(*views)
+    return scatter_call(scatter_kernel, parts, shared, plan, collective_id, [], [], [])[0]
 
 
 def sibling(value):
@@ -527,14 +786,12 @@
         axis=1,
     )
     down_local = jnp.transpose(expert_down, (2, 0, 1)).reshape(-1, hidden)
-    lead_full, value_full, output_turned, up_wide, down_turned = gather_parts(
-        [lead_local, value_weight, output_weight.T, up_local, down_local],
-        [True, True, True, False, False],
-        GATHER_PLAN,
-        1,
-    )
-    up_full = up_wide[:, :hidden]
-    router_cols = up_wide[:, hidden : hidden + local_experts]
+    lead_full, value_full = gather_parts(
+        [lead_local, value_weight], [True, True], LEAD_GATHER, 1
+    )
+    rest_local = [output_weight.T, up_local, down_local]
+    rest_shared = [True, False, False]
+    paired = by_grid() and key_span == 2 and lengths.shape[0] == 1
     extra_at = 2 * H * DH + 2 * gated
     extra = lead_full[:, extra_at : extra_at + 4].astype(jnp.float32)
     gain_one = extra[:, 0]
@@ -554,70 +811,96 @@
     normed_one, hat_one, inv_one = norm_parts(inputs_full, gain_one)
     normed_low = normed_one.astype(jnp.bfloat16)
     lead_raw = jnp.dot(normed_low, lead_full, preferred_element_type=jnp.float32)
-    query_raw = lead_raw[:, : H * DH]
-    key_raw = lead_raw[:, H * DH : 2 * H * DH]
-    route_logits = lead_raw[:, 2 * H * DH : extra_at]
     cosine, sines = rope_tables(seq_pos, DH)
-    query_scale = DH ** (-0.5)
-    query_rot = (rotate(query_raw.reshape(tok_rows, H, DH), cosine, sines) * query_scale).astype(
-        jnp.bfloat16
-    )
-    key_rot = rotate(key_raw.reshape(tok_rows, H, DH), cosine, sines).astype(jnp.bfloat16)
     chosen = jnp.any(
         head_routes[:, :, :, None] == jnp.arange(AEXP, dtype=jnp.int32)[None, None, None, :], axis=2
     ).astype(jnp.float32)
-    value_sig = jax.nn.sigmoid(route_logits[:, :gated]).reshape(tok_rows, H, AEXP)
-    output_sig = jax.nn.sigmoid(route_logits[:, gated:]).reshape(tok_rows, H, AEXP)
-    value_gates = value_sig * chosen
-    output_gates = output_sig * chosen
-    value_all = jnp.dot(block_input, value_full, preferred_element_type=jnp.float32).reshape(
-        tok_rows, H, AEXP, DH
-    )
-    values_low = jnp.sum(value_all * value_gates[..., None], axis=2).astype(jnp.bfloat16)
-    key_parts = [key_rot]
-    value_parts = [values_low]
-    id_parts = [group_ids]
-    for offset in range(1, key_span):
-        came_keys, came_values = shifted((key_rot, values_low), "col", offset)
-        key_parts.append(came_keys)
-        value_parts.append(came_values)
-        id_parts.append(group_ids - offset * tok_rows)
-    keys_all = jnp.concatenate(key_parts, axis=0)
-    values_all = jnp.concatenate(value_parts, axis=0)
-    key_ids = jnp.concatenate(id_parts, axis=0)
-    allowed = (
-        (key_ids[None, :] // seq_length == seq_ids[:, None])
-        & (key_ids[None, :] <= group_ids[:, None])
-        & (key_ids[None, :] % seq_length < tok_length[:, None])
-    )
-
-    def head_scores(head_idx):
-        raw_scores = jnp.einsum(
-            "qd,kd->qk",
-            query_rot[:, head_idx],
-            keys_all[:, head_idx],
-            preferred_element_type=jnp.float32,
-        )
-        return jnp.where(allowed, raw_scores, MASKED)
-
-    attended_list = []
-    lse_list = []
-    for head_idx in range(H):
-        scores = head_scores(head_idx)
-        row_top = jnp.max(scores, axis=1, keepdims=True)
-        exponent = jnp.exp(scores - row_top)
-        row_total = jnp.sum(exponent, axis=1, keepdims=True)
-        probs_low = (exponent / row_total).astype(jnp.bfloat16)
-        attended_list.append(
-            jnp.dot(probs_low, values_all[:, head_idx], preferred_element_type=jnp.float32)
-        )
-        lse_list.append(row_top + jnp.log(row_total))
-    attended = jnp.stack(attended_list, axis=1)
-    mixed_low = (
-        (attended[:, :, None, :] * output_gates[..., None])
-        .astype(jnp.bfloat16)
-        .reshape(tok_rows, gated * DH)
-    )
+    value_flat = jnp.dot(block_input, value_full, preferred_element_type=jnp.float32)
+    if paired:
+        sigs = jax.nn.sigmoid(lead_raw[:, 2 * H * DH :])
+        picked = chosen.reshape(tok_rows, gated)
+        both_gates = sigs * padded(jnp.concatenate([picked, picked], axis=1), 128)
+        cos_wide = jnp.concatenate([cosine, cosine], axis=1)
+        sin_wide = jnp.concatenate([-sines, sines], axis=1)
+        limits = jnp.broadcast_to(lengths[:, None], (8, 128))
+        low, full = (jnp.bfloat16, jnp.float32)
+        made = [jax.ShapeDtypeStruct((tok_rows, H * DH), kind) for kind in [low] * 5 + [full] * 2]
+        made.append(jax.ShapeDtypeStruct((tok_rows, gated * DH), low))
+        (output_turned, up_wide, down_turned), kept = gather_call(
+            attend_kernel,
+            rest_local,
+            rest_shared,
+            REST_GATHER,
+            2,
+            [lead_raw, value_flat, both_gates, cos_wide, sin_wide, limits],
+            made,
+            [pltpu.SemaphoreType.DMA((2,))] * 2,
+        )
+        mixed_low = kept[7]
+    else:
+        output_turned, up_wide, down_turned = gather_parts(
+            rest_local, rest_shared, REST_GATHER, 2
+        )
+        query_raw = lead_raw[:, : H * DH]
+        key_raw = lead_raw[:, H * DH : 2 * H * DH]
+        route_logits = lead_raw[:, 2 * H * DH : extra_at]
+        query_scale = DH ** (-0.5)
+        query_rot = (rotate(query_raw.reshape(tok_rows, H, DH), cosine, sines) * query_scale).astype(
+            jnp.bfloat16
+        )
+        key_rot = rotate(key_raw.reshape(tok_rows, H, DH), cosine, sines).astype(jnp.bfloat16)
+        value_sig = jax.nn.sigmoid(route_logits[:, :gated]).reshape(tok_rows, H, AEXP)
+        output_sig = jax.nn.sigmoid(route_logits[:, gated:]).reshape(tok_rows, H, AEXP)
+        value_gates = value_sig * chosen
+        output_gates = output_sig * chosen
+        value_all = value_flat.reshape(tok_rows, H, AEXP, DH)
+        values_low = jnp.sum(value_all * value_gates[..., None], axis=2).astype(jnp.bfloat16)
+        key_parts = [key_rot]
+        value_parts = [values_low]
+        id_parts = [group_ids]
+        for offset in range(1, key_span):
+            came_keys, came_values = shifted((key_rot, values_low), "col", offset)
+            key_parts.append(came_keys)
+            value_parts.append(came_values)
+            id_parts.append(group_ids - offset * tok_rows)
+        keys_all = jnp.concatenate(key_parts, axis=0)
+        values_all = jnp.concatenate(value_parts, axis=0)
+        key_ids = jnp.concatenate(id_parts, axis=0)
+        allowed = (
+            (key_ids[None, :] // seq_length == seq_ids[:, None])
+            & (key_ids[None, :] <= group_ids[:, None])
+            & (key_ids[None, :] % seq_length < tok_length[:, None])
+        )
+
+        def head_scores(head_idx):
+            raw_scores = jnp.einsum(
+                "qd,kd->qk",
+                query_rot[:, head_idx],
+                keys_all[:, head_idx],
+                preferred_element_type=jnp.float32,
+            )
+            return jnp.where(allowed, raw_scores, MASKED)
+
+        attended_list = []
+        lse_list = []
+        for head_idx in range(H):
+            scores = head_scores(head_idx)
+            row_top = jnp.max(scores, axis=1, keepdims=True)
+            exponent = jnp.exp(scores - row_top)
+            row_total = jnp.sum(exponent, axis=1, keepdims=True)
+            probs_low = (exponent / row_total).astype(jnp.bfloat16)
+            attended_list.append(
+                jnp.dot(probs_low, values_all[:, head_idx], preferred_element_type=jnp.float32)
+            )
+            lse_list.append(row_top + jnp.log(row_total))
+        attended = jnp.stack(attended_list, axis=1)
+        mixed_low = (
+            (attended[:, :, None, :] * output_gates[..., None])
+            .astype(jnp.bfloat16)
+            .reshape(tok_rows, gated * DH)
+        )
+    up_full = up_wide[:, :hidden]
+    router_cols = up_wide[:, hidden : hidden + local_experts]
     resid = inputs_full + contract_last(mixed_low, output_turned)
     resid_low = resid.astype(jnp.bfloat16)
     group_in = gather_col(resid_low)
@@ -659,79 +942,101 @@
     grad_resid = grad_output + moe_grad
     grad_branch = grad_resid.astype(jnp.bfloat16)
     output_grad = contract_first(grad_branch, mixed_low).astype(jnp.bfloat16)
-    grad_mixed = (
-        jnp.dot(grad_branch, output_turned, preferred_element_type=jnp.float32)
-        .astype(jnp.bfloat16)
-        .astype(jnp.float32)
-        .reshape(tok_rows, H, AEXP, DH)
-    )
-    grad_attended = jnp.sum(grad_mixed * output_gates[..., None], axis=2).astype(jnp.bfloat16)
-    grad_output_gates = jnp.sum(grad_mixed * attended[:, :, None, :], axis=3)
-    query_grads = []
-    key_grads = []
-    value_grads = []
-    for head_idx in range(H):
-        scores = head_scores(head_idx)
-        probs_full = jnp.exp(scores - lse_list[head_idx])
-        probs_low = probs_full.astype(jnp.bfloat16)
-        grad_probs = jnp.einsum(
-            "qd,kd->qk",
-            grad_attended[:, head_idx],
-            values_all[:, head_idx],
-            preferred_element_type=jnp.float32,
-        )
-        grad_scores = (
-            probs_full * (grad_probs - jnp.sum(probs_full * grad_probs, axis=1, keepdims=True))
+    grad_mixed_low = jnp.dot(
+        grad_branch, output_turned, preferred_element_type=jnp.float32
+    ).astype(jnp.bfloat16)
+    rest_grads = [output_grad, up_grad, router_grad, down_grad]
+    rest_shared = [True, False, False, False]
+    if paired:
+        wide = (tok_rows, H * DH)
+        sums, (lead_back, grad_value_all) = scatter_call(
+            attend_back_kernel,
+            rest_grads,
+            rest_shared,
+            REST_SCATTER,
+            3,
+            list(kept[:7])
+            + [grad_mixed_low, value_flat, both_gates, sigs, cos_wide, sin_wide, limits],
+            [
+                jax.ShapeDtypeStruct((tok_rows, 2 * H * DH + 128), low),
+                jax.ShapeDtypeStruct((tok_rows, gated * DH), low),
+            ],
+            [pltpu.SemaphoreType.DMA((2,))] * 2
+            + [pltpu.VMEM(wide, full)] * 2
+            + [pltpu.VMEM((tok_rows, 128), full)]
+            + [pltpu.VMEM(wide, low)] * 4,
+        )
+    else:
+        sums = scatter_parts(rest_grads, rest_shared, REST_SCATTER, 3)
+        grad_mixed = grad_mixed_low.astype(jnp.float32).reshape(tok_rows, H, AEXP, DH)
+        grad_attended = jnp.sum(grad_mixed * output_gates[..., None], axis=2).astype(jnp.bfloat16)
+        grad_output_gates = jnp.sum(grad_mixed * attended[:, :, None, :], axis=3)
+        query_grads = []
+        key_grads = []
+        value_grads = []
+        for head_idx in range(H):
+            scores = head_scores(head_idx)
+            probs_full = jnp.exp(scores - lse_list[head_idx])
+            probs_low = probs_full.astype(jnp.bfloat16)
+            grad_probs = jnp.einsum(
+                "qd,kd->qk",
+                grad_attended[:, head_idx],
+                values_all[:, head_idx],
+                preferred_element_type=jnp.float32,
+            )
+            grad_scores = (
+                probs_full * (grad_probs - jnp.sum(probs_full * grad_probs, axis=1, keepdims=True))
+            ).astype(jnp.bfloat16)
+            query_grads.append(
+                jnp.dot(grad_scores, keys_all[:, head_idx], preferred_element_type=jnp.float32)
+            )
+            key_grads.append(contract_first(grad_scores, query_rot[:, head_idx]))
+            value_grads.append(contract_first(probs_low, grad_attended[:, head_idx]))
+        grad_queries = jnp.stack(query_grads, axis=1)
+        key_grads_all = jnp.stack(key_grads, axis=1)
+        value_grads_all = jnp.stack(value_grads, axis=1)
+        grad_key_rot = key_grads_all[:tok_rows]
+        grad_values = value_grads_all[:tok_rows]
+        for offset in range(1, key_span):
+            back_keys, back_values = (
+                shifted(
+                    key_grads_all[offset * tok_rows : (offset + 1) * tok_rows].astype(jnp.bfloat16),
+                    "col",
+                    -offset,
+                ).astype(jnp.float32),
+                shifted(
+                    value_grads_all[offset * tok_rows : (offset + 1) * tok_rows].astype(jnp.bfloat16),
+                    "col",
+                    -offset,
+                ).astype(jnp.float32),
+            )
+            grad_key_rot = grad_key_rot + back_keys
+            grad_values = grad_values + back_values
+        grad_value_all = (
+            (grad_values[:, :, None, :] * value_gates[..., None])
+            .astype(jnp.bfloat16)
+            .reshape(tok_rows, gated * DH)
+        )
+        grad_value_gates = jnp.sum(value_all * grad_values[:, :, None, :], axis=3)
+        grad_query_raw = (
+            unrotate(grad_queries * query_scale, cosine, sines)
+            .astype(jnp.bfloat16)
+            .reshape(tok_rows, H * DH)
+        )
+        grad_key_raw = (
+            unrotate(grad_key_rot, cosine, sines).astype(jnp.bfloat16).reshape(tok_rows, H * DH)
+        )
+        grad_route = jnp.concatenate(
+            [
+                (grad_value_gates * chosen * value_sig * (1.0 - value_sig)).reshape(tok_rows, gated),
+                (grad_output_gates * chosen * output_sig * (1.0 - output_sig)).reshape(tok_rows, gated),
+            ],
+            axis=1,
         ).astype(jnp.bfloat16)
-        query_grads.append(
-            jnp.dot(grad_scores, keys_all[:, head_idx], preferred_element_type=jnp.float32)
-        )
-        key_grads.append(contract_first(grad_scores, query_rot[:, head_idx]))
-        value_grads.append(contract_first(probs_low, grad_attended[:, head_idx]))
-    grad_queries = jnp.stack(query_grads, axis=1)
-    key_grads_all = jnp.stack(key_grads, axis=1)
-    value_grads_all = jnp.stack(value_grads, axis=1)
-    grad_key_rot = key_grads_all[:tok_rows]
-    grad_values = value_grads_all[:tok_rows]
-    for offset in range(1, key_span):
-        back_keys, back_values = (
-            shifted(
-                key_grads_all[offset * tok_rows : (offset + 1) * tok_rows].astype(jnp.bfloat16),
-                "col",
-                -offset,
-            ).astype(jnp.float32),
-            shifted(
-                value_grads_all[offset * tok_rows : (offset + 1) * tok_rows].astype(jnp.bfloat16),
-                "col",
-                -offset,
-            ).astype(jnp.float32),
-        )
-        grad_key_rot = grad_key_rot + back_keys
-        grad_values = grad_values + back_values
-    grad_value_all = (
-        (grad_values[:, :, None, :] * value_gates[..., None])
-        .astype(jnp.bfloat16)
-        .reshape(tok_rows, gated * DH)
-    )
-    grad_value_gates = jnp.sum(value_all * grad_values[:, :, None, :], axis=3)
-    grad_query_raw = (
-        unrotate(grad_queries * query_scale, cosine, sines)
-        .astype(jnp.bfloat16)
-        .reshape(tok_rows, H * DH)
-    )
-    grad_key_raw = (
-        unrotate(grad_key_rot, cosine, sines).astype(jnp.bfloat16).reshape(tok_rows, H * DH)
-    )
-    grad_route = jnp.concatenate(
-        [
-            (grad_value_gates * chosen * value_sig * (1.0 - value_sig)).reshape(tok_rows, gated),
-            (grad_output_gates * chosen * output_sig * (1.0 - output_sig)).reshape(tok_rows, gated),
-        ],
-        axis=1,
-    ).astype(jnp.bfloat16)
-    lead_back = padded(
-        jnp.concatenate([grad_query_raw, grad_key_raw, grad_route], axis=1), 2 * H * DH + 128
-    )
+        lead_back = padded(
+            jnp.concatenate([grad_query_raw, grad_key_raw, grad_route], axis=1), 2 * H * DH + 128
+        )
+    output_turned_sum, up_sum, router_sum, down_sum = sums
     value_grad = contract_first(block_input, grad_value_all).astype(jnp.bfloat16)
     grad_norm_one = contract_last(lead_back, lead_full)
     first_gain_part = jnp.sum(grad_norm_one * hat_one, axis=0)
@@ -746,12 +1051,7 @@
         + jnp.where(lead_cols == extra_at, first_gain_part[:, None], 0.0)
         + jnp.where(lead_cols == extra_at + 1, second_gain_part[:, None], 0.0)
     ).astype(jnp.bfloat16)
-    lead_sum, value_sum, output_turned_sum, up_sum, router_sum, down_sum = scatter_parts(
-        [lead_grad, value_grad, output_grad, up_grad, router_grad, down_grad],
-        [True, True, True, False, False, False],
-        SCATTER_PLAN,
-        2,
-    )
+    lead_sum, value_sum = scatter_parts([lead_grad, value_grad], [True, True], LEAD_SCATTER, 4)
     output_sum = output_turned_sum.T
     router_sum = router_sum[:, :local_experts]
     up_out = jnp.transpose(up_sum.reshape(-1, local_experts, hidden_local), (1, 0, 2))

time: 549 us -> 500 us (0.911); the launches traced: 540 us -> 496 us
  Pallas kernels: 277 us -> 324 us
  other arithmetic: 57.6 us -> 22.8 us
  local copies, waits for them, and re-layouts: 65.9 us -> 33.7 us
  matrix products: 126 us -> 107 us
  starting transfers between devices: 7.02 us -> 0.95 us
    pallas_call x2 -> x4, Pallas kernels: 277 us -> 324 us  [the longest x2 173 us: gather_call(): pl.pallas_call(functools.partial(kernel, chunks, events, shared), out_sha...]
    reduce_sum x7 -> x0, other arithmetic: 12.2 us -> none  [the longest x1 5 us: shards(): grad_value_gates = jnp.sum(value_all * grad_values[:, :, None, :], axis=3)]
    dot_general x16 -> x0, matrix products: 9.72 us -> none  [the longest x4 3.15 us: head_scores(): jnp.einsum('qd,kd->qk', query_rot[:, head_idx], keys_all[:, head_idx], pr...]
    unnamed x205 -> x69, local copies, waits for them, and re-layouts: 20.1 us -> 12.3 us
    reshape x5 -> x0, local copies, waits for them, and re-layouts: 7.83 us -> none  [the longest x1 5.92 us: shards(): grad_mixed = jnp.dot(grad_branch, output_turned, preferred_element_type=j...]
    ppermute x4 -> x0, starting transfers between devices: 6.31 us -> none  [shifted(): lax.ppermute(value, axis, [(source, source + steps) for source in range(l...]
    dot_general x14 -> x6, matrix products: 35.7 us -> 29.7 us  [contract_first(): lax.dot_general(left, right, (((0,), (0,)), ((), ())), preferred_element_...]
  transfers between devices with their start and end apart: 8 -> 4, of which waited for: 1 -> 3; matrix products, arithmetic and copies ran while one was open for 10% -> 2% of each run, Pallas kernels for 0% -> 0%
where the time goes in v3:
time: 500 us; the launch traced here: 496 us
  Pallas kernels  324 us (65%)
  matrix products  107 us (21%)
  local copies, waits for them, and re-layouts  33.7 us (7%)
  other arithmetic  22.8 us (5%)
  waiting for transfers between devices  5.15 us (1%)
    pallas_call x2, Pallas kernels, gather_call(): pl.pallas_call(functools.partial(kernel, chunks, events, shared), out_sha...  173 us
    pallas_call x2, Pallas kernels, scatter_call(): pl.pallas_call(functools.partial(kernel, chunks, events, shared), out_sha...  151 us
    dot_general x6, matrix products, contract_last(): lax.dot_general(left, right, (((1,), (1,)), ((), ())), preferred_element_...  43.5 us
    dot_general x6, matrix products, contract_first(): lax.dot_general(left, right, (((0,), (0,)), ((), ())), preferred_element_...  29.7 us
    unnamed x69, local copies, waits for them, and re-layouts  12.3 us
    dot_general x1, matrix products, shards(): jnp.dot(group_grad, down_turned, preferred_element_type=jnp.float32)  12.2 us
  transfers between devices with their start and end apart: 4, of which 3 were waited for; matrix products, arithmetic and copies ran while one was open for 2% of the time, Pallas kernels for 0%

profile of v3, /device:TPU:0, one launch (start us, length us, event | category | flops | bytes accessed | tf_op | source)
XLA Modules:
  0.0 496.4 jit_solution(15716677511971506577)
XLA Ops:
  1.6 1.4 convert_reduce_fusion.1
  3.0 1.6 fusion.33
  4.7 0.8 copy.78
  7.0 0.8 copy.76
  9.5 49.6 %shard_map.238 = (bf16[4,2,2,2,32,1152]{5,4,3,2,1,0:T(8,128)(2,1)}, bf16[4,2,2,2,32,2560]{5,4,3,2,1,0:T(8,128)(2,1)}) custom-call(bf16[32,1152]{1,0:T(8,128)(2,1)} %pad.18.refs_0_, bf16[32,2560]{1,0:T(8,128)(2,1)} %refs_1_.1), custom_call_target="tpu_custom_call" | custom-call | tf_op jit(solution)/shard_map/pallas_call | solution.py:375
  59.2 1.1 slice.56
  60.4 7.2 %convolution_bitcast_fusion.refs_4_.refs_12_ = f32[512,2560]{1,0:T(8,128)} fusion(bf16[512,1024]{1,0:T(8,128)(2,1)S(1)} %copy-done.7, bf16[1024,2560]{1,0:T(8,128)(2,1)} %bitcast.124), kind=kOutput, calls=%fused_computation.18 | convolution fusion | flops 2684354560 | bytes 11534336 | tf_op jit(solution)/shard_map/dot_general | solution.py:818
  68.4 1.0 fusion.49
  69.3 3.3 fusion.59.refs_3_
  72.6 1.0 fusion.44
  73.6 1.0 pad_maximum_fusion
  75.2 123.2 %shard_map.239 = (bf16[4,2,2,2,32,2560]{5,4,3,2,1,0:T(8,128)(2,1)}, bf16[4,2,2,64,2176]{4,3,2,1,0:T(8,128)(2,1)}, bf16[4,2,2,64,2048]{4,3,2,1,0:T(8,128)(2,1)}, ...) custom-call(bf16[32,2560]{1,0:T(8,128)(2,1)} %bitcast.106, ...), custom_call_target="tpu_custom_call" | custom-call | tf_op jit(solution)/shard_map/pallas_call | solution.py:375
  198.7 8.3 %constant_dynamic-update-slice_fusion.3 = (bf16[1024,1024]{1,0:T(8,128)(2,1)S(1)}, bf16[512,1024]{1,0:T(8,128)(2,1)}, f32[512,1024]{1,0:T(8,128)}) fusion(bf16[1024,1024]{1,0:T(8,128)(2,1)S(1)} %broadcast.236.clone, s32[]{:T(128)S(6)} %select_n.72, bf16[512,2560]{1,0:T(8,128)(2,1)} %get-tuple-element.35, bf16[1024,2560]{1,0:T(8,128)(2,1)} %bitcast.126, ...), kind=kOutput, calls=%fused_computation.114 | convolution fusion | flops 2685927424 | bytes 13107204 | tf_op jit(solution)/shard_map/dot_general | solution.py:28
  207.2 2.8 collective-permute-done
  210.0 1.5 constant_dynamic-update-slice_fusion.2
  212.6 6.0 %maximum_convert_fusion = bf16[1024,2048]{1,0:T(8,128)(2,1)} fusion(bf16[1024,1024]{1,0:T(8,128)(2,1)S(1)} %constant_dynamic-update-slice_fusion.2, bf16[1024,2176]{1,0:T(8,128)(2,1)S(1)} %bitcast.116), kind=kOutput, calls=%fused_computation.7 | convolution fusion | flops 4299161600 | bytes 10485760 | tf_op jit(solution)/shard_map/dot_general | solution.py:917
  219.3 1.3 copy-done.2
  221.3 1.0 copy.85
  222.3 3.4 broadcast_in_dim.96
  225.7 10.9 %fusion.62 = f32[1024,1024]{1,0:T(8,128)S(1)} fusion(bf16[1024,2048]{1,0:T(8,128)(2,1)S(1)} %bitcast.131, bf16[1024,2048]{1,0:T(8,128)(2,1)} %maximum_convert_fusion, f32[128,8,16,128]{3,2,1,0:T(8,128)S(1)} %bitcast.96), kind=kOutput, calls=%fused_computation.127 | convolution fusion | flops 4301258752 | bytes 20971520 | tf_op jit(solution)/shard_map/dot_general | solution.py:28
  236.6 1.3 dynamic-slice_convert_fusion.1
  237.9 1.0 copy-done.11
  242.2 0.9 copy-done.8
  243.1 4.6 constant_dynamic-update-slice_fusion.1
  248.0 2.3 collective-permute-done.2
  250.4 8.9 %convolution_convert_fusion.3 = bf16[1024,2048]{1,0:T(8,128)(2,1)} fusion(bf16[1024,1024]{1,0:T(8,128)(2,1)S(1)} %constant_dynamic-update-slice_fusion, bf16[1024,2048]{1,0:T(8,128)(2,1)S(1)} %copy-done.27, f32[128,8,16,128]{3,2,1,0:T(8,128)S(1)} %bitcast.97), kind=kOutput, calls=%fused_computation.29 | convolution fusion | flops 4303355904 | bytes 18874368 | tf_op jit(solution)/shard_map/dot_general | solution.py:34
  259.3 12.2 %fusion.1 = (f32[128,8,16,128]{3,1,2,0:T(8,128)S(1)}, bf16[1024,2048]{1,0:T(8,128)(2,1)}) fusion(bf16[1024,2048]{1,0:T(8,128)(2,1)} %maximum_convert_fusion, f32[128,8,16,128]{3,2,1,0:T(8,128)S(1)} %bitcast.98, bf16[1024,1024]{1,0:T(8,128)(2,1)S(1)} %constant_dynamic-update-slice_fusion, bf16[1024,2048]{1,0:T(8,128)(2,1)} %bitcast.130), kind=kOutput, calls=%fused_computation.3 | convolution fusion | flops 4307550208 | bytes 31457280 | tf_op jit(solution)/shard_map/dot_general | solution.py:927
  271.5 5.2 %copy.100 = f32[128,8,16,128]{3,2,1,0:T(8,128)} copy(f32[128,8,16,128]{3,1,2,0:T(8,128)S(1)} %get-tuple-element.115) | data formatting | bytes 16777216
  276.7 6.4 %reduce_sum.134 = f32[1024,16]{1,0:T(8,128)} reduce(f32[1024,16,128]{2,1,0:T(8,128)} %bitcast.95, f32[]{:T(128)} %constant.80.clone.1), dimensions={2}, to_apply=%region_8.9 | reduce | flops 2080768 | bytes 8454148 | tf_op jit(solution)/shard_map/reduce_sum | solution.py:928
  283.1 1.2 copy.86
  284.4 3.0 fusion.15
  287.4 7.1 %fusion.14 = f32[1024,1024]{1,0:T(8,128)S(1)} fusion(bf16[1024,1024]{1,0:T(8,128)(2,1)S(1)} %constant_dynamic-update-slice_fusion.2, f32[1024,1024]{1,0:T(8,128)S(1)} %get-tuple-element.131, f32[1024]{0:T(1024)S(1)} %broadcast_multiply_fusion, f32[1024]{0:T(1024)S(1)} %broadcast_multiply_fusion.1, f32[1024]{0:T(1024)S(1)} %bitcast.113, ...), kind=kOutput, calls=%fused_computation.26 | convolution fusion | flops 4304404480 | bytes 18894848 | tf_op jit(solution)/shard_map/dot_general | solution.py:28
  295.1 1.5 convolution_convert_fusion.5
  296.6 6.5 %convolution_convert_fusion.4 = bf16[1024,2048]{1,0:T(8,128)(2,1)} fusion(bf16[1024,1024]{1,0:T(8,128)(2,1)S(1)} %constant_dynamic-update-slice_fusion.2, bf16[1024,2048]{1,0:T(8,128)(2,1)S(1)} %copy-done.28), kind=kOutput, calls=%fused_computation.30 | convolution fusion | flops 4297064448 | bytes 10485760 | tf_op jit(solution)/shard_map/dot_general | solution.py:34
  303.1 1.7 add_add_fusion
  304.8 4.2 convolution_convert_fusion.2.refs_11_
  309.0 4.7 convolution_convert_fusion.1
  313.7 107.2 %shard_map.240 = (f32[32,2560]{1,0:T(8,128)}, f32[64,2048]{1,0:T(8,128)}, f32[64,128]{1,0:T(8,128)}, f32[64,2048]{1,0:T(8,128)}, bf16[512,1152]{1,0:T(8,128)(2,1)}, /*index=5*/bf16[512,2560]{1,0:T(8,128)(2,1)}) custom-call(bf16[4,2,2,2,32,2560]{5,4,3,2,1,0:T(8,128)(2,1)} %bitcast.100, bf16[4,2,2,64,2048]{4,3,2,1,0:T(8,128)(2,1)} %bitcast.102, ...), custom_call_target="tpu_custom_call" | custom-call | tf_op jit(solution)/shard_map/pallas_call | solution.py:625
  420.9 5.3 %fusion.32 = (f32[1024]{0:T(1024)S(1)}, f32[512]{0:T(512)S(1)}, f32[512]{0:T(512)S(1)}, f32[512,1024]{1,0:T(8,128)}) fusion(bf16[512,1024]{1,0:T(8,128)(2,1)S(1)} %copy-done.7, f32[512]{0:T(512)S(1)} %add_rsqrt_fusion.1, f32[512]{0:T(512)S(1)} %broadcast_multiply_fusion.5, f32[1024]{0:T(1024)S(1)} %bitcast.119, bf16[512,1152]{1,0:T(8,128)(2,1)} %get-tuple-element.46, ...), kind=kOutput, calls=%fused_computation.50 | convolution fusion | flops 1212676096 | bytes 6701056 | tf_op jit(solution)/shard_map/dot_general | solution.py:28
  426.2 5.0 %convolution_convert_fusion = bf16[2560,1024]{0,1:T(8,128)(2,1)} fusion(bf16[512,2560]{1,0:T(8,128)(2,1)S(1)} %copy-done.25, bf16[512,1024]{1,0:T(8,128)(2,1)S(1)} %copy-done.7), kind=kOutput, calls=%fused_computation.8 | convolution fusion | flops 2686976000 | bytes 8912896 | tf_op jit(solution)/shard_map/dot_general | solution.py:34
  431.2 3.2 add_convert_fusion
  434.4 43.6 %shard_map.241 = (f32[32,1152]{1,0:T(8,128)}, f32[32,2560]{1,0:T(8,128)}) custom-call(bf16[4,2,2,2,32,1152]{5,4,3,2,1,0:T(8,128)(2,1)} %bitcast.103, bf16[4,2,2,2,32,2560]{5,4,3,2,1,0:T(8,128)(2,1)} %bitcast.99), custom_call_target="tpu_custom_call" | custom-call | tf_op jit(solution)/shard_map/pallas_call | solution.py:625
  478.0 1.5 slice_reduce_fusion
  479.5 1.3 slice.53
  480.8 1.5 fusion.65
  483.0 1.9 bitcast_bitcast_fusion.1
  484.9 0.8 bitcast_bitcast_fusion
  485.7 9.0 %fusion.31 = f32[512,1024]{1,0:T(8,128)} fusion(f32[512,1024]{1,0:T(8,128)} %copy-done.12, bf16[512,1024]{1,0:T(8,128)(2,1)S(1)} %copy-done.7, f32[512,1024]{1,0:T(8,128)} %get-tuple-element.132, f32[512]{0:T(512)S(1)} %broadcast_multiply_fusion.3, f32[512]{0:T(512)S(1)} %broadcast_multiply_fusion.4, f32[1024]{0:T(1024)S(1)} %bitcast.121, ...), kind=kOutput, calls=%fused_computation.49 | convolution fusion | flops 2689597440 | bytes 15216640 | tf_op jit(solution)/shard_map/dot_general | solution.py:28
  (113 shorter events, 12.9 us)
Async XLA Ops:
  0.6 7.3 %copy-start = (bf16[16,64,128]{2,1,0:T(8,128)(2,1)S(1)}, bf16[16,64,128]{2,1,0:T(8,128)(2,1)}, u32[]{:S(2)}) copy-start(bf16[16,64,128]{2,1,0:T(8,128)(2,1)} %param.28) | copy-start | bytes 786436
  0.7 59.8 %copy-start.7 = (bf16[512,1024]{1,0:T(8,128)(2,1)S(1)}, bf16[512,1024]{1,0:T(8,128)(2,1)}, u32[]{:S(2)}) copy-start(bf16[512,1024]{1,0:T(8,128)(2,1)} %param.15) | copy-start | bytes 3145732
  0.7 7.3 %copy-start.16 = (bf16[16,128,64]{1,2,0:T(8,128)(2,1)S(1)}, bf16[16,128,64]{1,2,0:T(8,128)(2,1)}, u32[]{:S(2)}) copy-start(bf16[16,128,64]{1,2,0:T(8,128)(2,1)} %param.29) | copy-start | bytes 786436
  0.7 8.1 %copy-start.22 = (bf16[32,40]{1,0:T(8,128)(2,1)S(1)}, bf16[32,40]{1,0:T(8,128)(2,1)}, u32[]{:S(2)}) copy-start(bf16[32,40]{1,0:T(8,128)(2,1)} %param.24) | copy-start | bytes 7684
  0.7 8.1 %copy-start.20 = (bf16[32,512]{1,0:T(8,128)(2,1)S(1)}, bf16[32,512]{1,0:T(8,128)(2,1)}, u32[]{:S(2)}) copy-start(bf16[32,512]{1,0:T(8,128)(2,1)} %param.22) | copy-start | bytes 98308
  0.7 8.1 %copy-start.19 = (bf16[32,512]{1,0:T(8,128)(2,1)S(1)}, bf16[32,512]{1,0:T(8,128)(2,1)}, u32[]{:S(2)}) copy-start(bf16[32,512]{1,0:T(8,128)(2,1)} %param.21) | copy-start | bytes 98308
  72.6 2.6 copy-start.10
  198.7 8.3 %copy-start.17 = (s32[1024,16]{0,1:T(8,128)S(1)}, s32[1024,16]{0,1:T(8,128)}, u32[]{:S(2)}) copy-start(s32[1024,16]{0,1:T(8,128)} %param.19) | copy-start | bytes 196612
  207.0 3.0 collective-permute-start
  210.0 2.6 copy-start.21
  219.3 1.3 copy-start.2
  222.3 3.4 copy-start.23
  225.7 10.9 %copy-start.4 = (f32[1024,16,128]{2,1,0:T(8,128)}, f32[1024,16,128]{2,1,0:T(8,128)S(1)}, u32[]{:S(2)}) copy-start(f32[1024,16,128]{2,1,0:T(8,128)S(1)} %broadcast_in_dim.96) | copy-start | bytes 25165828
  236.6 2.3 copy-start.11
  238.9 3.0 collective-permute-start.1
  241.8 1.2 copy-start.8
  243.1 7.4 %copy-start.5 = (f32[1024,16,128]{2,1,0:T(8,128)S(1)}, f32[1024,16,128]{2,1,0:T(8,128)}, u32[]{:S(2)}) copy-start(f32[1024,16,128]{2,1,0:T(8,128)} %copy-done.4) | copy-start | bytes 25165828
  243.1 7.4 %copy-start.27 = (bf16[1024,2048]{1,0:T(8,128)(2,1)S(1)}, bf16[1024,2048]{1,0:T(8,128)(2,1)}, u32[]{:S(2)}) copy-start(bf16[1024,2048]{1,0:T(8,128)(2,1)} %maximum_convert_fusion) | copy-start | bytes 12582916
  247.6 2.7 collective-permute-start.2
  284.4 3.0 copy-start.28
  287.4 7.7 %copy-start.3 = (bf16[1024,1024]{1,0:T(8,128)(2,1)S(1)}, bf16[1024,1024]{1,0:T(8,128)(2,1)}, u32[]{:S(2)}) copy-start(bf16[1024,1024]{1,0:T(8,128)(2,1)} %copy-done.2) | copy-start | bytes 6291460
  294.7 8.4 %collective-permute-start.3 = (bf16[512,1024]{1,0:T(8,128)(2,1)S(1)}, bf16[512,1024]{1,0:T(8,128)(2,1)S(1)}, u32[]{:S(2)}, u32[]{:S(2)}) collective-permute-start(bf16[512,1024]{1,0:T(8,128)(2,1)S(1)} %dynamic-slice_convert_fusion), channel_id=1, source_target_pairs={{0,1},{1,0},{2,3},{3,2},{4,5},{5,4},{6,7},{7,6},{8,9},{9,8},{10,11... | collective-permute-start | bytes 3145736 | tf_op jit(solution)/shard_map/ppermute | solution.py:660
  295.1 9.7 %slice-start = ((s8[5242880]{0:T(1024)(128)(4,1)}), s8[1048576]{0:T(1024)(128)(4,1)S(1)}, s32[]{:S(2)}) async-start(s8[5242880]{0:T(1024)(128)(4,1)} %bitcast.127), calls=%async_computation | async-start | bytes 2097152
  296.6 6.5 %copy-start.6 = (f32[512,1024]{1,0:T(8,128)S(1)}, f32[512,1024]{1,0:T(8,128)}, u32[]{:S(2)}) copy-start(f32[512,1024]{1,0:T(8,128)} %get-tuple-element.112) | copy-start | bytes 6291460
  296.6 6.5 %copy-start.9 = (bf16[512,1024]{1,0:T(8,128)(2,1)S(1)}, bf16[512,1024]{1,0:T(8,128)(2,1)}, u32[]{:S(2)}) copy-start(bf16[512,1024]{1,0:T(8,128)(2,1)} %param.16) | copy-start | bytes 3145732
  296.6 8.2 %slice-start.1 = ((s8[5242880]{0:T(1024)(128)(4,1)}), s8[4194304]{0:T(1024)(128)(4,1)S(1)}, s32[]{:S(2)}) async-start(s8[5242880]{0:T(1024)(128)(4,1)} %bitcast.127), calls=%async_computation.1 | async-start | bytes 8388608
  304.8 4.2 copy-start.12
  304.8 4.2 copy-start.24
  420.9 5.3 %copy-start.25 = (bf16[512,2560]{1,0:T(8,128)(2,1)S(1)}, bf16[512,2560]{1,0:T(8,128)(2,1)}, u32[]{:S(2)}) copy-start(bf16[512,2560]{1,0:T(8,128)(2,1)} %get-tuple-element.47) | copy-start | bytes 7864324
  426.2 5.0 %copy-start.26 = (bf16[512,1152]{1,0:T(8,128)(2,1)S(1)}, bf16[512,1152]{1,0:T(8,128)(2,1)}, u32[]{:S(2)}) copy-start(bf16[512,1152]{1,0:T(8,128)(2,1)} %get-tuple-element.46) | copy-start | bytes 3538948
  434.4 47.9 %copy-start.18 = (f32[64,128]{1,0:T(8,128)S(1)}, f32[64,128]{1,0:T(8,128)}, u32[]{:S(2)}) copy-start(f32[64,128]{1,0:T(8,128)} %get-tuple-element.51) | copy-start | bytes 98308
  434.4 50.5 %copy-start.13 = (f32[64,2048]{1,0:T(8,128)S(1)}, f32[64,2048]{1,0:T(8,128)}, u32[]{:S(2)}) copy-start(f32[64,2048]{1,0:T(8,128)} %get-tuple-element.53) | copy-start | bytes 1572868
  485.7 9.0 %copy-start.15 = (f32[32,2560]{1,0:T(8,128)S(1)}, f32[32,2560]{1,0:T(8,128)}, u32[]{:S(2)}) copy-start(f32[32,2560]{1,0:T(8,128)} %get-tuple-element.154) | copy-start | bytes 983044
  485.7 9.7 %copy-start.14 = (f32[32,2560]{1,0:T(8,128)S(1)}, f32[32,2560]{1,0:T(8,128)}, u32[]{:S(2)}) copy-start(f32[32,2560]{1,0:T(8,128)} %get-tuple-element.50) | copy-start | bytes 983044
  485.7 10.4 %copy-start.1 = (bf16[16,64,128]{2,1,0:T(8,128)(2,1)S(1)}, bf16[16,64,128]{2,1,0:T(8,128)(2,1)}, u32[]{:S(2)}) copy-start(bf16[16,64,128]{2,1,0:T(8,128)(2,1)} %param.28) | copy-start | bytes 786436

commit v4 on v3

--- a/solution.py
+++ b/solution.py
@@ -736,6 +736,280 @@
     )
 
 
+EXPERT_BLOCK = 512
+ROW_BLOCK = 128
+
+
+def gate_column(table, lane):
+    lanes = lax.broadcasted_iota(jnp.int32, table.shape, 1)
+    return jnp.sum(jnp.where(lanes == lane, table, 0.0), axis=1, keepdims=True)
+
+
+def halves(core, rows):
+    return (
+        pl.ds(pl.multiple_of(core * rows, rows), rows),
+        pl.ds(pl.multiple_of((1 - core) * rows, rows), rows),
+    )
+
+
+def hat_of(values):
+    average = jnp.mean(values, axis=-1, keepdims=True)
+    centred = values - average
+    inv_std = lax.rsqrt(jnp.mean(centred * centred, axis=-1, keepdims=True) + EPS)
+    return (centred * inv_std, inv_std)
+
+
+def expert_kernel(
+    own, other, gain, member, router, up, down, active, gated, normed, gates, mine, leaving, rows_in, total
+):
+    step, core = (pl.program_id(0), lax.axis_index("col"))
+    here, there = halves(core, own.shape[0])
+    hidden = 128
+
+    @pl.when(step == 0)
+    def _():
+        rows_in[here] = own[...]
+        rows_in[there] = other[...]
+
+        def norm_block(block, carry):
+            at = pl.ds(pl.multiple_of(block * ROW_BLOCK, ROW_BLOCK), ROW_BLOCK)
+            hat, _ = hat_of(rows_in[at].astype(jnp.float32))
+            normed[at] = (hat * gain[...]).astype(normed.dtype)
+            return carry
+
+        lax.fori_loop(0, rows_in.shape[0] // ROW_BLOCK, norm_block, 0)
+        gates[...] = jax.nn.sigmoid(
+            jnp.dot(normed[...], router[...], preferred_element_type=jnp.float32)
+        )
+
+    inner = jnp.dot(rows_in[...], up[...], preferred_element_type=jnp.float32)
+    active[...] = jnp.maximum(inner, 0.0).astype(active.dtype)
+    used = gates[...] * member[...]
+    count = EXPERT_BLOCK // hidden
+    for one in range(count):
+        at = slice(one * hidden, (one + 1) * hidden)
+        gate = gate_column(used, step * count + one)
+        gated[:, at] = (active[:, at].astype(jnp.float32) * gate).astype(gated.dtype)
+    part = contract_last(gated[...], down[...])
+
+    @pl.when(step == 0)
+    def _():
+        total[...] = part
+
+    @pl.when(step > 0)
+    def _():
+        total[...] += part
+
+    @pl.when(step == pl.num_programs(0) - 1)
+    def _():
+        mine[...] = total[here]
+        leaving[...] = total[there].astype(leaving.dtype)
+
+
+def expert_back_kernel(
+    own,
+    other,
+    grad_own,
+    grad_other,
+    gain,
+    member,
+    router,
+    gates,
+    normed,
+    active,
+    gated,
+    up,
+    down,
+    down_grad,
+    up_grad,
+    router_grad,
+    gain_grad,
+    mine,
+    leaving,
+    rows_turned,
+    grads,
+    grads_turned,
+    gate_grads,
+    logits,
+    total,
+):
+    step, core = (pl.program_id(0), lax.axis_index("col"))
+    here, there = halves(core, own.shape[0])
+    hidden = 128
+
+    @pl.when(step == 0)
+    def _():
+        rows_turned[:, here] = own[...].T
+        rows_turned[:, there] = other[...].T
+        grads[here] = grad_own[...]
+        grads[there] = grad_other[...]
+        grads_turned[:, here] = grad_own[...].T
+        grads_turned[:, there] = grad_other[...].T
+        gate_grads[...] = jnp.zeros_like(gate_grads)
+
+    grad_hidden = jnp.dot(grads[...], down[...], preferred_element_type=jnp.float32)
+    used = gates[...] * member[...]
+    lanes = lax.broadcasted_iota(jnp.int32, gate_grads.shape, 1)
+    count = EXPERT_BLOCK // hidden
+    pieces = []
+    for one in range(count):
+        at = slice(one * hidden, (one + 1) * hidden)
+        lane = step * count + one
+        act = active[:, at].astype(jnp.float32)
+        piece = grad_hidden[:, at]
+        column = jnp.sum(act * piece, axis=1, keepdims=True)
+        gate_grads[...] = jnp.where(lanes == lane, column, gate_grads[...])
+        pieces.append(jnp.where(act > 0, piece * gate_column(used, lane), 0.0).astype(jnp.bfloat16))
+    grad_inner = jnp.concatenate(pieces, axis=1)
+    down_grad[...] = jnp.dot(
+        grads_turned[...], gated[...], preferred_element_type=jnp.float32
+    ).astype(down_grad.dtype)
+    up_grad[...] = jnp.dot(
+        rows_turned[...], grad_inner, preferred_element_type=jnp.float32
+    ).astype(up_grad.dtype)
+    part = contract_last(grad_inner, up[...])
+
+    @pl.when(step == 0)
+    def _():
+        total[...] = part
+
+    @pl.when(step > 0)
+    def _():
+        total[...] += part
+
+    @pl.when(step == pl.num_programs(0) - 1)
+    def _():
+        logits[...] = (gate_grads[...] * used * (1.0 - gates[...])).astype(logits.dtype)
+        router_grad[...] = contract_first(normed[...], logits[...]).astype(router_grad.dtype)
+        gain_grad[...] = jnp.zeros_like(gain_grad)
+
+        def back_block(source, first):
+            def body(block, carry):
+                at = pl.ds(pl.multiple_of(block * ROW_BLOCK, ROW_BLOCK), ROW_BLOCK)
+                whole = pl.ds(pl.multiple_of(first + block * ROW_BLOCK, ROW_BLOCK), ROW_BLOCK)
+                hat, inv_std = hat_of(source[at].astype(jnp.float32))
+                grad_norm = contract_last(logits[whole], router[...])
+                gain_grad[...] += jnp.sum(grad_norm * hat, axis=0, keepdims=True)
+                total[whole] += norm_back(grad_norm, gain[...], hat, inv_std)
+                return carry
+
+            lax.fori_loop(0, source.shape[0] // ROW_BLOCK, body, 0)
+
+        back_block(own, core * own.shape[0])
+        back_block(other, (1 - core) * own.shape[0])
+        mine[...] = total[here]
+        leaving[...] = total[there].astype(leaving.dtype)
+
+
+def still(shape):
+    return pl.BlockSpec(shape, lambda step: (0,) * len(shape))
+
+
+def expert_calls(own, gain, member, up_wide, down_turned):
+    rows, width = own.shape
+    hidden = down_turned.shape[1]
+    steps = hidden // EXPERT_BLOCK
+    low, full = (jnp.bfloat16, jnp.float32)
+    other = sibling(own)
+    block = pl.BlockSpec((width, EXPERT_BLOCK), lambda step: (0, step))
+    pairs = pl.BlockSpec((2 * rows, EXPERT_BLOCK), lambda step: (0, step))
+    router = pl.BlockSpec((width, 128), lambda step: (0, hidden // 128))
+    params = pltpu.CompilerParams(vmem_limit_bytes=60 * 1024 * 1024)
+    active, gated, normed, gates, mine, leaving = pl.pallas_call(
+        expert_kernel,
+        grid=(steps,),
+        out_shape=[
+            jax.ShapeDtypeStruct((2 * rows, hidden), low),
+            jax.ShapeDtypeStruct((2 * rows, hidden), low),
+            jax.ShapeDtypeStruct((2 * rows, width), low),
+            jax.ShapeDtypeStruct((2 * rows, 128), full),
+            jax.ShapeDtypeStruct((rows, width), full),
+            jax.ShapeDtypeStruct((rows, width), low),
+        ],
+        in_specs=[
+            still((rows, width)),
+            still((rows, width)),
+            still((1, width)),
+            still((2 * rows, 128)),
+            router,
+            block,
+            block,
+        ],
+        out_specs=[
+            pairs,
+            pairs,
+            still((2 * rows, width)),
+            still((2 * rows, 128)),
+            still((rows, width)),
+            still((rows, width)),
+        ],
+        scratch_shapes=[pltpu.VMEM((2 * rows, width), low), pltpu.VMEM((2 * rows, width), full)],
+        compiler_params=params,
+    )(own, other, gain, member, up_wide, up_wide, down_turned)
+    expert_sum = mine + sibling(leaving).astype(full)
+
+    def back(grad_own):
+        down_grad, up_grad, router_grad, gain_grad, mine, leaving = pl.pallas_call(
+            expert_back_kernel,
+            grid=(steps,),
+            out_shape=[
+                jax.ShapeDtypeStruct((width, hidden), low),
+                jax.ShapeDtypeStruct((width, hidden), low),
+                jax.ShapeDtypeStruct((width, 128), low),
+                jax.ShapeDtypeStruct((1, width), full),
+                jax.ShapeDtypeStruct((rows, width), full),
+                jax.ShapeDtypeStruct((rows, width), low),
+            ],
+            in_specs=[still((rows, width))] * 4
+            + [
+                still((1, width)),
+                still((2 * rows, 128)),
+                router,
+                still((2 * rows, 128)),
+                still((2 * rows, width)),
+                pairs,
+                pairs,
+                block,
+                block,
+            ],
+            out_specs=[
+                block,
+                block,
+                still((width, 128)),
+                still((1, width)),
+                still((rows, width)),
+                still((rows, width)),
+            ],
+            scratch_shapes=[
+                pltpu.VMEM((width, 2 * rows), low),
+                pltpu.VMEM((2 * rows, width), low),
+                pltpu.VMEM((width, 2 * rows), low),
+                pltpu.VMEM((2 * rows, 128), full),
+                pltpu.VMEM((2 * rows, 128), low),
+                pltpu.VMEM((2 * rows, width), full),
+            ],
+            compiler_params=params,
+        )(
+            own,
+            other,
+            grad_own,
+            sibling(grad_own),
+            gain,
+            member,
+            up_wide,
+            gates,
+            normed,
+            active,
+            gated,
+            up_wide,
+            down_turned,
+        )
+        moe_grad = mine + sibling(leaving).astype(full)
+        return (down_grad, up_grad, router_grad, gain_grad[0], moe_grad)
+
+    return (expert_sum, back)
+
+
 def shards(
     block_input,
     teacher,
@@ -903,42 +1177,54 @@
     router_cols = up_wide[:, hidden : hidden + local_experts]
     resid = inputs_full + contract_last(mixed_low, output_turned)
     resid_low = resid.astype(jnp.bfloat16)
-    group_in = gather_col(resid_low)
-    normed_two, hat_two, inv_two = norm_parts(group_in.astype(jnp.float32), gain_two)
-    normed_two_low = normed_two.astype(jnp.bfloat16)
-    gates = jax.nn.sigmoid(jnp.dot(normed_two_low, router_cols, preferred_element_type=jnp.float32))
     expert_ids = col_index * local_experts + jnp.arange(local_experts, dtype=jnp.int32)
     member = jnp.any(expert_routes[:, :, None] == expert_ids[None, None, :], axis=1)
-    used_gates = gates * member.astype(jnp.float32)
-
-    def spread(columns):
-        return jnp.repeat(columns, hidden_local, axis=1)
-
-    inner = jnp.dot(group_in, up_full, preferred_element_type=jnp.float32)
-    active = jnp.maximum(inner, 0.0).astype(jnp.bfloat16)
-    gated_active = (active.astype(jnp.float32) * spread(used_gates)).astype(jnp.bfloat16)
-    expert_sum = scatter_col(contract_last(gated_active, down_turned))
+    if paired:
+        expert_sum, expert_back = expert_calls(
+            resid_low,
+            gain_two[None, :],
+            padded(member.astype(jnp.float32), 128),
+            up_wide,
+            down_turned,
+        )
+    else:
+        group_in = gather_col(resid_low)
+        normed_two, hat_two, inv_two = norm_parts(group_in.astype(jnp.float32), gain_two)
+        normed_two_low = normed_two.astype(jnp.bfloat16)
+        gates = jax.nn.sigmoid(jnp.dot(normed_two_low, router_cols, preferred_element_type=jnp.float32))
+        used_gates = gates * member.astype(jnp.float32)
+
+        def spread(columns):
+            return jnp.repeat(columns, hidden_local, axis=1)
+
+        inner = jnp.dot(group_in, up_full, preferred_element_type=jnp.float32)
+        active = jnp.maximum(inner, 0.0).astype(jnp.bfloat16)
+        gated_active = (active.astype(jnp.float32) * spread(used_gates)).astype(jnp.bfloat16)
+        expert_sum = scatter_col(contract_last(gated_active, down_turned))
     output_full_rows = resid + expert_sum
     block_output = output_full_rows.astype(jnp.bfloat16)
     ratio = total_rows / token_count
     grad_output = ratio * (output_full_rows - teacher.astype(jnp.float32)) * valid[:, None]
     grad_output_low = grad_output.astype(jnp.bfloat16)
-    group_grad = gather_col(grad_output_low)
-    grad_hidden = jnp.dot(group_grad, down_turned, preferred_element_type=jnp.float32)
-    gate_grad = jnp.sum(
-        (active.astype(jnp.float32) * grad_hidden).reshape(group_size, local_experts, hidden_local),
-        axis=2,
-    )
-    grad_inner = jnp.where(active > 0, grad_hidden * spread(used_gates), 0.0).astype(jnp.bfloat16)
-    down_grad = contract_first(group_grad, gated_active).astype(jnp.bfloat16)
-    up_grad = contract_first(group_in, grad_inner).astype(jnp.bfloat16)
-    slot_back = contract_last(grad_inner, up_full)
-    logit_low = (gate_grad * used_gates * (1.0 - gates)).astype(jnp.bfloat16)
-    router_grad = contract_first(normed_two_low, padded(logit_low, 128)).astype(jnp.bfloat16)
-    grad_norm_two = contract_last(logit_low, router_cols)
-    second_gain_part = jnp.sum(grad_norm_two * hat_two, axis=0)
-    grad_rows = slot_back + norm_back(grad_norm_two, gain_two, hat_two, inv_two)
-    moe_grad = scatter_col(grad_rows)
+    if paired:
+        down_grad, up_grad, router_grad, second_gain_part, moe_grad = expert_back(grad_output_low)
+    else:
+        group_grad = gather_col(grad_output_low)
+        grad_hidden = jnp.dot(group_grad, down_turned, preferred_element_type=jnp.float32)
+        gate_grad = jnp.sum(
+            (active.astype(jnp.float32) * grad_hidden).reshape(group_size, local_experts, hidden_local),
+            axis=2,
+        )
+        grad_inner = jnp.where(active > 0, grad_hidden * spread(used_gates), 0.0).astype(jnp.bfloat16)
+        down_grad = contract_first(group_grad, gated_active).astype(jnp.bfloat16)
+        up_grad = contract_first(group_in, grad_inner).astype(jnp.bfloat16)
+        slot_back = contract_last(grad_inner, up_full)
+        logit_low = (gate_grad * used_gates * (1.0 - gates)).astype(jnp.bfloat16)
+        router_grad = contract_first(normed_two_low, padded(logit_low, 128)).astype(jnp.bfloat16)
+        grad_norm_two = contract_last(logit_low, router_cols)
+        second_gain_part = jnp.sum(grad_norm_two * hat_two, axis=0)
+        grad_rows = slot_back + norm_back(grad_norm_two, gain_two, hat_two, inv_two)
+        moe_grad = scatter_col(grad_rows)
     grad_resid = grad_output + moe_grad
     grad_branch = grad_resid.astype(jnp.bfloat16)
     output_grad = contract_first(grad_branch, mixed_low).astype(jnp.bfloat16)

time: 500 us -> 487 us (0.974); the launches traced: 496 us -> 478 us
  Pallas kernels: 324 us -> 379 us
  matrix products: 107 us -> 53.3 us
  local copies, waits for them, and re-layouts: 33.7 us -> 20.7 us
  other arithmetic: 22.8 us -> 14.6 us
    pallas_call x0 -> x2, Pallas kernels: none -> 53.8 us  [the longest x1 33.6 us: back(): pl.pallas_call(expert_back_kernel, grid=(steps,), out_shape=[jax.ShapeDty...]
    dot_general x6 -> x3, matrix products: 43.5 us -> 21.8 us  [contract_last(): lax.dot_general(left, right, (((1,), (1,)), ((), ())), preferred_element_...]
    dot_general x3 -> x0, matrix products: 18.9 us -> none  [the longest x1 12.2 us: shards(): jnp.dot(group_grad, down_turned, preferred_element_type=jnp.float32)]
    dot_general x6 -> x3, matrix products: 29.7 us -> 12.7 us  [contract_first(): lax.dot_general(left, right, (((0,), (0,)), ((), ())), preferred_element_...]
    reduce_sum x1 -> x0, other arithmetic: 6.44 us -> none  [shards(): jnp.sum((active.astype(jnp.float32) * grad_hidden).reshape(group_size, lo...]
    unnamed x69 -> x48, local copies, waits for them, and re-layouts: 12.3 us -> 6.82 us
  transfers between devices with their start and end apart: 4 -> 4, of which waited for: 3 -> 3; matrix products, arithmetic and copies ran while one was open for 2% -> 1% of each run, Pallas kernels for 0% -> 0%
where the time goes in v4:
time: 487 us; the launch traced here: 478 us
  Pallas kernels  379 us (78%)
  matrix products  53.3 us (11%)
  local copies, waits for them, and re-layouts  20.7 us (4%)
  other arithmetic  14.6 us (3%)
  waiting for transfers between devices  5.63 us (1%)
    pallas_call x2, Pallas kernels, gather_call(): pl.pallas_call(functools.partial(kernel, chunks, events, shared), out_sha...  173 us
    pallas_call x2, Pallas kernels, scatter_call(): pl.pallas_call(functools.partial(kernel, chunks, events, shared), out_sha...  152 us
    pallas_call x1, Pallas kernels, back(): pl.pallas_call(expert_back_kernel, grid=(steps,), out_shape=[jax.ShapeDty...  33.6 us
    dot_general x3, matrix products, contract_last(): lax.dot_general(left, right, (((1,), (1,)), ((), ())), preferred_element_...  21.8 us
    pallas_call x1, Pallas kernels, expert_calls(): pl.pallas_call(expert_kernel, grid=(steps,), out_shape=[jax.ShapeDtypeStr...  20.2 us
    dot_general x3, matrix products, contract_first(): lax.dot_general(left, right, (((0,), (0,)), ((), ())), preferred_element_...  12.7 us
  transfers between devices with their start and end apart: 4, of which 3 were waited for; matrix products, arithmetic and copies ran while one was open for 1% of the time, Pallas kernels for 0%

profile of v4, /device:TPU:0, one launch (start us, length us, event | category | flops | bytes accessed | tf_op | source)
XLA Modules:
  0.0 477.7 jit_solution(9802501543064384358)
XLA Ops:
  1.4 0.8 copy.68
  2.2 0.8 copy.69
  2.9 1.4 convert_reduce_fusion
  4.4 0.9 concatenate.17
  5.3 0.6 pad.20.refs_0_
  5.9 49.6 %shard_map.238 = (bf16[4,2,2,2,32,1152]{5,4,3,2,1,0:T(8,128)(2,1)}, bf16[4,2,2,2,32,2560]{5,4,3,2,1,0:T(8,128)(2,1)}) custom-call(bf16[32,1152]{1,0:T(8,128)(2,1)} %pad.20.refs_0_, bf16[32,2560]{1,0:T(8,128)(2,1)} %refs_1_.1), custom_call_target="tpu_custom_call" | custom-call | tf_op jit(solution)/shard_map/pallas_call | solution.py:375
  55.6 8.1 %convolution_bitcast_fusion.refs_4_.refs_12_ = f32[512,2560]{1,0:T(8,128)} fusion(bf16[512,1024]{1,0:T(8,128)(2,1)} %param.15, bf16[1024,2560]{1,0:T(8,128)(2,1)} %bitcast.97), kind=kOutput, calls=%fused_computation.2 | convolution fusion | flops 2684354560 | bytes 11534336 | tf_op jit(solution)/shard_map/dot_general | solution.py:1092
  63.7 1.1 slice.48
  65.9 0.7 copy_bitcast_fusion.refs_2_
  66.6 3.3 fusion.31.refs_3_
  69.9 1.4 copy-done.5
  71.3 0.9 fusion.21
  72.2 1.0 fusion.22
  73.2 0.7 fusion.18.refs_1_
  73.9 1.0 pad_maximum_fusion
  74.9 0.6 broadcast_in_dim.86.refs_8_.refs_17_
  75.5 123.2 %shard_map.239 = (bf16[4,2,2,2,32,2560]{5,4,3,2,1,0:T(8,128)(2,1)}, bf16[4,2,2,64,2176]{4,3,2,1,0:T(8,128)(2,1)}, bf16[4,2,2,64,2048]{4,3,2,1,0:T(8,128)(2,1)}, ...) custom-call(bf16[32,2560]{1,0:T(8,128)(2,1)} %bitcast.86, ...), custom_call_target="tpu_custom_call" | custom-call | tf_op jit(solution)/shard_map/pallas_call | solution.py:375
  198.7 7.5 %fusion.34 = (bf16[512,1024]{1,0:T(8,128)(2,1)S(1)}, f32[512,1024]{1,0:T(8,128)}) fusion(bf16[512,2560]{1,0:T(8,128)(2,1)} %get-tuple-element.47, bf16[1024,2560]{1,0:T(8,128)(2,1)} %bitcast.99, bf16[512,1024]{1,0:T(8,128)(2,1)S(1)} %copy-done.2), kind=kOutput, calls=%fused_computation.79 | convolution fusion | flops 2685927424 | bytes 12058624 | tf_op jit(solution)/shard_map/dot_general | solution.py:28
  206.8 0.8 pad_convert_fusion.member
  207.6 0.6 slice_bitcast_fusion.gain
  208.2 0.8 collective-permute-done.other
  209.1 20.2 %shard_map.240 = (bf16[1024,2048]{1,0:T(8,128)(2,1)}, bf16[1024,2048]{1,0:T(8,128)(2,1)}, bf16[1024,1024]{1,0:T(8,128)(2,1)}, f32[1024,128]{1,0:T(8,128)}, f32[5...) custom-call(bf16[512,1024]{1,0:T(8,128)(2,1)} %copy-done.3, bf16[512,1024]{1,0:T(8,128)(2,1)} %collective-permute-done.other, ...), custom_call_target="tpu_custom_call" | custom-call | tf_op jit(solution)/shard_map/pallas_call | solution.py:918
  229.7 0.6 reduce_sum.76
  230.3 0.6 reduce_sum.77
  232.2 1.0 copy-done.7
  233.2 3.3 fusion.14
  236.5 1.0 copy-done.4
  237.9 2.3 collective-permute-done.2.grad_other
  240.2 1.0 copy-done.8
  241.2 33.6 %shard_map.241 = (bf16[1024,2048]{1,0:T(8,128)(2,1)}, bf16[1024,2048]{1,0:T(8,128)(2,1)}, bf16[1024,128]{1,0:T(8,128)(2,1)}, f32[1,1024]{1,0:T(1,128)}, f32[512,1024]{1,0:T(8,128)}, /*index=5*/bf16[512,1024]{1,0:T(8,128)(2,1)}) custom-call(bf16[512,1024]{1,0:T(8,128)(2,1)} %copy-done.3, bf16[512,1024]{1,0:T(8,128)(2,1)} %collective-permute-done.other, ...), custom_call_target="tpu_custom_call" | custom-call | tf_op jit(solution)/shard_map/pallas_call | solution.py:952
  275.2 2.5 collective-permute-done.3
  277.7 3.5 add_add_fusion
  281.2 7.4 %convolution_convert_fusion.2.refs_11_ = bf16[512,2560]{1,0:T(8,128)(2,1)} fusion(bf16[1024,2560]{1,0:T(8,128)(2,1)} %bitcast.100, f32[512,1024]{1,0:T(8,128)S(1)} %get-tuple-element.135), kind=kOutput, calls=%fused_computation.5 | convolution fusion | flops 2686189568 | bytes 9961472 | tf_op jit(solution)/shard_map/dot_general | solution.py:1231
  288.7 4.6 convolution_convert_fusion.1
  293.3 107.4 %shard_map.242 = (f32[32,2560]{1,0:T(8,128)}, f32[64,2048]{1,0:T(8,128)}, f32[64,128]{1,0:T(8,128)}, f32[64,2048]{1,0:T(8,128)}, bf16[512,1152]{1,0:T(8,128)(2,1)}, /*index=5*/bf16[512,2560]{1,0:T(8,128)(2,1)}) custom-call(bf16[4,2,2,2,32,2560]{5,4,3,2,1,0:T(8,128)(2,1)} %bitcast.80, bf16[4,2,2,64,2048]{4,3,2,1,0:T(8,128)(2,1)} %bitcast.82, ...), custom_call_target="tpu_custom_call" | custom-call | tf_op jit(solution)/shard_map/pallas_call | solution.py:625
  400.7 5.3 %fusion.12 = (f32[1024]{0:T(1024)S(1)}, f32[512]{0:T(512)S(1)}, f32[512]{0:T(512)S(1)}, f32[512,1024]{1,0:T(8,128)}) fusion(bf16[512,1024]{1,0:T(8,128)(2,1)S(1)} %copy-done.2, f32[512]{0:T(512)S(1)} %add_rsqrt_fusion, f32[512]{0:T(512)S(1)} %broadcast_multiply_fusion.2, f32[1024]{0:T(1024)S(1)} %bitcast.92, bf16[512,1152]{1,0:T(8,128)(2,1)} %get-tuple-element.69, ...), kind=kOutput, calls=%fused_computation.21 | convolution fusion | flops 1212676096 | bytes 6701056 | tf_op jit(solution)/shard_map/dot_general | solution.py:28
  406.0 4.8 %convolution_convert_fusion = bf16[2560,1024]{0,1:T(8,128)(2,1)} fusion(bf16[512,2560]{1,0:T(8,128)(2,1)S(1)} %copy-done.18, bf16[512,1024]{1,0:T(8,128)(2,1)S(1)} %copy-done.2), kind=kOutput, calls=%fused_computation | convolution fusion | flops 2686976000 | bytes 8912896 | tf_op jit(solution)/shard_map/dot_general | solution.py:34
  410.8 3.3 add_convert_fusion
  414.1 45.0 %shard_map.243 = (f32[32,1152]{1,0:T(8,128)}, f32[32,2560]{1,0:T(8,128)}) custom-call(bf16[4,2,2,2,32,1152]{5,4,3,2,1,0:T(8,128)(2,1)} %bitcast.83, bf16[4,2,2,2,32,2560]{5,4,3,2,1,0:T(8,128)(2,1)} %bitcast.79), custom_call_target="tpu_custom_call" | custom-call | tf_op jit(solution)/shard_map/pallas_call | solution.py:625
  459.1 1.5 fusion.33
  460.6 1.3 slice.45
  461.9 1.5 slice_reduce_fusion
  463.4 1.9 bitcast_bitcast_fusion
  465.3 0.8 bitcast_bitcast_fusion.1
  466.2 0.7 copy.78
  466.9 9.0 %fusion.11 = f32[512,1024]{1,0:T(8,128)} fusion(f32[512,1024]{1,0:T(8,128)} %copy-done.6, bf16[512,1024]{1,0:T(8,128)(2,1)S(1)} %copy-done.2, f32[512,1024]{1,0:T(8,128)} %get-tuple-element.144, f32[512]{0:T(512)S(1)} %broadcast_multiply_fusion, f32[512]{0:T(512)S(1)} %broadcast_multiply_fusion.1, f32[1024]{0:T(1024)S(1)} %bitcast.94, ...), kind=kOutput, calls=%fused_computation.20 | convolution fusion | flops 2689597440 | bytes 15216640 | tf_op jit(solution)/shard_map/dot_general | solution.py:28
  475.8 0.7 copy.92
  476.6 0.7 copy.93
  (70 shorter events, 2.8 us)
Async XLA Ops:
  0.6 65.1 %copy-start = (bf16[16,64,128]{2,1,0:T(8,128)(2,1)S(1)}, bf16[16,64,128]{2,1,0:T(8,128)(2,1)}, u32[]{:S(2)}) copy-start(bf16[16,64,128]{2,1,0:T(8,128)(2,1)} %param.28) | copy-start | bytes 786436
  55.5 9.4 %copy-start.2 = (bf16[512,1024]{1,0:T(8,128)(2,1)S(1)}, bf16[512,1024]{1,0:T(8,128)(2,1)}, u32[]{:S(2)}) copy-start(bf16[512,1024]{1,0:T(8,128)(2,1)} %param.15) | copy-start | bytes 3145732
  55.5 9.8 %copy-start.15 = (s32[512,4,2]{0,2,1:T(2,128)S(1)}, s32[512,4,2]{0,2,1:T(2,128)}, u32[]{:S(2)}) copy-start(s32[512,4,2]{0,2,1:T(2,128)} %param.18) | copy-start | bytes 49156
  63.7 2.1 copy-start.16
  63.7 2.2 copy-start.12
  69.9 1.4 copy-start.5
  198.7 7.6 %copy-start.13 = (s32[1024,16]{0,1:T(8,128)S(1)}, s32[1024,16]{0,1:T(8,128)}, u32[]{:S(2)}) copy-start(s32[1024,16]{0,1:T(8,128)} %param.19) | copy-start | bytes 196612
  206.3 2.8 copy-start.3
  206.3 2.8 collective-permute-start
  229.3 3.0 collective-permute-start.1
  232.2 1.0 copy-start.7
  236.5 1.0 copy-start.4
  237.6 2.7 collective-permute-start.2
  240.2 1.0 copy-start.8
  274.8 2.9 collective-permute-start.3
  281.2 7.4 %copy-start.6 = (f32[512,1024]{1,0:T(8,128)}, f32[512,1024]{1,0:T(8,128)S(1)}, u32[]{:S(2)}) copy-start(f32[512,1024]{1,0:T(8,128)S(1)} %get-tuple-element.135) | copy-start | bytes 6291460
  281.2 7.4 %copy-start.17 = (bf16[512,2560]{1,0:T(8,128)(2,1)S(1)}, bf16[512,2560]{1,0:T(8,128)(2,1)}, u32[]{:S(2)}) copy-start(bf16[512,2560]{1,0:T(8,128)(2,1)} %get-tuple-element.47) | copy-start | bytes 7864324
  400.7 5.3 %copy-start.18 = (bf16[512,2560]{1,0:T(8,128)(2,1)S(1)}, bf16[512,2560]{1,0:T(8,128)(2,1)}, u32[]{:S(2)}) copy-start(bf16[512,2560]{1,0:T(8,128)(2,1)} %get-tuple-element.70) | copy-start | bytes 7864324
  406.0 4.8 %copy-start.19 = (bf16[512,1152]{1,0:T(8,128)(2,1)S(1)}, bf16[512,1152]{1,0:T(8,128)(2,1)}, u32[]{:S(2)}) copy-start(bf16[512,1152]{1,0:T(8,128)(2,1)} %get-tuple-element.69) | copy-start | bytes 3538948
  406.0 4.8 %copy-start.20 = (f32[1,1024]{1,0:T(1,128)S(1)}, f32[1,1024]{1,0:T(1,128)}, u32[]{:S(2)}) copy-start(f32[1,1024]{1,0:T(1,128)} %get-tuple-element.71) | copy-start | bytes 12292
  414.1 51.3 %copy-start.9 = (f32[64,2048]{1,0:T(8,128)S(1)}, f32[64,2048]{1,0:T(8,128)}, u32[]{:S(2)}) copy-start(f32[64,2048]{1,0:T(8,128)} %get-tuple-element.76) | copy-start | bytes 1572868
  459.1 7.1 %copy-start.14 = (f32[64,128]{1,0:T(8,128)S(1)}, f32[64,128]{1,0:T(8,128)}, u32[]{:S(2)}) copy-start(f32[64,128]{1,0:T(8,128)} %get-tuple-element.75) | copy-start | bytes 98308
  466.9 9.0 %copy-start.11 = (f32[32,2560]{1,0:T(8,128)S(1)}, f32[32,2560]{1,0:T(8,128)}, u32[]{:S(2)}) copy-start(f32[32,2560]{1,0:T(8,128)} %get-tuple-element.166) | copy-start | bytes 983044
  466.9 9.7 %copy-start.10 = (f32[32,2560]{1,0:T(8,128)S(1)}, f32[32,2560]{1,0:T(8,128)}, u32[]{:S(2)}) copy-start(f32[32,2560]{1,0:T(8,128)} %get-tuple-element.74) | copy-start | bytes 983044
  466.9 10.4 %copy-start.1 = (bf16[16,64,128]{2,1,0:T(8,128)(2,1)S(1)}, bf16[16,64,128]{2,1,0:T(8,128)(2,1)}, u32[]{:S(2)}) copy-start(bf16[16,64,128]{2,1,0:T(8,128)(2,1)} %param.28) | copy-start | bytes 786436
